TPU v7x, 128 devices: a whole 4x4x4 slice. The times are simulated.
128 devices in a mesh: dp: 16 (over y, z_lo, core), mp: 8 (over z_hi, x).
Axes of the slice: x: 4, y: 4, z: 4 (z_hi: 2, z_lo: 2; z = z_hi * 2 + z_lo), core: 2. Of those that a mesh axis runs over, the one named last changes fastest.
Arguments:
- doc_ids: int32 [16, 512], P('dp'), may hold values from 0 to 128255
- doc_lengths: int32 [16], P('dp'), may hold values from 128 to 512
- activations: bfloat16 [8192, 4096], P('dp'), may hold values from -6 to 6
- out_grads: bfloat16 [8192, 14336], P('dp'), may hold values from -0.29882812 to 0.29882812
- input_basis: bfloat16 [4096, 2048], P(None, 'mp'), may hold values from -0.09375 to 0.09375
- output_basis: bfloat16 [14336, 7168], P('dp', 'mp'), may hold values from -0.046875 to 0.046875
- eigenvalues: bfloat16 [2048, 7168], P(None, 'mp'), may hold values from 0.5 to 50
- query_left: bfloat16 [64, 32, 2048], P('dp'), may hold values from -0.125 to 0.125
- query_right: bfloat16 [64, 32, 7168], P('dp', None, 'mp'), may hold values from -0.0625 to 0.0625
Outputs:
- scores: float32 [16, 64], P('dp')
Inputs may be any that keep to these rules, and one draw needn't show every extreme that they name: `doc_lengths`: the live tokens are the first ones of each document.
All inputs are finite; a program needn't handle non-finite values.
Results may differ from a plain program's by a relative error of at most 0.023.
Values may be sent and summed in bfloat16 or wider, within the bound.
No kernel may reach another device: no remote copies, remote signals or barrier semaphores. Data moves between devices by JAX's collectives and lax.ppermute only.
A program may use at most 192 MiB of HBM per device.

v0:
```python
import jax
import jax.numpy as jnp
from jax import lax
from jax.sharding import PartitionSpec as P

damping = 0.5


def laid_out(blocks, dim):
    blocks = jnp.moveaxis(blocks, 0, dim)
    dims = blocks.shape
    return blocks.reshape(*dims[:dim], dims[dim] * dims[dim + 1], *dims[dim + 2 :])


def from_everyone(array, axis):
    length = lax.axis_size(axis)
    return lax.all_to_all(
        jnp.broadcast_to(array[None], (length, *array.shape)), axis, 0, 0, tiled=True
    )


def gather_directly(array, axis, dim):
    return laid_out(from_everyone(array, axis), dim)


def taken_together(array, axis):
    everything = from_everyone(array, axis)
    return jnp.sum(everything, axis=0)


def token_weights(doc_ids, doc_lengths):
    positions = jnp.arange(doc_ids.shape[1], dtype=jnp.int32)
    active = positions[None, :] < doc_lengths[:, None]
    matches = (doc_ids[:, :, None] == doc_ids[:, None, :]) & active[:, None, :]
    repeats = jnp.sum(matches.astype(jnp.float32), axis=2)
    return jnp.where(active, 1.0 / jnp.maximum(repeats, 1.0), 0.0)


def per_device(
    doc_ids,
    doc_lengths,
    activations,
    out_grads,
    input_basis,
    output_basis,
    eigenvalues,
    query_left,
    query_right,
):
    tok_rows = activations.shape[0]
    shard_rows = output_basis.shape[0]
    out_cols = output_basis.shape[1]
    rotated_share = jnp.dot(activations, input_basis, preferred_element_type=jnp.float32).astype(
        jnp.bfloat16
    )
    rotated_in = gather_directly(rotated_share, "mp", 1)
    empty = jnp.zeros((tok_rows, out_cols), jnp.float32)
    running = empty
    pieces = lax.all_gather(output_basis, "dp", axis=0, tiled=True)
    for member in range(pieces.shape[0] // shard_rows):
        grad_cols = lax.dynamic_slice_in_dim(out_grads, member * shard_rows, shard_rows, 1)
        partial_value = jnp.dot(
            grad_cols,
            pieces[member * shard_rows : (member + 1) * shard_rows],
            preferred_element_type=jnp.float32,
        )
        running = running + lax.optimization_barrier(partial_value.astype(jnp.bfloat16)).astype(
            jnp.float32
        )
    rotated_out = running.astype(jnp.bfloat16)
    weights = token_weights(doc_ids, doc_lengths)
    docs_here = doc_ids.shape[0]
    acts_doc = rotated_in.reshape(docs_here, -1, rotated_in.shape[1])
    grads_doc = rotated_out.reshape(docs_here, -1, out_cols)
    scaled = (weights[:, :, None] * grads_doc.astype(jnp.float32)).astype(jnp.bfloat16)
    gradient = jnp.einsum("dti,dtj->dij", acts_doc, scaled, preferred_element_type=jnp.float32)
    conditioned = (gradient / (eigenvalues.astype(jnp.float32) + damping)).astype(jnp.bfloat16)
    rank_rows = query_left.shape[1]
    left_part = lax.all_gather(query_left, "dp", axis=0, tiled=True)
    right_part = lax.all_gather(query_right, "dp", axis=0, tiled=True)
    number = left_part.shape[0]
    left_rows = left_part.reshape(number * rank_rows, left_part.shape[2])
    right_rows = right_part.reshape(number * rank_rows, right_part.shape[2]).astype(jnp.float32)
    mixture = jnp.einsum("ri,dij->drj", left_rows, conditioned, preferred_element_type=jnp.float32)
    values = jnp.sum((mixture * right_rows[None]).reshape(docs_here, number, -1), axis=2)
    return taken_together(values, "mp")


def solution(mesh):
    return jax.shard_map(
        per_device,
        mesh=mesh,
        in_specs=(
            P("dp", None),
            P("dp"),
            P("dp", None),
            P("dp", None),
            P(None, "mp"),
            P("dp", "mp"),
            P(None, "mp"),
            P("dp", None, None),
            P("dp", None, "mp"),
        ),
        out_specs=P("dp", None),
        check_vma=False,
    )
```

profile of v0, /device:TPU:0, one launch (start us, length us, event | category | flops | bytes accessed | tf_op | source)
XLA Modules:
  0.0 307.4 jit_solution(3509372564559330316)
XLA Ops:
  8.8 3.4 %convolution_convert_fusion = bf16[512,256]{1,0:T(8,128)(2,1)S(1)} fusion(bf16[512,4096]{1,0:T(8,128)(2,1)} %param.11, bf16[4096,256]{1,0:T(8,128)(2,1)S(1)} %copy-done), kind=kOutput, calls=%fused_computation.56 | convolution fusion | flops 1073872896 | bytes 6553600 | tf_op jit(solution)/shard_map/dot_general | solution.py:53
  13.8 7.8 %all-to-all-start = ((bf16[8,512,256]{1,2,0:T(8,128)(2,1)}), bf16[8,512,256]{1,2,0:T(8,128)(2,1)}, u32[]{:S(2)}, u32[]{:S(2)}) async-start(bf16[8,512,256]{1,2,0:T(8,128)(2,1)} %broadcast_in_dim.7), calls=%async_computation | async-start | bytes 4194304 | tf_op jit(solution)/shard_map/all_to_all | solution.py:17
  22.7 46.0 %all-gather.8.cloned.1.call-done = bf16[64,32,896]{2,1,0:T(8,128)(2,1)} async-done(((bf16[4,32,896]{2,1,0:T(8,128)(2,1)}), bf16[64,32,896]{2,1,0:T(8,128)(2,1)}) %all-gather.8.cloned.1.call-update) | async-done | bytes 3670032 | tf_op jit(solution)/shard_map/all_gather | solution.py:80
  68.6 5.5 %bitcast_convert_fusion = f32[1,2048,896]{2,1,0:T(8,128)} fusion(bf16[1,2048,896]{2,1,0:T(8,128)(2,1)} %bitcast.24), kind=kLoop, calls=%fused_computation.3 | loop fusion | flops 1835008 | bytes 11010048 | tf_op jit(solution)/shard_map/convert_element_type | solution.py:83
  74.1 8.7 %copy.18 = f32[1,2048,896]{1,2,0:T(8,128)} copy(f32[1,2048,896]{2,1,0:T(8,128)} %bitcast_convert_fusion) | data formatting | bytes 14680064 | tf_op jit(solution)/shard_map/convert_element_type | solution.py:83
  82.8 121.5 %all-gather.4.cloned.1.call-done = bf16[14336,896]{1,0:T(8,128)(2,1)} async-done(((bf16[896,896]{1,0:T(8,128)(2,1)}), bf16[14336,896]{1,0:T(8,128)(2,1)}) %all-gather.4.cloned.1.call-update) | async-done | bytes 25690128 | tf_op jit(solution)/shard_map/all_gather | solution.py:59
  204.3 3.1 fusion.36
  207.4 4.6 %fusion.39 = bf16[512,896]{1,0:T(8,128)(2,1)} fusion(bf16[14336,896]{1,0:T(8,128)(2,1)} %all-gather.4.cloned.1.call-done, bf16[512,14336]{1,0:T(8,128)(2,1)} %param.12), kind=kOutput, calls=%fused_computation.41 | convolution fusion | flops 822542336 | bytes 3440640 | tf_op jit(solution)/shard_map/dot_general | solution.py:62
  212.0 4.6 %fusion.42 = bf16[512,896]{1,0:T(8,128)(2,1)} fusion(bf16[14336,896]{1,0:T(8,128)(2,1)} %all-gather.4.cloned.1.call-done, bf16[512,14336]{1,0:T(8,128)(2,1)} %param.12), kind=kOutput, calls=%fused_computation.42 | convolution fusion | flops 822542336 | bytes 3440640 | tf_op jit(solution)/shard_map/dot_general | solution.py:62
  216.6 3.8 %fusion.45 = bf16[512,896]{1,0:T(8,128)(2,1)} fusion(bf16[14336,896]{1,0:T(8,128)(2,1)} %all-gather.4.cloned.1.call-done, bf16[512,14336]{1,0:T(8,128)(2,1)} %param.12), kind=kOutput, calls=%fused_computation.43 | convolution fusion | flops 822542336 | bytes 3440640 | tf_op jit(solution)/shard_map/dot_general | solution.py:62
  220.5 3.9 %fusion.48 = bf16[512,896]{1,0:T(8,128)(2,1)} fusion(bf16[14336,896]{1,0:T(8,128)(2,1)} %all-gather.4.cloned.1.call-done, bf16[512,14336]{1,0:T(8,128)(2,1)} %param.12), kind=kOutput, calls=%fused_computation.44 | convolution fusion | flops 822542336 | bytes 3440640 | tf_op jit(solution)/shard_map/dot_general | solution.py:62
  224.4 3.4 %fusion.51 = bf16[512,896]{1,0:T(8,128)(2,1)} fusion(bf16[14336,896]{1,0:T(8,128)(2,1)S(1)} %copy-done.3, bf16[512,14336]{1,0:T(8,128)(2,1)} %param.12), kind=kOutput, calls=%fused_computation.45 | convolution fusion | flops 822542336 | bytes 3440640 | tf_op jit(solution)/shard_map/dot_general | solution.py:62
  227.7 3.3 %fusion.54 = bf16[512,896]{1,0:T(8,128)(2,1)} fusion(bf16[14336,896]{1,0:T(8,128)(2,1)S(1)} %copy-done.3, bf16[512,14336]{1,0:T(8,128)(2,1)} %param.12), kind=kOutput, calls=%fused_computation.46 | convolution fusion | flops 822542336 | bytes 3440640 | tf_op jit(solution)/shard_map/dot_general | solution.py:62
  231.1 3.4 %fusion.57 = bf16[512,896]{1,0:T(8,128)(2,1)} fusion(bf16[14336,896]{1,0:T(8,128)(2,1)S(1)} %copy-done.3, bf16[512,14336]{1,0:T(8,128)(2,1)} %param.12), kind=kOutput, calls=%fused_computation.47 | convolution fusion | flops 822542336 | bytes 3440640 | tf_op jit(solution)/shard_map/dot_general | solution.py:62
  234.4 3.4 %fusion.60 = bf16[512,896]{1,0:T(8,128)(2,1)} fusion(bf16[14336,896]{1,0:T(8,128)(2,1)S(1)} %copy-done.3, bf16[512,14336]{1,0:T(8,128)(2,1)} %param.12), kind=kOutput, calls=%fused_computation.48 | convolution fusion | flops 822542336 | bytes 3440640 | tf_op jit(solution)/shard_map/dot_general | solution.py:62
  237.8 3.3 %fusion.63 = bf16[512,896]{1,0:T(8,128)(2,1)} fusion(bf16[14336,896]{1,0:T(8,128)(2,1)S(1)} %copy-done.3, bf16[512,14336]{1,0:T(8,128)(2,1)} %param.12), kind=kOutput, calls=%fused_computation.49 | convolution fusion | flops 822542336 | bytes 3440640 | tf_op jit(solution)/shard_map/dot_general | solution.py:62
  241.1 3.4 %fusion.66 = bf16[512,896]{1,0:T(8,128)(2,1)} fusion(bf16[14336,896]{1,0:T(8,128)(2,1)S(1)} %copy-done.3, bf16[512,14336]{1,0:T(8,128)(2,1)} %param.12), kind=kOutput, calls=%fused_computation.50 | convolution fusion | flops 822542336 | bytes 3440640 | tf_op jit(solution)/shard_map/dot_general | solution.py:62
  244.5 3.3 %fusion.69 = bf16[512,896]{1,0:T(8,128)(2,1)} fusion(bf16[14336,896]{1,0:T(8,128)(2,1)S(1)} %copy-done.3, bf16[512,14336]{1,0:T(8,128)(2,1)} %param.12), kind=kOutput, calls=%fused_computation.51 | convolution fusion | flops 822542336 | bytes 3440640 | tf_op jit(solution)/shard_map/dot_general | solution.py:62
  247.8 3.3 %fusion.72 = bf16[512,896]{1,0:T(8,128)(2,1)} fusion(bf16[14336,896]{1,0:T(8,128)(2,1)S(1)} %copy-done.3, bf16[512,14336]{1,0:T(8,128)(2,1)} %param.12), kind=kOutput, calls=%fused_computation.52 | convolution fusion | flops 822542336 | bytes 3440640 | tf_op jit(solution)/shard_map/dot_general | solution.py:62
  251.1 3.6 %fusion.75 = bf16[512,896]{1,0:T(8,128)(2,1)} fusion(bf16[14336,896]{1,0:T(8,128)(2,1)S(1)} %copy-done.3, bf16[512,14336]{1,0:T(8,128)(2,1)} %param.12), kind=kOutput, calls=%fused_computation.53 | convolution fusion | flops 822542336 | bytes 3440640 | tf_op jit(solution)/shard_map/dot_general | solution.py:62
  254.7 3.3 %fusion.78 = bf16[512,896]{1,0:T(8,128)(2,1)} fusion(bf16[14336,896]{1,0:T(8,128)(2,1)S(1)} %copy-done.3, bf16[512,14336]{1,0:T(8,128)(2,1)} %param.12), kind=kOutput, calls=%fused_computation.54 | convolution fusion | flops 822542336 | bytes 3440640 | tf_op jit(solution)/shard_map/dot_general | solution.py:62
  258.1 3.3 %fusion.81 = bf16[512,896]{1,0:T(8,128)(2,1)} fusion(bf16[14336,896]{1,0:T(8,128)(2,1)S(1)} %copy-done.3, bf16[512,14336]{1,0:T(8,128)(2,1)} %param.12), kind=kOutput, calls=%fused_computation.55 | convolution fusion | flops 822542336 | bytes 3440640 | tf_op jit(solution)/shard_map/dot_general | solution.py:62
  261.4 24.7 %fusion = f32[2048]{0:T(1024)S(1)} fusion(f32[1,2048,896]{1,2,0:T(8,128)} %copy.18, bf16[2048,2048]{1,0:T(8,128)(2,1)} %bitcast.27, bf16[2048,896]{1,0:T(8,128)(2,1)} %param.15, bf16[512,2048]{0,1:T(8,128)(2,1)} %bitcast.1, f32[512]{0:T(512)S(1)} %divide_select_fusion, bf16[512,896]{1,0:T(8,128)(2,1)} %fusion.81, bf16[512,896]{1,0:T(8,128)(2,1)} %fusion.78, ...), kind=kOutput, calls=%fused_computation.1 | convolution fusion | flops 9422305280 | bytes 36186112 | tf_op jit(solution)/shard_map/ri,dij->drj/dot_general | solution.py:84
  286.3 14.0 %all_to_all.10 = f32[8,1,64]{2,1,0:T(1,128)S(1)} all-to-all(f32[8,1,64]{2,1,0:T(1,128)S(1)} %broadcast_in_dim.9), channel_id=1, replica_groups=mesh['dp'=16,'mp'=8] {'mp'}, dimensions={0} | all-to-all | bytes 4096 | tf_op jit(solution)/shard_map/all_to_all | solution.py:17
  (25 shorter events, 4.9 us)
Async XLA Ops:
  6.5 2.2 copy-start
  6.5 62.1 %all-gather.8.cloned.1.call-start = ((), (), s32[]{:S(2)}) async-start(), calls=%async_computation.4 | async-start | bytes 3899392 | tf_op jit(solution)/shard_map/all_gather | solution.py:80
  7.3 197.1 %all-gather.4.cloned.1.call-start = ((), (), s32[]{:S(2)}) async-start(), calls=%async_computation.2 | async-start | bytes 27295744 | tf_op jit(solution)/shard_map/all_gather | solution.py:59
  8.0 253.4 %all-gather.6.cloned.1.call-start = ((), (), s32[]{:S(2)}) async-start(), calls=%async_computation.3 | async-start | bytes 8912896 | tf_op jit(solution)/shard_map/all_gather | solution.py:79
  13.8 8.5 %copy-start.2 = (s32[1,512]{1,0:T(1,128)S(1)}, s32[1,512]{1,0:T(1,128)}, u32[]{:S(2)}) copy-start(s32[1,512]{1,0:T(1,128)} %param.9) | copy-start | bytes 6148
  13.8 247.6 %all-to-all-start = ((bf16[8,512,256]{1,2,0:T(8,128)(2,1)}), bf16[8,512,256]{1,2,0:T(8,128)(2,1)}, u32[]{:S(2)}, u32[]{:S(2)}) async-start(bf16[8,512,256]{1,2,0:T(8,128)(2,1)} %broadcast_in_dim.7), calls=%async_computation | async-start | bytes 4194304 | tf_op jit(solution)/shard_map/all_to_all | solution.py:17
  204.3 20.0 %copy-start.3 = (bf16[14336,896]{1,0:T(8,128)(2,1)S(1)}, bf16[14336,896]{1,0:T(8,128)(2,1)}, u32[]{:S(2)}) copy-start(bf16[14336,896]{1,0:T(8,128)(2,1)} %all-gather.4.cloned.1.call-done) | copy-start | bytes 77070336
  261.4 39.4 %copy-start.1 = (bf16[4096,256]{1,0:T(8,128)(2,1)S(1)}, bf16[4096,256]{1,0:T(8,128)(2,1)}, u32[]{:S(2)}) copy-start(bf16[4096,256]{1,0:T(8,128)(2,1)} %param.13) | copy-start | bytes 6291460
Sparse Core Ops, SparseCore 0:
  9.1 59.5 all-gather.7
  70.3 133.9 all-gather.3
  206.0 52.8 all-gather.5
where the time goes:
time: 308 us; the launch traced here: 307 us
  waiting for transfers between devices  170 us (55%)
  matrix products  85.1 us (28%)
  blocking collectives  14 us (5%)
  between operations  13.8 us (4%)
  local copies, waits for them, and re-layouts  10.4 us (3%)
  starting transfers between devices  7.9 us (3%)
  other arithmetic  6.48 us (2%)
    all_gather x1, waiting for transfers between devices, per_device(): pieces = lax.all_gather(output_basis, 'dp', axis=0, tiled=True)  122 us
    dot_general x16, matrix products, per_device(): jnp.dot(grad_cols, pieces[member * shard_rows:(member + 1) * shard_rows],...  57.1 us
    all_gather x1, waiting for transfers between devices, per_device(): right_part = lax.all_gather(query_right, 'dp', axis=0, tiled=True)  46 us
    dot_general x1, matrix products, per_device(): jnp.einsum('ri,dij->drj', left_rows, conditioned, preferred_element_type=...  24.7 us
    all_to_all x1, blocking collectives, from_everyone(): lax.all_to_all(jnp.broadcast_to(array[None], (length, *array.shape)), axi...  14 us
    convert_element_type x1, local copies, waits for them, and re-layouts, per_device(): right_part.reshape(number * rank_rows, right_part.shape[2])  8.68 us
    all_to_all x1, starting transfers between devices, from_everyone(): lax.all_to_all(jnp.broadcast_to(array[None], (length, *array.shape)), axi...  7.83 us
  transfers between devices with their start and end apart: 4, of which 2 were waited for; matrix products, arithmetic and copies ran while one was open for 25% of the time, Pallas kernels for 0%

commit v1 on v0

v1 whole, which is shorter than its diff:
```python
import jax
import jax.numpy as jnp
from jax import lax
from jax.experimental import pallas as pl
from jax.experimental.pallas import tpu as pltpu
from jax.sharding import Mesh, PartitionSpec as P

damping = 0.5
f32 = jnp.float32
bf16 = jnp.bfloat16


def shifted(value, axis, step):
    size = lax.axis_size(axis)
    return lax.ppermute(value, axis, [(i, (i + step) % size) for i in range(size)])


def token_weights(doc_ids, doc_lengths):
    positions = jnp.arange(doc_ids.shape[1], dtype=jnp.int32)
    active = positions[None, :] < doc_lengths[:, None]
    matches = (doc_ids[:, :, None] == doc_ids[:, None, :]) & active[:, None, :]
    repeats = jnp.sum(matches.astype(f32), axis=2)
    return jnp.where(active, 1.0 / jnp.maximum(repeats, 1.0), 0.0)


def score_kernel(
    core_ref, own_ref, peer_ref, weight_ref, acts_ref, eig_ref, left_a, left_b, right_a, right_b,
    out_ref, scaled_ref, cond_ref, sums_ref, *, steps_in, steps_half, rank, x_size,
):
    step = pl.program_id(0)
    rows_in = acts_ref.shape[0]
    rows_q = left_a.shape[0]

    @pl.when(step == 0)
    def _():
        total = own_ref[...] + peer_ref[...].astype(f32)
        rotated = total.astype(bf16).astype(f32)
        scaled_ref[...] = (weight_ref[...] * rotated).astype(bf16)

    @pl.when(step < steps_in)
    def _():
        gradient = jnp.dot(acts_ref[...], scaled_ref[...], preferred_element_type=f32)
        conditioned = gradient / (eig_ref[...].astype(f32) + damping)
        start = pl.multiple_of(jnp.minimum(step, steps_in - 1) * rows_in, rows_in)
        cond_ref[pl.ds(start, rows_in), :] = conditioned.astype(bf16)

    def scored(left, right, slot):
        mixture = jnp.dot(left[...], cond_ref[...], preferred_element_type=f32)
        product = mixture * right[...].astype(f32)
        groups = product.reshape(rows_q // rank, rank, product.shape[1])
        part = jnp.sum(groups, axis=1)
        start = pl.multiple_of(slot * (rows_q // rank), rows_q // rank)
        sums_ref[pl.ds(start, rows_q // rank), :] = part

    @pl.when((step >= steps_in) & (step < steps_in + steps_half))
    def _():
        scored(left_a, right_a, jnp.clip(step - steps_in, 0, steps_half - 1))

    @pl.when(step >= steps_in + steps_half)
    def _():
        scored(left_b, right_b, jnp.clip(step - steps_in, steps_half, 2 * steps_half - 1))

    @pl.when(step == steps_in + 2 * steps_half - 1)
    def _():
        number = sums_ref.shape[0]
        values = jnp.sum(sums_ref[...], axis=1, keepdims=True)
        source = lax.broadcasted_iota(jnp.int32, (number, number), 0)
        target = lax.broadcasted_iota(jnp.int32, (number, number), 1)
        half = number // 2
        chips = half // x_size
        which = source // half
        parity = jnp.where(which == 0, core_ref[0], 1 - core_ref[0])
        inner = source % half
        place = (2 * (inner % chips) + parity) * x_size + inner // chips
        picked = jnp.where(place == target, values, 0.0)
        out_ref[...] = jnp.sum(picked, axis=0, keepdims=True)


def scores_of(core, own, peer, weights, acts, eig, left_a, left_b, right_a, right_b, rank, x_size):
    kin, tokens = acts.shape
    cols = own.shape[1]
    half = left_a.shape[0]
    steps_in = 4
    steps_half = 2
    rows_in = kin // steps_in
    rows_q = half // steps_half
    number = 2 * half // rank

    def first(g, core):
        return (jnp.minimum(g, steps_in - 1), 0)

    def second(g, core):
        return (jnp.clip(g - steps_in, 0, steps_half - 1), 0)

    def third(g, core):
        return (jnp.clip(g - steps_in - steps_half, 0, steps_half - 1), 0)

    def whole(g, core):
        return (0, 0)

    import functools

    body = functools.partial(
        score_kernel, steps_in=steps_in, steps_half=steps_half, rank=rank, x_size=x_size
    )
    return pl.pallas_call(
        body,
        grid_spec=pltpu.PrefetchScalarGridSpec(
            num_scalar_prefetch=1,
            grid=(steps_in + 2 * steps_half,),
            in_specs=[
                pl.BlockSpec((tokens, cols), whole),
                pl.BlockSpec((tokens, cols), whole),
                pl.BlockSpec((tokens, 1), whole),
                pl.BlockSpec((rows_in, tokens), first),
                pl.BlockSpec((rows_in, cols), first),
                pl.BlockSpec((rows_q, kin), second),
                pl.BlockSpec((rows_q, kin), third),
                pl.BlockSpec((rows_q, cols), second),
                pl.BlockSpec((rows_q, cols), third),
            ],
            out_specs=pl.BlockSpec((1, number), whole),
            scratch_shapes=[
                pltpu.VMEM((tokens, cols), bf16),
                pltpu.VMEM((kin, cols), bf16),
                pltpu.VMEM((number, cols), f32),
            ],
        ),
        out_shape=jax.ShapeDtypeStruct((1, number), f32),
        compiler_params=pltpu.CompilerParams(
            dimension_semantics=("arbitrary",), vmem_limit_bytes=48 * 1024 * 1024
        ),
        name="scores",
    )(core, own, peer, weights, acts, eig, left_a, left_b, right_a, right_b)


def per_device(
    doc_ids,
    doc_lengths,
    activations,
    out_grads,
    input_basis,
    output_basis,
    eigenvalues,
    query_left,
    query_right,
):
    tokens = activations.shape[0]
    rows, cols = output_basis.shape
    queries, rank, kin = query_left.shape
    n_y, n_zl, n_c = lax.axis_size("y"), lax.axis_size("zl"), lax.axis_size("c")
    n_zh, n_x = lax.axis_size("zh"), lax.axis_size("x")
    y, zl, core = lax.axis_index("y"), lax.axis_index("zl"), lax.axis_index("c")
    zh, x = lax.axis_index("zh"), lax.axis_index("x")
    chips = n_y * n_zl
    tile = 128

    block = jnp.concatenate([output_basis, query_right.reshape(queries * rank, cols)], axis=0)
    forth = lambda v: shifted(v, "y", 1)
    back = lambda v: shifted(v, "y", -1)
    across = lambda v: shifted(v, "zl", 1)
    sibling = lambda v: shifted(v, "c", 1)

    before, after, beside = forth(block), back(block), across(block)
    grads_out = jnp.stack(
        [
            lax.dynamic_slice(out_grads, (0, (2 * k + 1 - core) * rows), (tokens, rows))
            for k in range(chips)
        ]
    )
    grads_peer = sibling(grads_out)

    cut = 4 * tile
    before_beside_a = forth(beside[:cut])
    after_beside_a = back(beside[:cut])
    before_beside_b = across(before[cut:])
    after_beside_b = across(after[cut:])
    far_a = forth(before[:cut])
    far_b = back(after[cut:])
    far_beside_a = forth(before_beside_a[: 3 * tile])
    far_beside_b = across(far_a[3 * tile :])
    far_beside_c = back(after_beside_b[: 3 * tile])
    far_beside_d = across(far_b[3 * tile :])

    def chip(dy, dz):
        return ((y + dy) % n_y) * n_zl + (zl + dz) % n_zl

    pieces = [
        (chip(0, 0), 0, output_basis),
        (chip(3, 0), 0, before[:rows]),
        (chip(1, 0), 0, after[:rows]),
        (chip(0, 1), 0, beside[:rows]),
        (chip(3, 1), 0, before_beside_a),
        (chip(1, 1), 0, after_beside_a),
        (chip(3, 1), cut, before_beside_b[: rows - cut]),
        (chip(1, 1), cut, after_beside_b[: rows - cut]),
        (chip(2, 0), 0, far_a),
        (chip(2, 0), cut, far_b[: rows - cut]),
        (chip(2, 1), 0, far_beside_a),
        (chip(2, 1), 3 * tile, far_beside_b),
        (chip(2, 1), cut, far_beside_c),
    ]
    running_own = jnp.zeros((tokens, cols), f32)
    running_peer = jnp.zeros((tokens, cols), f32)
    for k, offset, piece in pieces:
        deep = piece.shape[0]
        mine = lax.dynamic_slice(out_grads, (0, (2 * k + core) * rows + offset), (tokens, deep))
        theirs = lax.dynamic_slice(grads_peer, (k, 0, offset), (1, tokens, deep))[0]
        running_peer = running_peer + jnp.dot(theirs, piece, preferred_element_type=f32)
        running_own = running_own + jnp.dot(mine, piece, preferred_element_type=f32)
    from_peer = sibling(running_peer.astype(bf16))

    share = lax.dot_general(
        input_basis, activations, (((0,), (1,)), ((), ())), preferred_element_type=f32
    ).astype(bf16)
    other = shifted(share, "zh", 1)
    pair = jnp.where(zh == 0, jnp.stack([share, other]), jnp.stack([other, share]))
    acts = lax.all_gather(pair, "x", axis=0)
    acts = jnp.swapaxes(acts, 0, 1).reshape(kin, tokens)

    mine_left = lax.dynamic_index_in_dim(query_left, x, 0, keepdims=False)
    left_chips = lax.all_to_all(
        jnp.broadcast_to(mine_left[None], (chips, rank, kin)), ("y", "zl"), 0, 0, tiled=True
    )
    left_own = lax.all_gather(left_chips, "x", axis=0).reshape(n_x * chips * rank, kin)
    left_peer = sibling(left_own)

    right_rows = queries * rank
    right_pieces = [
        (chip(0, 0), block[rows:]),
        (chip(3, 0), before[rows:]),
        (chip(1, 0), after[rows:]),
        (chip(0, 1), beside[rows:]),
        (chip(3, 1), before_beside_b[rows - cut :]),
        (chip(1, 1), after_beside_b[rows - cut :]),
        (chip(2, 0), far_b[rows - cut :]),
        (chip(2, 1), far_beside_d),
    ]
    right_own = jnp.zeros((n_x, chips, rank, cols), bf16)
    for k, piece in right_pieces:
        right_own = lax.dynamic_update_slice(
            right_own, piece.reshape(queries, 1, rank, cols), (0, k, 0, 0)
        )
    right_own = right_own.reshape(n_x * chips * rank, cols)
    right_peer = sibling(right_own)

    weights = token_weights(doc_ids, doc_lengths).reshape(tokens, 1)
    values = scores_of(
        core.reshape(1).astype(jnp.int32), running_own, from_peer, weights, acts, eigenvalues,
        left_own, left_peer, right_own, right_peer, rank, n_x,
    )
    values = values + lax.ppermute(values, "x", [(i, i ^ 1) for i in range(n_x)])
    values = values + lax.ppermute(values, "x", [(i, n_x - 1 - i) for i in range(n_x)])
    return values + shifted(values, "zh", 1)


def solution(mesh):
    parts = Mesh(mesh.devices.reshape(4, 2, 2, 2, 4), ("y", "zl", "c", "zh", "x"))
    dp, mp = ("y", "zl", "c"), ("zh", "x")
    return jax.shard_map(
        per_device,
        mesh=parts,
        in_specs=(
            P(dp, None),
            P(dp),
            P(dp, None),
            P(dp, None),
            P(None, mp),
            P(dp, mp),
            P(None, mp),
            P(dp, None, None),
            P(dp, None, mp),
        ),
        out_specs=P(dp, None),
        check_vma=False,
    )
```

time: 308 us -> 272 us (0.88)
  waiting for transfers between devices: 170 us -> 74.9 us
  local copies, waits for them, and re-layouts: 10.4 us -> 38.5 us
  starting transfers between devices: 7.9 us -> 33.1 us
  Pallas kernels: 0 us -> 16.9 us
  blocking collectives: 14 us -> 0 us
    all_gather x3 -> x2, waiting for transfers between devices: 167 us -> 0.01 us  [the longest x1 0.01 us: per_device(): acts = lax.all_gather(pair, 'x', axis=0)]
    ppermute x0 -> x21, waiting for transfers between devices: none -> 61.6 us  [the longest x19 57.6 us: shifted(): lax.ppermute(value, axis, [(i, (i + step) % size) for i in range(size)])]
    ppermute x0 -> x21, starting transfers between devices: none -> 27.8 us  [the longest x19 23.5 us: shifted(): lax.ppermute(value, axis, [(i, (i + step) % size) for i in range(size)])]
    unnamed x8 -> x57, local copies, waits for them, and re-layouts: 0.02 us -> 19.5 us
    pallas_call x0 -> x1, Pallas kernels: none -> 16.9 us  [scores_of(): pl.pallas_call(body, grid_spec=pltpu.PrefetchScalarGridSpec(num_scalar_pr...]
    all_to_all x1 -> x0, blocking collectives: 14 us -> none  [from_everyone(): lax.all_to_all(jnp.broadcast_to(array[None], (length, *array.shape)), axi...]
    all_to_all x1, waiting for transfers between devices: 0.01 us -> 13.2 us  [per_device(): lax.all_to_all(jnp.broadcast_to(mine_left[None], (chips, rank, kin)), ('y...]
    slice x0 -> x13, local copies, waits for them, and re-layouts: none -> 11 us  [the longest x1 2.84 us: per_device(): before_beside_b = across(before[cut:])]
  transfers between devices with their start and end apart: 4 -> 24, of which waited for: 2 -> 11; matrix products, arithmetic and copies ran while one was open for 25% -> 45% of each run, Pallas kernels for 0% -> 0%
where the time goes in v1:
time: 272 us; the launch traced here: 270 us
  matrix products  87.7 us (32%)
  waiting for transfers between devices  74.9 us (28%)
  local copies, waits for them, and re-layouts  38.5 us (14%)
  starting transfers between devices  33.1 us (12%)
  Pallas kernels  16.9 us (6%)
  between operations  14.7 us (5%)
  other arithmetic  4.59 us (2%)
    ppermute x19, waiting for transfers between devices, shifted(): lax.ppermute(value, axis, [(i, (i + step) % size) for i in range(size)])  57.6 us
    dot_general x13, matrix products, per_device(): running_own = running_own + jnp.dot(mine, piece, preferred_element_type=f32)  45.8 us
    dot_general x13, matrix products, per_device(): jnp.dot(theirs, piece, preferred_element_type=f32)  38.4 us
    ppermute x19, starting transfers between devices, shifted(): lax.ppermute(value, axis, [(i, (i + step) % size) for i in range(size)])  23.5 us
    unnamed x57, local copies, waits for them, and re-layouts  19.5 us
    pallas_call x1, Pallas kernels, scores_of(): pl.pallas_call(body, grid_spec=pltpu.PrefetchScalarGridSpec(num_scalar_pr...  16.9 us
    all_to_all x1, waiting for transfers between devices, per_device(): lax.all_to_all(jnp.broadcast_to(mine_left[None], (chips, rank, kin)), ('y...  13.2 us
  transfers between devices with their start and end apart: 24, of which 11 were waited for; matrix products, arithmetic and copies ran while one was open for 45% of the time, Pallas kernels for 0%

profile of v1, /device:TPU:0, one launch (start us, length us, event | category | flops | bytes accessed | tf_op | source)
XLA Modules:
  0.0 270.3 jit_solution(9305355116111912254)
XLA Ops:
  8.1 3.5 %convolution_convert_fusion = bf16[256,512]{1,0:T(8,128)(2,1)S(1)} fusion(bf16[4096,256]{1,0:T(8,128)(2,1)S(1)} %copy-done, bf16[512,4096]{1,0:T(8,128)(2,1)} %param.11), kind=kOutput, calls=%fused_computation.15 | convolution fusion | flops 1073872896 | bytes 6553600 | tf_op jit(solution)/shard_map/dot_general | solution.py:213
  11.6 4.0 %collective-permute-start.14 = (bf16[256,512]{1,0:T(8,128)(2,1)S(1)}, bf16[256,512]{1,0:T(8,128)(2,1)S(1)}, u32[]{:S(2)}, u32[]{:S(2)}) collective-permute-start(bf16[256,512]{1,0:T(8,128)(2,1)S(1)} %convolution_convert_fusion), channel_id=1, source_target_pairs={{0,4},{4,0},{1,5},{5,1},{2,6},{6,2},{3,7},{7,3},{8,12},{12,8},{9,1... | collective-permute-start | bytes 786440 | tf_op jit(solution)/shard_map/ppermute | solution.py:15
  15.7 6.3 %collective-permute-done.14 = bf16[256,512]{1,0:T(8,128)(2,1)S(1)} collective-permute-done((bf16[256,512]{1,0:T(8,128)(2,1)S(1)}, bf16[256,512]{1,0:T(8,128)(2,1)S(1)}, u32[]{:S(2)}, u32[]{:S(2)}) %collective-permute-start.14) | collective-permute-done | bytes 262176 | tf_op jit(solution)/shard_map/ppermute | solution.py:15
  42.7 5.2 %all-to-all-start = ((bf16[8,32,2048]{2,1,0:T(8,128)(2,1)}), bf16[8,32,2048]{2,1,0:T(8,128)(2,1)S(1)}, u32[]{:S(2)}, u32[]{:S(2)}) async-start(bf16[8,32,2048]{2,1,0:T(8,128)(2,1)} %broadcast_in_dim.22), calls=%async_computation | async-start | bytes 2097152 | tf_op jit(solution)/shard_map/all_to_all | solution.py:222
  52.7 13.2 %all-to-all-done = bf16[8,32,2048]{2,1,0:T(8,128)(2,1)S(1)} async-done(((bf16[8,32,2048]{2,1,0:T(8,128)(2,1)}), bf16[8,32,2048]{2,1,0:T(8,128)(2,1)S(1)}, u32[]{:S(2)}, u32[]{:S(2)}) %all-to-all-start) | async-done | bytes 1048608 | tf_op jit(solution)/shard_map/all_to_all | solution.py:222
  69.1 4.2 %fusion.24 = f32[512,896]{1,0:T(8,128)} fusion(bf16[896,896]{1,0:T(8,128)(2,1)} %param.14, bf16[512,14336]{1,0:T(8,128)(2,1)} %param.12, s32[]{:T(128)S(6)} %select_n.233), kind=kOutput, calls=%fused_computation.37 | convolution fusion | flops 822083584 | bytes 4358148 | tf_op jit(solution)/shard_map/dot_general | solution.py:210
  73.3 29.4 %collective-permute-done = bf16[1024,896]{1,0:T(8,128)(2,1)} collective-permute-done((bf16[1024,896]{1,0:T(8,128)(2,1)}, bf16[1024,896]{1,0:T(8,128)(2,1)}, u32[]{:S(2)}, u32[]{:S(2)}) %collective-permute-start) | collective-permute-done | bytes 1835040 | tf_op jit(solution)/shard_map/ppermute | solution.py:15
  116.4 4.2 %fusion.2 = f32[512,896]{1,0:T(8,128)} fusion(bf16[1024,896]{1,0:T(8,128)(2,1)} %collective-permute-done.2, bf16[512,14336]{1,0:T(8,128)(2,1)} %param.12, s32[]{:T(128)S(6)} %select_n.239), kind=kOutput, calls=%fused_computation.5 | convolution fusion | flops 822083584 | bytes 4358148 | tf_op jit(solution)/shard_map/dot_general | solution.py:210
  120.6 4.2 %fusion.6 = f32[512,896]{1,0:T(8,128)} fusion(bf16[1024,896]{1,0:T(8,128)(2,1)} %collective-permute-done.1, bf16[512,14336]{1,0:T(8,128)(2,1)} %param.12, s32[]{:T(128)S(6)} %select_n.237), kind=kOutput, calls=%fused_computation.9 | convolution fusion | flops 822083584 | bytes 4358148 | tf_op jit(solution)/shard_map/dot_general | solution.py:210
  124.9 5.5 %collective-permute-done.7 = bf16[512,896]{1,0:T(8,128)(2,1)} collective-permute-done((bf16[512,896]{1,0:T(8,128)(2,1)}, bf16[512,896]{1,0:T(8,128)(2,1)}, u32[]{:S(2)}, u32[]{:S(2)}) %collective-permute-start.7) | collective-permute-done | bytes 917536 | tf_op jit(solution)/shard_map/ppermute | solution.py:15
  132.0 4.1 %fusion.10 = f32[512,896]{1,0:T(8,128)} fusion(bf16[1024,896]{1,0:T(8,128)(2,1)} %collective-permute-done, bf16[512,14336]{1,0:T(8,128)(2,1)} %param.12, s32[]{:T(128)S(6)} %select_n.235), kind=kOutput, calls=%fused_computation.13 | convolution fusion | flops 822083584 | bytes 4358148 | tf_op jit(solution)/shard_map/dot_general | solution.py:210
  137.1 11.1 %collective-permute-done.3 = bf16[512,896]{1,0:T(8,128)(2,1)S(1)} collective-permute-done((bf16[512,896]{1,0:T(8,128)(2,1)S(1)}, bf16[512,896]{1,0:T(8,128)(2,1)S(1)}, u32[]{:S(2)}, u32[]{:S(2)}) %collective-permute-start.3) | collective-permute-done | bytes 917536 | tf_op jit(solution)/shard_map/ppermute | solution.py:15
  164.3 3.3 %fusion.43 = f32[512,896]{1,0:T(8,128)} fusion(bf16[512,896]{1,0:T(8,128)(2,1)} %collective-permute-done.7, bf16[512,14336]{1,0:T(8,128)(2,1)} %param.12, s32[]{:T(128)S(6)} %select_n.245), kind=kOutput, calls=%fused_computation.57 | convolution fusion | flops 469762048 | bytes 3276804 | tf_op jit(solution)/shard_map/dot_general | solution.py:210
  167.7 3.0 %fusion.47 = f32[512,896]{1,0:T(8,128)} fusion(bf16[512,896]{1,0:T(8,128)(2,1)S(1)} %collective-permute-done.3, bf16[512,14336]{1,0:T(8,128)(2,1)} %param.12, s32[]{:T(128)S(6)} %select_n.240), kind=kOutput, calls=%fused_computation.61 | convolution fusion | flops 469762048 | bytes 3276804 | tf_op jit(solution)/shard_map/dot_general | solution.py:210
  180.6 3.1 %copy.40 = bf16[2,4,256,512]{3,2,1,0:T(8,128)(2,1)} copy(bf16[2,4,256,512]{3,2,0,1:T(8,128)(2,1)} %bitcast.119) | data formatting | bytes 4194304 | tf_op jit(solution)/shard_map/transpose | solution.py:219
  183.7 3.1 %fusion.68 = f32[512,896]{1,0:T(8,128)} fusion(bf16[384,896]{1,0:T(8,128)(2,1)} %collective-permute-done.9, bf16[512,14336]{1,0:T(8,128)(2,1)} %param.12, s32[]{:T(128)S(6)} %select_n.247), kind=kOutput, calls=%fused_computation.78 | convolution fusion | flops 352321536 | bytes 2916356 | tf_op jit(solution)/shard_map/dot_general | solution.py:210
  199.9 4.2 %fusion = f32[512,896]{1,0:T(8,128)} fusion(bf16[1024,896]{1,0:T(8,128)(2,1)} %collective-permute-done.2, bf16[8,512,896]{2,1,0:T(8,128)(2,1)} %collective-permute-done.12, s32[]{:T(128)S(6)} %select_n.261), kind=kOutput, calls=%fused_computation.3 | convolution fusion | flops 822083584 | bytes 4358148 | tf_op jit(solution)/shard_map/dot_general | solution.py:209
  204.1 4.2 %fusion.4 = f32[512,896]{1,0:T(8,128)} fusion(bf16[1024,896]{1,0:T(8,128)(2,1)} %collective-permute-done.1, bf16[8,512,896]{2,1,0:T(8,128)(2,1)} %collective-permute-done.12, s32[]{:T(128)S(6)} %select_n.260), kind=kOutput, calls=%fused_computation.7 | convolution fusion | flops 822083584 | bytes 4358148 | tf_op jit(solution)/shard_map/dot_general | solution.py:209
  210.9 3.6 %fusion.15 = f32[512,896]{1,0:T(8,128)} fusion(bf16[896,896]{1,0:T(8,128)(2,1)S(1)} %copy-done.21, bf16[8,512,896]{2,1,0:T(8,128)(2,1)} %collective-permute-done.12, s32[]{:T(128)S(6)} %select_n.258), kind=kOutput, calls=%fused_computation.20 | convolution fusion | flops 822083584 | bytes 4358148 | tf_op jit(solution)/shard_map/dot_general | solution.py:209
  214.5 4.2 %fusion.8 = f32[512,896]{1,0:T(8,128)} fusion(bf16[1024,896]{1,0:T(8,128)(2,1)} %collective-permute-done, bf16[8,512,896]{2,1,0:T(8,128)(2,1)} %collective-permute-done.12, s32[]{:T(128)S(6)} %select_n.259), kind=kOutput, calls=%fused_computation.11 | convolution fusion | flops 822083584 | bytes 4358148 | tf_op jit(solution)/shard_map/dot_general | solution.py:209
  218.8 6.9 %add_convert_fusion = bf16[512,896]{1,0:T(8,128)(2,1)} fusion(f32[512,896]{1,0:T(8,128)} %fusion.75, f32[512,896]{1,0:T(8,128)S(1)} %fusion.53, f32[512,896]{1,0:T(8,128)S(1)} %fusion.26, f32[512,896]{1,0:T(8,128)S(1)} %fusion.34, f32[512,896]{1,0:T(8,128)S(1)} %fusion.56, f32[512,896]{1,0:T(8,128)S(1)} %fusion.30, f32[512,896]{1,0:T(8,128)S(1)} %fusion.36, ...), kind=kOutput, calls=%fused_computation.1 | convolution fusion | flops 358285312 | bytes 24018948 | tf_op jit(solution)/shard_map/dot_general | solution.py:209
  227.4 5.2 %add_add_fusion.own_ref = f32[512,896]{1,0:T(8,128)S(1)} fusion(f32[512,896]{1,0:T(8,128)S(1)} %copy-done.11, f32[512,896]{1,0:T(8,128)S(1)} %copy-done.7, f32[512,896]{1,0:T(8,128)S(1)} %copy-done.4, f32[512,896]{1,0:T(8,128)S(1)} %copy-done.8, f32[512,896]{1,0:T(8,128)S(1)} %copy-done.5, f32[512,896]{1,0:T(8,128)S(1)} %copy-done.6, ...), kind=kOutput, calls=%fused_computation.2 | convolution fusion | flops 357826560 | bytes 24936452 | tf_op jit(solution)/shard_map/dot_general | solution.py:210
  232.6 16.9 %scores.1 = f32[1,64]{1,0:T(1,128)S(1)} custom-call(s32[1]{0:T(128)} %bitcast.core_ref, f32[512,896]{1,0:T(8,128)S(1)} %add_add_fusion.own_ref, bf16[512,896]{1,0:T(8,128)(2,1)S(1)} %collective-permute-done.13.peer_ref, f32[512,1]{1,0:T(8,128)S(1)} %fusion.74.weight_ref, bf16[2048,512]{1,0:T(8,128)(2,1)} %bitcast.115, bf16[2048,896]{1,0:T(8,128)(2,1)} %eig_ref.1, ...), custom_call_target="tpu_custom_call" | custom-call | tf_op jit(solution)/shard_map/scores/pallas_call | solution.py:106
  257.8 3.6 %collective-permute-start.20 = (f32[1,64]{1,0:T(1,128)S(1)}, f32[1,64]{1,0:T(1,128)S(1)}, u32[]{:S(2)}, u32[]{:S(2)}) collective-permute-start(f32[1,64]{1,0:T(1,128)S(1)} %add.454), channel_id=1, source_target_pairs={{0,4},{4,0},{1,5},{5,1},{2,6},{6,2},{3,7},{7,3},{8,12},{12,8},{9,1... | collective-permute-start | bytes 776 | tf_op jit(solution)/shard_map/ppermute | solution.py:15
  (147 shorter events, 99.3 us)
Async XLA Ops:
  6.5 174.0 %all-gather.4.cloned.1.call-start = ((), (), s32[]{:S(2)}) async-start(), calls=%async_computation.1 | async-start | bytes 2621440 | tf_op jit(solution)/shard_map/all_gather | solution.py:218
  11.6 10.3 %collective-permute-start.14 = (bf16[256,512]{1,0:T(8,128)(2,1)S(1)}, bf16[256,512]{1,0:T(8,128)(2,1)S(1)}, u32[]{:S(2)}, u32[]{:S(2)}) collective-permute-start(bf16[256,512]{1,0:T(8,128)(2,1)S(1)} %convolution_convert_fusion), channel_id=1, source_target_pairs={{0,4},{4,0},{1,5},{5,1},{2,6},{6,2},{3,7},{7,3},{8,12},{12,8},{9,1... | collective-permute-start | bytes 786440 | tf_op jit(solution)/shard_map/ppermute | solution.py:15
  40.6 146.5 %collective-permute-start.12 = (bf16[8,512,896]{2,1,0:T(8,128)(2,1)}, bf16[8,512,896]{2,1,0:T(8,128)(2,1)}, u32[]{:S(2)}, u32[]{:S(2)}) collective-permute-start(bf16[8,512,896]{2,1,0:T(8,128)(2,1)} %bitcast_dynamic-update-slice_fusion), channel_id=1, source_target_pairs={{0,8},{8,0},{1,9},{9,1},{2,10},{10,2},{3,11},{11,3},{4,12},{12,4},... | collective-permute-start | bytes 22020104 | tf_op jit(solution)/shard_map/ppermute | solution.py:15
  42.7 23.3 %all-to-all-start = ((bf16[8,32,2048]{2,1,0:T(8,128)(2,1)}), bf16[8,32,2048]{2,1,0:T(8,128)(2,1)S(1)}, u32[]{:S(2)}, u32[]{:S(2)}) async-start(bf16[8,32,2048]{2,1,0:T(8,128)(2,1)} %broadcast_in_dim.22), calls=%async_computation | async-start | bytes 2097152 | tf_op jit(solution)/shard_map/all_to_all | solution.py:222
  47.9 138.9 %all-gather.6.cloned.1.call-start = ((), (), s32[]{:S(2)}) async-start(), calls=%async_computation.2 | async-start | bytes 5242880 | tf_op jit(solution)/shard_map/all_gather | solution.py:225
  50.7 52.0 %collective-permute-start = (bf16[1024,896]{1,0:T(8,128)(2,1)}, bf16[1024,896]{1,0:T(8,128)(2,1)}, u32[]{:S(2)}, u32[]{:S(2)}) collective-permute-start(bf16[1024,896]{1,0:T(8,128)(2,1)} %pad_maximum_fusion), channel_id=1, source_target_pairs={{0,32},{32,64},{64,96},{96,0},{1,33},{33,65},{65,97},{97,1},{2,34}... | collective-permute-start | bytes 5505032 | tf_op jit(solution)/shard_map/ppermute | solution.py:15
  67.0 40.9 %collective-permute-start.1 = (bf16[1024,896]{1,0:T(8,128)(2,1)}, bf16[1024,896]{1,0:T(8,128)(2,1)}, u32[]{:S(2)}, u32[]{:S(2)}) collective-permute-start(bf16[1024,896]{1,0:T(8,128)(2,1)} %pad_maximum_fusion), channel_id=1, source_target_pairs={{0,96},{32,0},{64,32},{96,64},{1,97},{33,1},{65,33},{97,65},{2,98}... | collective-permute-start | bytes 5505032 | tf_op jit(solution)/shard_map/ppermute | solution.py:15
  67.1 45.1 %collective-permute-start.2 = (bf16[1024,896]{1,0:T(8,128)(2,1)}, bf16[1024,896]{1,0:T(8,128)(2,1)}, u32[]{:S(2)}, u32[]{:S(2)}) collective-permute-start(bf16[1024,896]{1,0:T(8,128)(2,1)} %pad_maximum_fusion), channel_id=1, source_target_pairs={{0,16},{16,0},{1,17},{17,1},{2,18},{18,2},{3,19},{19,3},{4,20},{20... | collective-permute-start | bytes 5505032 | tf_op jit(solution)/shard_map/ppermute | solution.py:15
  105.5 24.8 %collective-permute-start.7 = (bf16[512,896]{1,0:T(8,128)(2,1)}, bf16[512,896]{1,0:T(8,128)(2,1)}, u32[]{:S(2)}, u32[]{:S(2)}) collective-permute-start(bf16[512,896]{1,0:T(8,128)(2,1)} %get-tuple-element.6), channel_id=1, source_target_pairs={{0,32},{32,64},{64,96},{96,0},{1,33},{33,65},{65,97},{97,1},{2,34}... | collective-permute-start | bytes 2752520 | tf_op jit(solution)/shard_map/ppermute | solution.py:15
  109.1 41.3 %collective-permute-start.8 = (bf16[512,896]{1,0:T(8,128)(2,1)S(1)}, bf16[512,896]{1,0:T(8,128)(2,1)S(1)}, u32[]{:S(2)}, u32[]{:S(2)}) collective-permute-start(bf16[512,896]{1,0:T(8,128)(2,1)S(1)} %slice.82), channel_id=1, source_target_pairs={{0,96},{32,0},{64,32},{96,64},{1,97},{33,1},{65,33},{97,65},{2,98}... | collective-permute-start | bytes 2752520 | tf_op jit(solution)/shard_map/ppermute | solution.py:15
  110.7 43.6 %collective-permute-start.6 = (bf16[512,896]{1,0:T(8,128)(2,1)S(1)}, bf16[512,896]{1,0:T(8,128)(2,1)S(1)}, u32[]{:S(2)}, u32[]{:S(2)}) collective-permute-start(bf16[512,896]{1,0:T(8,128)(2,1)S(1)} %slice.82), channel_id=1, source_target_pairs={{0,16},{16,0},{1,17},{17,1},{2,18},{18,2},{3,19},{19,3},{4,20},{20... | collective-permute-start | bytes 2752520 | tf_op jit(solution)/shard_map/ppermute | solution.py:15
  113.4 34.8 %collective-permute-start.3 = (bf16[512,896]{1,0:T(8,128)(2,1)S(1)}, bf16[512,896]{1,0:T(8,128)(2,1)S(1)}, u32[]{:S(2)}, u32[]{:S(2)}) collective-permute-start(bf16[512,896]{1,0:T(8,128)(2,1)S(1)} %slice.79), channel_id=1, source_target_pairs={{0,32},{32,64},{64,96},{96,0},{1,33},{33,65},{65,97},{97,1},{2,34}... | collective-permute-start | bytes 2752520 | tf_op jit(solution)/shard_map/ppermute | solution.py:15
  130.4 29.7 %collective-permute-start.5 = (bf16[512,896]{1,0:T(8,128)(2,1)S(1)}, bf16[512,896]{1,0:T(8,128)(2,1)S(1)}, u32[]{:S(2)}, u32[]{:S(2)}) collective-permute-start(bf16[512,896]{1,0:T(8,128)(2,1)S(1)} %copy-done.23), channel_id=1, source_target_pairs={{0,16},{16,0},{1,17},{17,1},{2,18},{18,2},{3,19},{19,3},{4,20},{20... | collective-permute-start | bytes 2752520 | tf_op jit(solution)/shard_map/ppermute | solution.py:15
  148.2 23.3 %collective-permute-start.4 = (bf16[512,896]{1,0:T(8,128)(2,1)S(1)}, bf16[512,896]{1,0:T(8,128)(2,1)S(1)}, u32[]{:S(2)}, u32[]{:S(2)}) collective-permute-start(bf16[512,896]{1,0:T(8,128)(2,1)S(1)} %slice.79), channel_id=1, source_target_pairs={{0,96},{32,0},{64,32},{96,64},{1,97},{33,1},{65,33},{97,65},{2,98}... | collective-permute-start | bytes 2752520 | tf_op jit(solution)/shard_map/ppermute | solution.py:15
  150.5 27.3 %collective-permute-start.10 = (bf16[128,896]{1,0:T(8,128)(2,1)S(1)}, bf16[128,896]{1,0:T(8,128)(2,1)S(1)}, u32[]{:S(2)}, u32[]{:S(2)}) collective-permute-start(bf16[128,896]{1,0:T(8,128)(2,1)S(1)} %slice.87), channel_id=1, source_target_pairs={{0,16},{16,0},{1,17},{17,1},{2,18},{18,2},{3,19},{19,3},{4,20},{20... | collective-permute-start | bytes 688136 | tf_op jit(solution)/shard_map/ppermute | solution.py:15
  154.3 29.4 %collective-permute-start.9 = (bf16[384,896]{1,0:T(8,128)(2,1)}, bf16[384,896]{1,0:T(8,128)(2,1)}, u32[]{:S(2)}, u32[]{:S(2)}) collective-permute-start(bf16[384,896]{1,0:T(8,128)(2,1)} %slice.86), channel_id=1, source_target_pairs={{0,32},{32,64},{64,96},{96,0},{1,33},{33,65},{65,97},{97,1},{2,34}... | collective-permute-start | bytes 2064392 | tf_op jit(solution)/shard_map/ppermute | solution.py:15
  160.1 58.7 %collective-permute-start.11 = (bf16[384,896]{1,0:T(8,128)(2,1)}, bf16[384,896]{1,0:T(8,128)(2,1)}, u32[]{:S(2)}, u32[]{:S(2)}) collective-permute-start(bf16[384,896]{1,0:T(8,128)(2,1)} %slice.83), channel_id=1, source_target_pairs={{0,96},{32,0},{64,32},{96,64},{1,97},{33,1},{65,33},{97,65},{2,98}... | collective-permute-start | bytes 2064392 | tf_op jit(solution)/shard_map/ppermute | solution.py:15
  171.5 6.1 %collective-permute-start.16 = (bf16[128,896]{1,0:T(8,128)(2,1)S(1)}, bf16[128,896]{1,0:T(8,128)(2,1)S(1)}, u32[]{:S(2)}, u32[]{:S(2)}) collective-permute-start(bf16[128,896]{1,0:T(8,128)(2,1)S(1)} %slice.93), channel_id=1, source_target_pairs={{0,16},{16,0},{1,17},{17,1},{2,18},{18,2},{3,19},{19,3},{4,20},{20... | collective-permute-start | bytes 688136 | tf_op jit(solution)/shard_map/ppermute | solution.py:15
  177.7 54.9 %collective-permute-start.17 = (bf16[1024,896]{1,0:T(8,128)(2,1)S(1)}, bf16[1024,896]{1,0:T(8,128)(2,1)}, u32[]{:S(2)}, u32[]{:S(2)}) collective-permute-start(bf16[1024,896]{1,0:T(8,128)(2,1)S(1)} %bitcast.113), channel_id=1, source_target_pairs={{0,8},{8,0},{1,9},{9,1},{2,10},{10,2},{3,11},{11,3},{4,12},{12,4},... | collective-permute-start | bytes 5505032 | tf_op jit(solution)/shard_map/ppermute | solution.py:15
  186.8 45.8 %collective-permute-start.15 = (bf16[1024,2048]{1,0:T(8,128)(2,1)}, bf16[1024,2048]{1,0:T(8,128)(2,1)}, u32[]{:S(2)}, u32[]{:S(2)}) collective-permute-start(bf16[1024,2048]{1,0:T(8,128)(2,1)} %bitcast.116), channel_id=1, source_target_pairs={{0,8},{8,0},{1,9},{9,1},{2,10},{10,2},{3,11},{11,3},{4,12},{12,4},... | collective-permute-start | bytes 12582920 | tf_op jit(solution)/shard_map/ppermute | solution.py:15
  225.7 6.8 %collective-permute-start.13 = (bf16[512,896]{1,0:T(8,128)(2,1)}, bf16[512,896]{1,0:T(8,128)(2,1)S(1)}, u32[]{:S(2)}, u32[]{:S(2)}) collective-permute-start(bf16[512,896]{1,0:T(8,128)(2,1)} %add_convert_fusion), channel_id=1, source_target_pairs={{0,8},{8,0},{1,9},{9,1},{2,10},{10,2},{3,11},{11,3},{4,12},{12,4},... | collective-permute-start | bytes 2752520 | tf_op jit(solution)/shard_map/ppermute | solution.py:15
  249.5 3.6 %collective-permute-start.18 = (f32[1,64]{1,0:T(1,128)S(1)}, f32[1,64]{1,0:T(1,128)S(1)}, u32[]{:S(2)}, u32[]{:S(2)}) collective-permute-start(f32[1,64]{1,0:T(1,128)S(1)} %scores.1), channel_id=1, source_target_pairs={{0,1},{1,0},{2,3},{3,2},{4,5},{5,4},{6,7},{7,6},{8,9},{9,8},{10,11... | collective-permute-start | bytes 776 | tf_op jit(solution)/shard_map/ppermute | solution.py:252
  253.1 4.8 %collective-permute-start.19 = (f32[1,64]{1,0:T(1,128)S(1)}, f32[1,64]{1,0:T(1,128)S(1)}, u32[]{:S(2)}, u32[]{:S(2)}) collective-permute-start(f32[1,64]{1,0:T(1,128)S(1)} %add.453), channel_id=1, source_target_pairs={{0,3},{1,2},{2,1},{3,0},{4,7},{5,6},{6,5},{7,4},{8,11},{9,10},{10,... | collective-permute-start | bytes 776 | tf_op jit(solution)/shard_map/ppermute | solution.py:253
  257.8 5.1 %collective-permute-start.20 = (f32[1,64]{1,0:T(1,128)S(1)}, f32[1,64]{1,0:T(1,128)S(1)}, u32[]{:S(2)}, u32[]{:S(2)}) collective-permute-start(f32[1,64]{1,0:T(1,128)S(1)} %add.454), channel_id=1, source_target_pairs={{0,4},{4,0},{1,5},{5,1},{2,6},{6,2},{3,7},{7,3},{8,12},{12,8},{9,1... | collective-permute-start | bytes 776 | tf_op jit(solution)/shard_map/ppermute | solution.py:15
  (26 other events, 202.1 us)
Sparse Core Ops, SparseCore 0:
  23.0 32.5 all-gather.3
  67.1 47.5 all-gather.5

commit v2 on v0

v2 whole, which is shorter than its diff:
```python
import functools

import jax
import jax.numpy as jnp
from jax import lax
from jax.experimental import pallas as pl
from jax.experimental.pallas import tpu as pltpu
from jax.sharding import Mesh, PartitionSpec as P

damping = 0.5
f32 = jnp.float32
bf16 = jnp.bfloat16


def shifted(value, axis, step):
    size = lax.axis_size(axis)
    return lax.ppermute(value, axis, [(i, (i + step) % size) for i in range(size)])


def token_weights(doc_ids, doc_lengths):
    positions = jnp.arange(doc_ids.shape[1], dtype=jnp.int32)
    active = positions[None, :] < doc_lengths[:, None]
    matches = (doc_ids[:, :, None] == doc_ids[:, None, :]) & active[:, None, :]
    repeats = jnp.sum(matches.astype(f32), axis=2)
    return jnp.where(active, 1.0 / jnp.maximum(repeats, 1.0), 0.0)


def score_kernel(
    chips_ref, tiles_ref, core_ref, mine, more, own_weight_ref, peer_weight_ref, own_acts,
    peer_acts, eig, left, *refs,
):
    rights = refs[:8]
    own_out, peer_out = refs[8:10]
    (
        mine_ref, more_ref, acts_ref, eig_ref, left_ref, right_ref, scaled_ref, cond_ref, sums_ref,
        sems, tile_sems,
    ) = refs[10:]
    tiles, rows_in, tokens = own_acts.shape
    n_x, chips, rank, kin = left.shape
    cols = eig.shape[1]
    tile = 128
    queries = n_x * chips

    tile_copies = []
    for at in range(tiles):
        start = pl.multiple_of(tiles_ref[at] * rows_in, rows_in)
        tile_copies.append(
            [
                pltpu.make_async_copy(own_acts.at[at], acts_ref.at[0, at], tile_sems.at[0, at]),
                pltpu.make_async_copy(peer_acts.at[at], acts_ref.at[1, at], tile_sems.at[1, at]),
                pltpu.make_async_copy(
                    eig.at[pl.ds(start, rows_in), :],
                    eig_ref.at[pl.ds(start, rows_in), :],
                    tile_sems.at[2, at],
                ),
            ]
        )
    left_copy = pltpu.make_async_copy(left, left_ref, sems.at[3])
    right_copies = [
        [
            pltpu.make_async_copy(
                piece.at[pl.ds(piece.shape[0] - tile + q * rank, rank), :],
                right_ref.at[q, chips_ref[index]],
                sems.at[4 + index * n_x + q],
            )
            for q in range(n_x)
        ]
        for index, piece in enumerate(rights)
    ]
    sum_copies = [
        pltpu.make_async_copy(mine, mine_ref, sems.at[4 + len(rights) * n_x]),
        pltpu.make_async_copy(more, more_ref, sems.at[5 + len(rights) * n_x]),
    ]
    for copy in sum_copies:
        copy.start()
    for group in tile_copies:
        for copy in group:
            copy.start()
    left_copy.start()
    for group in right_copies:
        for copy in group:
            copy.start()

    for copy in sum_copies:
        copy.wait()
    for index, (weight, mine_at, more_at) in enumerate(
        ((own_weight_ref, tokens, 0), (peer_weight_ref, 0, tokens))
    ):
        total = mine_ref[mine_at : mine_at + tokens, :].astype(f32)
        total = total + more_ref[more_at : more_at + tokens, :].astype(f32)
        rotated = total.astype(bf16).astype(f32)
        scaled_ref[index] = (weight[...] * rotated).astype(bf16)

    for first in range(0, tiles, 2):
        pair = (first, first + 1)
        for at in pair:
            for copy in tile_copies[at]:
                copy.wait()
        starts = [pl.multiple_of(tiles_ref[at] * rows_in, rows_in) for at in pair]
        scales = [
            1.0 / (eig_ref[pl.ds(start, rows_in), :].astype(f32) + damping) for start in starts
        ]
        for index in range(2):
            acts = acts_ref[index, first : first + 2].reshape(2 * rows_in, tokens)
            gradient = jnp.dot(acts, scaled_ref[index], preferred_element_type=f32)
            for half_at, (start, scale) in enumerate(zip(starts, scales)):
                cond_ref[pl.ds(start, rows_in), index * cols : (index + 1) * cols] = (
                    gradient[half_at * rows_in : (half_at + 1) * rows_in] * scale
                ).astype(bf16)

    left_copy.wait()
    for group in right_copies:
        for copy in group:
            copy.wait()
    wide = 2 * tile
    half = n_x // 2
    for part in range(2):
        rows = left_ref[part * half : (part + 1) * half].reshape(half * chips * rank, kin)
        for at in range(0, 2 * cols, wide):
            mixture = jnp.dot(rows, cond_ref[:, at : at + wide], preferred_element_type=f32)
            for one in range(at, at + wide, tile):
                index, column = one // cols, one % cols
                right = right_ref[part * half : (part + 1) * half, :, :, column : column + tile]
                right = right.reshape(half * chips * rank, tile).astype(f32)
                product = mixture[:, one - at : one - at + tile] * right
                groups = jnp.sum(product.reshape(half * chips, rank, tile), axis=1)
                rows_at = part * half * chips
                if column == 0:
                    sums_ref[index, rows_at : rows_at + half * chips, :] = groups
                else:
                    sums_ref[index, rows_at : rows_at + half * chips, :] += groups

    number = own_out.shape[1]
    source = lax.broadcasted_iota(jnp.int32, (queries, number), 0)
    target = lax.broadcasted_iota(jnp.int32, (queries, number), 1)
    place = (2 * (source % chips) + core_ref[0]) * n_x + source // chips
    for index, out in enumerate((own_out, peer_out)):
        values = jnp.sum(sums_ref[index], axis=1, keepdims=True)
        out[...] = jnp.sum(jnp.where(place == target, values, 0.0), axis=0, keepdims=True)


def scores_of(chips_at, tiles_at, core, mine, more, weights, acts, eig, left, rights, number):
    tokens = acts[0].shape[2]
    kin, cols = eig.shape
    n_x, chips, rank, _ = left.shape
    scalars = pl.BlockSpec(memory_space=pltpu.SMEM)
    held = pl.BlockSpec(memory_space=pltpu.VMEM)
    anywhere = pl.BlockSpec(memory_space=pltpu.HBM)
    return pl.pallas_call(
        score_kernel,
        in_specs=[*[scalars] * 3, *[anywhere] * 2, *[held] * 2, *[anywhere] * 12],
        out_specs=[held, held],
        scratch_shapes=[
            pltpu.VMEM(mine.shape, bf16),
            pltpu.VMEM(more.shape, bf16),
            pltpu.VMEM((2, *acts[0].shape), bf16),
            pltpu.VMEM(eig.shape, bf16),
            pltpu.VMEM(left.shape, bf16),
            pltpu.VMEM((n_x, chips, rank, cols), bf16),
            pltpu.VMEM((2, tokens, cols), bf16),
            pltpu.VMEM((kin, 2 * cols), bf16),
            pltpu.VMEM((2, n_x * chips, 128), f32),
            pltpu.SemaphoreType.DMA((6 + 8 * n_x,)),
            pltpu.SemaphoreType.DMA((3, acts[0].shape[0])),
        ],
        out_shape=[jax.ShapeDtypeStruct((1, number), f32)] * 2,
        compiler_params=pltpu.CompilerParams(vmem_limit_bytes=62 * 1024 * 1024),
        name="scores",
    )(chips_at, tiles_at, core, mine, more, *weights, *acts, eig, left, *rights)


def cut_kernel(*refs, cuts):
    count = len(cuts)
    sems = refs[-1]
    copies = [
        pltpu.make_async_copy(
            refs[at].at[pl.ds(start, size)], refs[count + at], sems.at[at]
        )
        for at, (start, size) in enumerate(cuts)
    ]
    for copy in copies:
        copy.start()
    for copy in copies:
        copy.wait()


def cut_out(arrays, cuts):
    return pl.pallas_call(
        functools.partial(cut_kernel, cuts=cuts),
        in_specs=[pl.BlockSpec(memory_space=pltpu.HBM)] * len(arrays),
        out_specs=[pl.BlockSpec(memory_space=pltpu.VMEM)] * len(arrays),
        out_shape=[
            jax.ShapeDtypeStruct((size, array.shape[1]), array.dtype)
            for array, (_, size) in zip(arrays, cuts)
        ],
        scratch_shapes=[pltpu.SemaphoreType.DMA((len(arrays),))],
        name="cut",
    )(*arrays)


def accumulate_kernel(places_ref, mine, theirs, *refs, plan, carried):
    count = sum(len(cuts) for cuts in plan)
    pieces = refs[:count]
    before = refs[count] if carried else None
    out_ref, grads_ref, basis_ref = refs[count + carried : count + carried + 3]
    sems = refs[-1]
    tokens = mine.shape[0]
    rows = sum(deep for _, deep in plan[0])

    groups = []
    used = 0
    at = 0
    for index, cuts in enumerate(plan):
        if index % 2 == 0:
            groups.append([])
        column = pl.multiple_of(places_ref[index] * rows, 128)
        for row, source in ((0, theirs), (tokens, mine)):
            groups[-1].append(
                pltpu.make_async_copy(
                    source.at[:, pl.ds(column, rows)],
                    grads_ref.at[pl.ds(row, tokens), pl.ds(index * rows, rows)],
                    sems.at[used],
                )
            )
            used += 1
        for offset, deep in cuts:
            groups[-1].append(
                pltpu.make_async_copy(
                    pieces[at].at[pl.ds(0, deep)],
                    basis_ref.at[pl.ds(index * rows + offset, deep)],
                    sems.at[used],
                )
            )
            used += 1
            at += 1
    for group in groups:
        for copy in group:
            copy.start()
    total = before[...] if carried else None
    for index, group in enumerate(groups):
        for copy in group:
            copy.wait()
        first, last = 2 * index * rows, min(2 * index + 2, len(plan)) * rows
        product = jnp.dot(
            grads_ref[:, first:last], basis_ref[first:last, :], preferred_element_type=f32
        )
        total = product if total is None else total + product
    out_ref[...] = total.astype(out_ref.dtype)


def accumulate(places, mine, theirs, plan, pieces, carried, kind):
    tokens = mine.shape[0]
    rows = sum(deep for _, deep in plan[0])
    cols = pieces[0].shape[1]
    held = pl.BlockSpec(memory_space=pltpu.VMEM)
    anywhere = pl.BlockSpec(memory_space=pltpu.HBM)
    return pl.pallas_call(
        functools.partial(accumulate_kernel, plan=plan, carried=len(carried)),
        in_specs=[
            pl.BlockSpec(memory_space=pltpu.SMEM),
            *[anywhere] * (2 + len(pieces)),
            *[held for _ in carried],
        ],
        out_specs=held,
        out_shape=jax.ShapeDtypeStruct((2 * tokens, cols), kind),
        scratch_shapes=[
            pltpu.VMEM((2 * tokens, len(plan) * rows), bf16),
            pltpu.VMEM((len(plan) * rows, cols), bf16),
            pltpu.SemaphoreType.DMA((2 * len(plan) + len(pieces),)),
        ],
        compiler_params=pltpu.CompilerParams(vmem_limit_bytes=62 * 1024 * 1024),
        name="accumulate",
    )(places, mine, theirs, *pieces, *carried)


def per_device(
    doc_ids,
    doc_lengths,
    activations,
    out_grads,
    input_basis,
    output_basis,
    eigenvalues,
    query_left,
    query_right,
):
    tokens = activations.shape[0]
    rows, cols = output_basis.shape
    queries, rank, kin = query_left.shape
    n_y, n_zl = lax.axis_size("y"), lax.axis_size("zl")
    n_x = lax.axis_size("x")
    y, zl, core = lax.axis_index("y"), lax.axis_index("zl"), lax.axis_index("c")
    zh, x = lax.axis_index("zh"), lax.axis_index("x")
    chips = n_y * n_zl
    tile = 128

    def forth(v):
        return shifted(v, "y", 1)

    def back(v):
        return shifted(v, "y", -1)

    def across(v):
        return shifted(v, "zl", 1)

    def sibling(v):
        return shifted(v, "c", 1)

    def chip(dy, dz):
        return ((y + dy) % n_y) * n_zl + (zl + dz) % n_zl

    def places(*relative):
        return jnp.stack([2 * chip(dy, dz) + core for dy, dz in relative]).astype(jnp.int32)

    def x_shift(v, step):
        return shifted(v, "x", step)

    mine_left = lax.dynamic_index_in_dim(query_left, x, 0, keepdims=False)
    left_dp = lax.all_gather(mine_left, ("y", "zl", "c"), axis=0)

    grads_peer = sibling(out_grads)
    share = lax.dot_general(
        input_basis, activations, (((0,), (1,)), ((), ())), preferred_element_type=f32
    ).astype(bf16)
    share, output_basis, query_right = lax.optimization_barrier(
        (share, output_basis, query_right)
    )
    other = shifted(share, "zh", 1)

    block = jnp.concatenate([output_basis, query_right.reshape(queries * rank, cols)], axis=0)
    before, after = forth(block), back(block)
    block_z, other = lax.optimization_barrier((block, other))
    beside = across(block_z)

    pair = jnp.where(zh == 0, jnp.stack([share, other]), jnp.stack([other, share]))
    weights = token_weights(doc_ids, doc_lengths)
    weights_peer = sibling(weights)
    pair, grads_peer, weights_peer = lax.optimization_barrier((pair, grads_peer, weights_peer))
    pair_before, pair_after = x_shift(pair, 1), x_shift(pair, -1)
    left_dp, pair_before, pair_after = lax.optimization_barrier((left_dp, pair_before, pair_after))
    left_chips = lax.dynamic_index_in_dim(
        left_dp.reshape(chips, 2, rank, kin), core, 1, keepdims=False
    )
    pair_far_0 = x_shift(pair_before[:1], 1)
    pair_far_1 = x_shift(pair_after[1:], -1)
    n_zh = lax.axis_size("zh")
    tiles_at = jnp.stack(
        [h * n_x + (x + dx) % n_x for dx in (0, -1, 1) for h in range(n_zh)]
        + [h * n_x + (x + 2) % n_x for h in range(n_zh)]
    ).astype(jnp.int32)
    chips_at = jnp.stack(
        [
            chip(0, 0), chip(3, 0), chip(1, 0), chip(0, 1),
            chip(3, 1), chip(1, 1), chip(2, 0), chip(2, 1),
        ]
    ).astype(jnp.int32)
    core_at = core.reshape(1).astype(jnp.int32)
    places_a = places((0, 0), (3, 0), (1, 0), (0, 1))
    places_b = places((2, 0), (3, 1), (1, 1))
    places_c = places((2, 1))
    weights = weights.reshape(tokens, 1)
    weights_peer = weights_peer.reshape(tokens, 1)
    (
        before, after, beside, weights, weights_peer, left_chips, pair_far_0, pair_far_1, tiles_at,
        chips_at, core_at, places_a, places_b, places_c,
    ) = lax.optimization_barrier(
        (
            before, after, beside, weights, weights_peer, left_chips, pair_far_0, pair_far_1,
            tiles_at, chips_at, core_at, places_a, places_b, places_c,
        )
    )

    left = lax.all_gather(left_chips, "x", axis=0)
    far = forth(before)
    after_beside = back(beside)
    before_beside = across(before)
    one = ((0, rows),)
    sums = accumulate(
        places_a, out_grads, grads_peer, (one, one, one, one),
        (output_basis, before, after, beside), (), f32,
    )
    sums, pair, pair_before, pair_after, pair_far_0, pair_far_1 = lax.optimization_barrier(
        (sums, pair, pair_before, pair_after, pair_far_0, pair_far_1)
    )
    acts = jnp.concatenate([pair, pair_before, pair_after, pair_far_0, pair_far_1])
    far, after_beside, before_beside, sums, acts = lax.optimization_barrier(
        (far, after_beside, before_beside, sums, acts)
    )
    acts_peer = sibling(acts)

    part_a, part_b, part_c = cut_out(
        (before_beside, after_beside, far),
        ((0, 3 * tile), (3 * tile, 3 * tile), (6 * tile, far.shape[0] - 6 * tile)),
    )
    far_beside_a, far_beside_b, far_beside_c = forth(part_a), back(part_b), across(part_c)
    sums = accumulate(
        places_b, out_grads, grads_peer, (one, one, one),
        (far, before_beside, after_beside), (sums,), f32,
    )
    three = ((0, 3 * tile), (3 * tile, 3 * tile), (6 * tile, tile))
    mine = accumulate(
        places_c, out_grads, grads_peer, (three,),
        (far_beside_a, far_beside_b, far_beside_c), (sums,), bf16,
    )
    more = sibling(mine)

    rights = (
        block, before, after, beside, before_beside, after_beside, far, far_beside_c,
    )
    values, values_peer = scores_of(
        chips_at, tiles_at, core_at, mine, more,
        (weights, weights_peer), (acts, acts_peer),
        eigenvalues, left, rights, queries * 2 * chips,
    )
    values = values + sibling(values_peer)
    values = values + lax.ppermute(values, "x", [(i, i ^ 1) for i in range(n_x)])
    values = values + lax.ppermute(values, "x", [(i, n_x - 1 - i) for i in range(n_x)])
    return values + shifted(values, "zh", 1)


def solution(mesh):
    parts = Mesh(mesh.devices.reshape(4, 2, 2, 2, 4), ("y", "zl", "c", "zh", "x"))
    dp, mp = ("y", "zl", "c"), ("zh", "x")
    return jax.shard_map(
        per_device,
        mesh=parts,
        in_specs=(
            P(dp, None),
            P(dp),
            P(dp, None),
            P(dp, None),
            P(None, mp),
            P(dp, mp),
            P(None, mp),
            P(dp, None, None),
            P(dp, None, mp),
        ),
        out_specs=P(dp, None),
        check_vma=False,
    )
```

time: 308 us -> 194 us (0.63)
  waiting for transfers between devices: 170 us -> 62.1 us
  matrix products: 85.1 us -> 4.24 us
  Pallas kernels: 0 us -> 58.3 us
  starting transfers between devices: 7.9 us -> 32.3 us
  blocking collectives: 14 us -> 0 us
  local copies, waits for them, and re-layouts: 10.4 us -> 16 us
    all_gather x3 -> x2, waiting for transfers between devices: 167 us -> 14.4 us  [the longest x1 14.4 us: per_device(): left_dp = lax.all_gather(mine_left, ('y', 'zl', 'c'), axis=0)]
    dot_general x18 -> x1, matrix products: 85.1 us -> 4.24 us  [per_device(): lax.dot_general(input_basis, activations, (((0,), (1,)), ((), ())), prefe...]
    pallas_call x0 -> x5, Pallas kernels: none -> 58.3 us  [the longest x3 36.3 us: accumulate(): pl.pallas_call(functools.partial(accumulate_kernel, plan=plan, carried=le...]
    ppermute x0 -> x22, waiting for transfers between devices: none -> 47.6 us  [the longest x20 43.7 us: shifted(): lax.ppermute(value, axis, [(i, (i + step) % size) for i in range(size)])]
    ppermute x0 -> x22, starting transfers between devices: none -> 32.3 us  [the longest x20 27.9 us: shifted(): lax.ppermute(value, axis, [(i, (i + step) % size) for i in range(size)])]
    all_to_all x1 -> x0, blocking collectives: 14 us -> none  [from_everyone(): lax.all_to_all(jnp.broadcast_to(array[None], (length, *array.shape)), axi...]
    convert_element_type x2 -> x0, local copies, waits for them, and re-layouts: 8.83 us -> none  [the longest x1 8.68 us: per_device(): right_part.reshape(number * rank_rows, right_part.shape[2])]
    all_to_all x1 -> x0, starting transfers between devices: 7.83 us -> none  [from_everyone(): lax.all_to_all(jnp.broadcast_to(array[None], (length, *array.shape)), axi...]
  transfers between devices with their start and end apart: 4 -> 24, of which waited for: 2 -> 14; matrix products, arithmetic and copies ran while one was open for 25% -> 11% of each run, Pallas kernels for 0% -> 20%
where the time goes in v2:
time: 194 us; the launch traced here: 193 us
  waiting for transfers between devices  62.1 us (32%)
  Pallas kernels  58.3 us (30%)
  starting transfers between devices  32.3 us (17%)
  local copies, waits for them, and re-layouts  16 us (8%)
  between operations  14.3 us (7%)
  other arithmetic  5.97 us (3%)
  matrix products  4.24 us (2%)
    ppermute x20, waiting for transfers between devices, shifted(): lax.ppermute(value, axis, [(i, (i + step) % size) for i in range(size)])  43.7 us
    pallas_call x3, Pallas kernels, accumulate(): pl.pallas_call(functools.partial(accumulate_kernel, plan=plan, carried=le...  36.3 us
    ppermute x20, starting transfers between devices, shifted(): lax.ppermute(value, axis, [(i, (i + step) % size) for i in range(size)])  27.9 us
    pallas_call x1, Pallas kernels, scores_of(): pl.pallas_call(score_kernel, in_specs=[*[scalars] * 3, *[anywhere] * 2, *...  19.3 us
    all_gather x1, waiting for transfers between devices, per_device(): left_dp = lax.all_gather(mine_left, ('y', 'zl', 'c'), axis=0)  14.4 us
    unnamed x36, local copies, waits for them, and re-layouts  6.98 us
    dot_general x1, matrix products, per_device(): lax.dot_general(input_basis, activations, (((0,), (1,)), ((), ())), prefe...  4.24 us
  transfers between devices with their start and end apart: 24, of which 14 were waited for; matrix products, arithmetic and copies ran while one was open for 11% of the time, Pallas kernels for 20%

profile of v2, /device:TPU:0, one launch (start us, length us, event | category | flops | bytes accessed | tf_op | source)
XLA Modules:
  0.0 193.3 jit_solution(4707323143782216036)
XLA Ops:
  8.3 4.2 %convolution_convert_fusion = bf16[256,512]{1,0:T(8,128)(2,1)S(1)} fusion(bf16[4096,256]{1,0:T(8,128)(2,1)} %param.13, bf16[512,4096]{1,0:T(8,128)(2,1)} %param.11), kind=kOutput, calls=%fused_computation.1 | convolution fusion | flops 1073872896 | bytes 6553600 | tf_op jit(solution)/shard_map/dot_general | solution.py:322
  12.6 4.0 %collective-permute-start.2 = (bf16[256,512]{1,0:T(8,128)(2,1)S(1)}, bf16[256,512]{1,0:T(8,128)(2,1)S(1)}, u32[]{:S(2)}, u32[]{:S(2)}) collective-permute-start(bf16[256,512]{1,0:T(8,128)(2,1)S(1)} %convolution_convert_fusion), channel_id=1, source_target_pairs={{0,4},{4,0},{1,5},{5,1},{2,6},{6,2},{3,7},{7,3},{8,12},{12,8},{9,1... | collective-permute-start | bytes 786440 | tf_op jit(solution)/shard_map/ppermute | solution.py:17
  20.1 3.5 %collective-permute-done.2 = bf16[256,512]{1,0:T(8,128)(2,1)S(1)} collective-permute-done((bf16[256,512]{1,0:T(8,128)(2,1)S(1)}, bf16[256,512]{1,0:T(8,128)(2,1)S(1)}, u32[]{:S(2)}, u32[]{:S(2)}) %collective-permute-start.2) | collective-permute-done | bytes 262176 | tf_op jit(solution)/shard_map/ppermute | solution.py:17
  33.8 1.7 fusion.own_weight_ref
  35.5 14.4 %all-gather.4.cloned.1.call-done = bf16[16,32,2048]{2,1,0:T(8,128)(2,1)} async-done(((bf16[1,32,2048]{2,1,0:T(8,128)(2,1)}), bf16[16,32,2048]{2,1,0:T(8,128)(2,1)}) %all-gather.4.cloned.1.call-update) | async-done | bytes 2097168 | tf_op jit(solution)/shard_map/all_gather | solution.py:319
  52.9 1.8 collective-permute-start.9
  56.5 2.3 %dynamic-slice_bitcast_fusion = bf16[8,32,2048]{2,1,0:T(8,128)(2,1)} fusion(bf16[8,2,32,2048]{3,2,1,0:T(8,128)(2,1)} %bitcast.43, s32[]{:T(128)S(6)} %select_n.145), kind=kLoop, calls=%fused_computation.2 | loop fusion | bytes 2097156 | tf_op jit(solution)/shard_map/jit(dynamic_index_in_dim)/squeeze | solution.py:341
  58.8 8.4 %collective-permute-done.refs_1_ = bf16[1024,896]{1,0:T(8,128)(2,1)} collective-permute-done((bf16[1024,896]{1,0:T(8,128)(2,1)S(1)}, bf16[1024,896]{1,0:T(8,128)(2,1)}, u32[]{:S(2)}, u32[]{:S(2)}) %collective-permute-start) | collective-permute-done | bytes 1835040 | tf_op jit(solution)/shard_map/ppermute | solution.py:17
  67.3 2.3 %collective-permute-done.1.refs_2_ = bf16[1024,896]{1,0:T(8,128)(2,1)} collective-permute-done((bf16[1024,896]{1,0:T(8,128)(2,1)S(1)}, bf16[1024,896]{1,0:T(8,128)(2,1)}, u32[]{:S(2)}, u32[]{:S(2)}) %collective-permute-start.1) | collective-permute-done | bytes 1835040 | tf_op jit(solution)/shard_map/ppermute | solution.py:17
  69.6 3.8 %collective-permute-done.3.refs_3_ = bf16[1024,896]{1,0:T(8,128)(2,1)} collective-permute-done((bf16[1024,896]{1,0:T(8,128)(2,1)S(1)}, bf16[1024,896]{1,0:T(8,128)(2,1)}, u32[]{:S(2)}, u32[]{:S(2)}) %collective-permute-start.3) | collective-permute-done | bytes 1835040 | tf_op jit(solution)/shard_map/ppermute | solution.py:17
  73.5 3.2 %collective-permute-start.11 = (bf16[1024,896]{1,0:T(8,128)(2,1)}, bf16[1024,896]{1,0:T(8,128)(2,1)}, u32[]{:S(2)}, u32[]{:S(2)}) collective-permute-start(bf16[1024,896]{1,0:T(8,128)(2,1)} %collective-permute-done.3.refs_3_), channel_id=1, source_target_pairs={{0,96},{32,0},{64,32},{96,64},{1,97},{33,1},{65,33},{97,65},{2,98}... | collective-permute-start | bytes 5505032 | tf_op jit(solution)/shard_map/ppermute | solution.py:17
  77.8 15.4 %accumulate.3.refs_3_ = f32[1024,896]{1,0:T(8,128)} custom-call(s32[4]{0:T(128)} %pad_add_fusion.places_ref, bf16[512,14336]{1,0:T(8,128)(2,1)} %mine.5, bf16[512,14336]{1,0:T(8,128)(2,1)} %collective-permute-done.4.theirs, bf16[896,896]{1,0:T(8,128)(2,1)} %refs_0_, bf16[1024,896]{1,0:T(8,128)(2,1)} %collective-permute-done.refs_1_, ...), custom_call_target="tpu_custom_call" | custom-call | tf_op jit(solution)/shard_map/accumulate/pallas_call | solution.py:257
  99.1 16.4 %collective-permute-done.10.refs_2_.refs_0_.refs_6_ = bf16[1024,896]{1,0:T(8,128)(2,1)} collective-permute-done((bf16[1024,896]{1,0:T(8,128)(2,1)}, bf16[1024,896]{1,0:T(8,128)(2,1)}, u32[]{:S(2)}, u32[]{:S(2)}) %collective-permute-start.10) | collective-permute-done | bytes 1835040 | tf_op jit(solution)/shard_map/ppermute | solution.py:17
  117.1 2.8 %cut.1 = (bf16[384,896]{1,0:T(8,128)(2,1)}, bf16[384,896]{1,0:T(8,128)(2,1)}, bf16[256,896]{1,0:T(8,128)(2,1)}) custom-call(bf16[1024,896]{1,0:T(8,128)(2,1)} %collective-permute-done.12.refs_0_.refs_1_.refs_4_, bf16[1024,896]{1,0:T(8,128)(2,1)} %collective-permute-done.11.refs_1_.refs_2_.refs_5_, ...), custom_call_target="tpu_custom_call" | custom-call | tf_op jit(solution)/shard_map/cut/pallas_call | solution.py:188
  120.1 3.2 %collective-permute-start.14 = (bf16[384,896]{1,0:T(8,128)(2,1)}, bf16[384,896]{1,0:T(8,128)(2,1)}, u32[]{:S(2)}, u32[]{:S(2)}) collective-permute-start(bf16[384,896]{1,0:T(8,128)(2,1)} %get-tuple-element.77), channel_id=1, source_target_pairs={{0,96},{32,0},{64,32},{96,64},{1,97},{33,1},{65,33},{97,65},{2,98}... | collective-permute-start | bytes 2064392 | tf_op jit(solution)/shard_map/ppermute | solution.py:17
  124.6 13.4 %accumulate.4.refs_3_ = f32[1024,896]{1,0:T(8,128)} custom-call(s32[3]{0:T(128)} %pad_add_fusion.1.places_ref, bf16[512,14336]{1,0:T(8,128)(2,1)} %mine.5, bf16[512,14336]{1,0:T(8,128)(2,1)} %collective-permute-done.4.theirs, bf16[1024,896]{1,0:T(8,128)(2,1)} %collective-permute-done.10.refs_2_.refs_0_.refs_6_, ...), custom_call_target="tpu_custom_call" | custom-call | tf_op jit(solution)/shard_map/accumulate/pallas_call | solution.py:257
  139.1 7.5 %accumulate.5.mine = bf16[1024,896]{1,0:T(8,128)(2,1)} custom-call(s32[1]{0:T(128)} %bitcast.34.places_ref, bf16[512,14336]{1,0:T(8,128)(2,1)} %mine.5, bf16[512,14336]{1,0:T(8,128)(2,1)} %collective-permute-done.4.theirs, bf16[384,896]{1,0:T(8,128)(2,1)} %copy-done.11, bf16[384,896]{1,0:T(8,128)(2,1)} %collective-permute-done.14.refs_1_, ...), custom_call_target="tpu_custom_call" | custom-call | tf_op jit(solution)/shard_map/accumulate/pallas_call | solution.py:257
  148.2 2.9 %collective-permute-done.16.more = bf16[1024,896]{1,0:T(8,128)(2,1)} collective-permute-done((bf16[1024,896]{1,0:T(8,128)(2,1)}, bf16[1024,896]{1,0:T(8,128)(2,1)}, u32[]{:S(2)}, u32[]{:S(2)}) %collective-permute-start.16) | collective-permute-done | bytes 1835040 | tf_op jit(solution)/shard_map/ppermute | solution.py:17
  151.1 19.3 %scores.1 = (f32[1,64]{1,0:T(1,128)}, f32[1,64]{1,0:T(1,128)}) custom-call(s32[8]{0:T(128)} %stack.119.chips_ref, s32[8]{0:T(128)} %stack.110.tiles_ref, s32[1]{0:T(128)} %bitcast.26.core_ref, bf16[1024,896]{1,0:T(8,128)(2,1)} %accumulate.5.mine, bf16[1024,896]{1,0:T(8,128)(2,1)} %collective-permute-done.16.more, f32[512,1]{1,0:T(8,128)} %fusion.own_weight_ref, ...), custom_call_target="tpu_custom_call" | custom-call | tf_op jit(solution)/shard_map/scores/pallas_call | solution.py:149
  174.1 2.0 %collective-permute-done.19 = f32[1,64]{1,0:T(1,128)S(1)} collective-permute-done((f32[1,64]{1,0:T(1,128)S(1)}, f32[1,64]{1,0:T(1,128)S(1)}, u32[]{:S(2)}, u32[]{:S(2)}) %collective-permute-start.19) | collective-permute-done | bytes 288 | tf_op jit(solution)/shard_map/ppermute | solution.py:416
  176.1 2.8 %collective-permute-start.20 = (f32[1,64]{1,0:T(1,128)S(1)}, f32[1,64]{1,0:T(1,128)S(1)}, u32[]{:S(2)}, u32[]{:S(2)}) collective-permute-start(f32[1,64]{1,0:T(1,128)S(1)} %add.229), channel_id=1, source_target_pairs={{0,3},{1,2},{2,1},{3,0},{4,7},{5,6},{6,5},{7,4},{8,11},{9,10},{10,... | collective-permute-start | bytes 776 | tf_op jit(solution)/shard_map/ppermute | solution.py:417
  178.9 1.9 collective-permute-done.20
  180.9 2.6 %collective-permute-start.21 = (f32[1,64]{1,0:T(1,128)S(1)}, f32[1,64]{1,0:T(1,128)S(1)}, u32[]{:S(2)}, u32[]{:S(2)}) collective-permute-start(f32[1,64]{1,0:T(1,128)S(1)} %add.230), channel_id=1, source_target_pairs={{0,4},{4,0},{1,5},{5,1},{2,6},{6,2},{3,7},{7,3},{8,12},{12,8},{9,1... | collective-permute-start | bytes 776 | tf_op jit(solution)/shard_map/ppermute | solution.py:17
  183.4 2.5 %collective-permute-done.21 = f32[1,64]{1,0:T(1,128)S(1)} collective-permute-done((f32[1,64]{1,0:T(1,128)S(1)}, f32[1,64]{1,0:T(1,128)S(1)}, u32[]{:S(2)}, u32[]{:S(2)}) %collective-permute-start.21) | collective-permute-done | bytes 288 | tf_op jit(solution)/shard_map/ppermute | solution.py:17
  (90 shorter events, 36.5 us)
Async XLA Ops:
  6.5 43.4 %all-gather.4.cloned.1.call-start = ((), (), s32[]{:S(2)}) async-start(), calls=%async_computation | async-start | bytes 2228224 | tf_op jit(solution)/shard_map/all_gather | solution.py:319
  6.5 22.5 %collective-permute-start.4 = (bf16[512,14336]{1,0:T(8,128)(2,1)}, bf16[512,14336]{1,0:T(8,128)(2,1)}, u32[]{:S(2)}, u32[]{:S(2)}) collective-permute-start(bf16[512,14336]{1,0:T(8,128)(2,1)} %mine.5), channel_id=1, source_target_pairs={{0,8},{8,0},{1,9},{9,1},{2,10},{10,2},{3,11},{11,3},{4,12},{12,4},... | collective-permute-start | bytes 44040200 | tf_op jit(solution)/shard_map/ppermute | solution.py:17
  8.3 142.8 %all-gather.6.cloned.1.call-start = ((), (), s32[]{:S(2)}) async-start(), calls=%async_computation.1 | async-start | bytes 5242880 | tf_op jit(solution)/shard_map/all_gather | solution.py:373
  12.6 11.0 %collective-permute-start.2 = (bf16[256,512]{1,0:T(8,128)(2,1)S(1)}, bf16[256,512]{1,0:T(8,128)(2,1)S(1)}, u32[]{:S(2)}, u32[]{:S(2)}) collective-permute-start(bf16[256,512]{1,0:T(8,128)(2,1)S(1)} %convolution_convert_fusion), channel_id=1, source_target_pairs={{0,4},{4,0},{1,5},{5,1},{2,6},{6,2},{3,7},{7,3},{8,12},{12,8},{9,1... | collective-permute-start | bytes 786440 | tf_op jit(solution)/shard_map/ppermute | solution.py:17
  16.8 50.5 %collective-permute-start = (bf16[1024,896]{1,0:T(8,128)(2,1)S(1)}, bf16[1024,896]{1,0:T(8,128)(2,1)}, u32[]{:S(2)}, u32[]{:S(2)}) collective-permute-start(bf16[1024,896]{1,0:T(8,128)(2,1)S(1)} %pad_maximum_fusion.refs_0_), channel_id=1, source_target_pairs={{0,32},{32,64},{64,96},{96,0},{1,33},{33,65},{65,97},{97,1},{2,34}... | collective-permute-start | bytes 5505032 | tf_op jit(solution)/shard_map/ppermute | solution.py:17
  18.4 51.1 %collective-permute-start.1 = (bf16[1024,896]{1,0:T(8,128)(2,1)S(1)}, bf16[1024,896]{1,0:T(8,128)(2,1)}, u32[]{:S(2)}, u32[]{:S(2)}) collective-permute-start(bf16[1024,896]{1,0:T(8,128)(2,1)S(1)} %pad_maximum_fusion.refs_0_), channel_id=1, source_target_pairs={{0,96},{32,0},{64,32},{96,64},{1,97},{33,1},{65,33},{97,65},{2,98}... | collective-permute-start | bytes 5505032 | tf_op jit(solution)/shard_map/ppermute | solution.py:17
  24.3 49.1 %collective-permute-start.3 = (bf16[1024,896]{1,0:T(8,128)(2,1)S(1)}, bf16[1024,896]{1,0:T(8,128)(2,1)}, u32[]{:S(2)}, u32[]{:S(2)}) collective-permute-start(bf16[1024,896]{1,0:T(8,128)(2,1)S(1)} %pad_maximum_fusion.refs_0_), channel_id=1, source_target_pairs={{0,16},{16,0},{1,17},{17,1},{2,18},{18,2},{3,19},{19,3},{4,20},{20... | collective-permute-start | bytes 5505032 | tf_op jit(solution)/shard_map/ppermute | solution.py:17
  26.3 2.4 %collective-permute-start.5 = (f32[1,512]{1,0:T(1,128)S(1)}, f32[1,512]{1,0:T(1,128)S(1)}, u32[]{:S(2)}, u32[]{:S(2)}) collective-permute-start(f32[1,512]{1,0:T(1,128)S(1)} %compare_select_fusion), channel_id=1, source_target_pairs={{0,8},{8,0},{1,9},{9,1},{2,10},{10,2},{3,11},{11,3},{4,12},{12,4},... | collective-permute-start | bytes 6152 | tf_op jit(solution)/shard_map/ppermute | solution.py:17
  29.0 20.9 %collective-permute-start.6 = (bf16[2,256,512]{2,1,0:T(8,128)(2,1)S(1)}, bf16[2,256,512]{2,1,0:T(8,128)(2,1)S(1)}, u32[]{:S(2)}, u32[]{:S(2)}) collective-permute-start(bf16[2,256,512]{2,1,0:T(8,128)(2,1)S(1)} %maximum_select_fusion), channel_id=1, source_target_pairs={{0,1},{1,2},{2,3},{3,0},{4,5},{5,6},{6,7},{7,4},{8,9},{9,10},{10,1... | collective-permute-start | bytes 1572872 | tf_op jit(solution)/shard_map/ppermute | solution.py:17
  30.6 19.3 %collective-permute-start.7 = (bf16[2,256,512]{2,1,0:T(8,128)(2,1)S(1)}, bf16[2,256,512]{2,1,0:T(8,128)(2,1)S(1)}, u32[]{:S(2)}, u32[]{:S(2)}) collective-permute-start(bf16[2,256,512]{2,1,0:T(8,128)(2,1)S(1)} %maximum_select_fusion), channel_id=1, source_target_pairs={{0,3},{1,0},{2,1},{3,2},{4,7},{5,4},{6,5},{7,6},{8,11},{9,8},{10,9... | collective-permute-start | bytes 1572872 | tf_op jit(solution)/shard_map/ppermute | solution.py:17
  50.7 22.7 %collective-permute-start.8 = (bf16[1,256,512]{2,1,0:T(8,128)(2,1)}, bf16[1,256,512]{2,1,0:T(8,128)(2,1)}, u32[]{:S(2)}, u32[]{:S(2)}) collective-permute-start(bf16[1,256,512]{2,1,0:T(8,128)(2,1)} %slice.6), channel_id=1, source_target_pairs={{0,1},{1,2},{2,3},{3,0},{4,5},{5,6},{6,7},{7,4},{8,9},{9,10},{10,1... | collective-permute-start | bytes 786440 | tf_op jit(solution)/shard_map/ppermute | solution.py:17
  52.9 20.5 %collective-permute-start.9 = (bf16[1,256,512]{2,1,0:T(8,128)(2,1)}, bf16[1,256,512]{2,1,0:T(8,128)(2,1)}, u32[]{:S(2)}, u32[]{:S(2)}) collective-permute-start(bf16[1,256,512]{2,1,0:T(8,128)(2,1)} %slice.7), channel_id=1, source_target_pairs={{0,3},{1,0},{2,1},{3,2},{4,7},{5,4},{6,5},{7,6},{8,11},{9,8},{10,9... | collective-permute-start | bytes 786440 | tf_op jit(solution)/shard_map/ppermute | solution.py:17
  73.4 42.2 %collective-permute-start.10 = (bf16[1024,896]{1,0:T(8,128)(2,1)}, bf16[1024,896]{1,0:T(8,128)(2,1)}, u32[]{:S(2)}, u32[]{:S(2)}) collective-permute-start(bf16[1024,896]{1,0:T(8,128)(2,1)} %collective-permute-done.refs_1_), channel_id=1, source_target_pairs={{0,32},{32,64},{64,96},{96,0},{1,33},{33,65},{65,97},{97,1},{2,34}... | collective-permute-start | bytes 5505032 | tf_op jit(solution)/shard_map/ppermute | solution.py:17
  73.5 42.1 %collective-permute-start.11 = (bf16[1024,896]{1,0:T(8,128)(2,1)}, bf16[1024,896]{1,0:T(8,128)(2,1)}, u32[]{:S(2)}, u32[]{:S(2)}) collective-permute-start(bf16[1024,896]{1,0:T(8,128)(2,1)} %collective-permute-done.3.refs_3_), channel_id=1, source_target_pairs={{0,96},{32,0},{64,32},{96,64},{1,97},{33,1},{65,33},{97,65},{2,98}... | collective-permute-start | bytes 5505032 | tf_op jit(solution)/shard_map/ppermute | solution.py:17
  76.7 40.3 %collective-permute-start.12 = (bf16[1024,896]{1,0:T(8,128)(2,1)}, bf16[1024,896]{1,0:T(8,128)(2,1)}, u32[]{:S(2)}, u32[]{:S(2)}) collective-permute-start(bf16[1024,896]{1,0:T(8,128)(2,1)} %collective-permute-done.refs_1_), channel_id=1, source_target_pairs={{0,16},{16,0},{1,17},{17,1},{2,18},{18,2},{3,19},{19,3},{4,20},{20... | collective-permute-start | bytes 5505032 | tf_op jit(solution)/shard_map/ppermute | solution.py:17
  119.8 18.2 %collective-permute-start.13 = (bf16[384,896]{1,0:T(8,128)(2,1)}, bf16[384,896]{1,0:T(8,128)(2,1)S(1)}, u32[]{:S(2)}, u32[]{:S(2)}) collective-permute-start(bf16[384,896]{1,0:T(8,128)(2,1)} %get-tuple-element.76), channel_id=1, source_target_pairs={{0,32},{32,64},{64,96},{96,0},{1,33},{33,65},{65,97},{97,1},{2,34}... | collective-permute-start | bytes 2064392 | tf_op jit(solution)/shard_map/ppermute | solution.py:17
  120.1 18.0 %collective-permute-start.14 = (bf16[384,896]{1,0:T(8,128)(2,1)}, bf16[384,896]{1,0:T(8,128)(2,1)}, u32[]{:S(2)}, u32[]{:S(2)}) collective-permute-start(bf16[384,896]{1,0:T(8,128)(2,1)} %get-tuple-element.77), channel_id=1, source_target_pairs={{0,96},{32,0},{64,32},{96,64},{1,97},{33,1},{65,33},{97,65},{2,98}... | collective-permute-start | bytes 2064392 | tf_op jit(solution)/shard_map/ppermute | solution.py:17
  123.3 14.7 %collective-permute-start.15 = (bf16[256,896]{1,0:T(8,128)(2,1)}, bf16[256,896]{1,0:T(8,128)(2,1)S(1)}, u32[]{:S(2)}, u32[]{:S(2)}) collective-permute-start(bf16[256,896]{1,0:T(8,128)(2,1)} %get-tuple-element.78), channel_id=1, source_target_pairs={{0,16},{16,0},{1,17},{17,1},{2,18},{18,2},{3,19},{19,3},{4,20},{20... | collective-permute-start | bytes 1376264 | tf_op jit(solution)/shard_map/ppermute | solution.py:17
  124.6 23.6 %collective-permute-start.17 = (bf16[8,256,512]{2,1,0:T(8,128)(2,1)}, bf16[8,256,512]{2,1,0:T(8,128)(2,1)}, u32[]{:S(2)}, u32[]{:S(2)}) collective-permute-start(bf16[8,256,512]{2,1,0:T(8,128)(2,1)} %constant_dynamic-update-slice_fusion.own_acts), channel_id=1, source_target_pairs={{0,8},{8,0},{1,9},{9,1},{2,10},{10,2},{3,11},{11,3},{4,12},{12,4},... | collective-permute-start | bytes 6291464 | tf_op jit(solution)/shard_map/ppermute | solution.py:17
  146.5 4.6 %collective-permute-start.16 = (bf16[1024,896]{1,0:T(8,128)(2,1)}, bf16[1024,896]{1,0:T(8,128)(2,1)}, u32[]{:S(2)}, u32[]{:S(2)}) collective-permute-start(bf16[1024,896]{1,0:T(8,128)(2,1)} %accumulate.5.mine), channel_id=1, source_target_pairs={{0,8},{8,0},{1,9},{9,1},{2,10},{10,2},{3,11},{11,3},{4,12},{12,4},... | collective-permute-start | bytes 5505032 | tf_op jit(solution)/shard_map/ppermute | solution.py:17
  170.4 1.5 collective-permute-start.18
  172.6 3.5 %collective-permute-start.19 = (f32[1,64]{1,0:T(1,128)S(1)}, f32[1,64]{1,0:T(1,128)S(1)}, u32[]{:S(2)}, u32[]{:S(2)}) collective-permute-start(f32[1,64]{1,0:T(1,128)S(1)} %add.228), channel_id=1, source_target_pairs={{0,1},{1,0},{2,3},{3,2},{4,5},{5,4},{6,7},{7,6},{8,9},{9,8},{10,11... | collective-permute-start | bytes 776 | tf_op jit(solution)/shard_map/ppermute | solution.py:416
  176.1 4.8 %collective-permute-start.20 = (f32[1,64]{1,0:T(1,128)S(1)}, f32[1,64]{1,0:T(1,128)S(1)}, u32[]{:S(2)}, u32[]{:S(2)}) collective-permute-start(f32[1,64]{1,0:T(1,128)S(1)} %add.229), channel_id=1, source_target_pairs={{0,3},{1,2},{2,1},{3,0},{4,7},{5,6},{6,5},{7,4},{8,11},{9,10},{10,... | collective-permute-start | bytes 776 | tf_op jit(solution)/shard_map/ppermute | solution.py:417
  180.9 5.0 %collective-permute-start.21 = (f32[1,64]{1,0:T(1,128)S(1)}, f32[1,64]{1,0:T(1,128)S(1)}, u32[]{:S(2)}, u32[]{:S(2)}) collective-permute-start(f32[1,64]{1,0:T(1,128)S(1)} %add.230), channel_id=1, source_target_pairs={{0,4},{4,0},{1,5},{5,1},{2,6},{6,2},{3,7},{7,3},{8,12},{12,8},{9,1... | collective-permute-start | bytes 776 | tf_op jit(solution)/shard_map/ppermute | solution.py:17
  (16 other events, 238.7 us)
Sparse Core Ops, SparseCore 0:
  9.1 40.8 all-gather.3
  73.5 49.4 all-gather.5

commit v3 on v2

--- a/solution.py
+++ b/solution.py
@@ -26,15 +26,15 @@
 
 
 def score_kernel(
-    chips_ref, tiles_ref, core_ref, mine, more, own_weight_ref, peer_weight_ref, own_acts,
-    peer_acts, eig, left, *refs,
+    chips_ref, tiles_ref, core_ref, mine, more, own_weight, peer_weight, own_acts,
+    peer_acts, eig, left, *refs, right_rows, count,
 ):
-    rights = refs[:8]
-    own_out, peer_out = refs[8:10]
+    rights = refs[:count]
+    own_out, peer_out = refs[count : count + 2]
     (
         mine_ref, more_ref, acts_ref, eig_ref, left_ref, right_ref, scaled_ref, cond_ref, sums_ref,
-        sems, tile_sems,
-    ) = refs[10:]
+        sems, tile_sems, weights_ref,
+    ) = refs[count + 2 :]
     tiles, rows_in, tokens = own_acts.shape
     n_x, chips, rank, kin = left.shape
     cols = eig.shape[1]
@@ -59,17 +59,19 @@
     right_copies = [
         [
             pltpu.make_async_copy(
-                piece.at[pl.ds(piece.shape[0] - tile + q * rank, rank), :],
+                rights[piece].at[pl.ds(row + q * rank, rank), :],
                 right_ref.at[q, chips_ref[index]],
                 sems.at[4 + index * n_x + q],
             )
             for q in range(n_x)
         ]
-        for index, piece in enumerate(rights)
+        for index, (piece, row) in enumerate(right_rows)
     ]
     sum_copies = [
-        pltpu.make_async_copy(mine, mine_ref, sems.at[4 + len(rights) * n_x]),
-        pltpu.make_async_copy(more, more_ref, sems.at[5 + len(rights) * n_x]),
+        pltpu.make_async_copy(mine, mine_ref, sems.at[4 + len(right_rows) * n_x]),
+        pltpu.make_async_copy(more, more_ref, sems.at[5 + len(right_rows) * n_x]),
+        pltpu.make_async_copy(own_weight, weights_ref.at[0], sems.at[0]),
+        pltpu.make_async_copy(peer_weight, weights_ref.at[1], sems.at[1]),
     ]
     for copy in sum_copies:
         copy.start()
@@ -83,13 +85,11 @@
 
     for copy in sum_copies:
         copy.wait()
-    for index, (weight, mine_at, more_at) in enumerate(
-        ((own_weight_ref, tokens, 0), (peer_weight_ref, 0, tokens))
-    ):
+    for index, (mine_at, more_at) in enumerate(((tokens, 0), (0, tokens))):
         total = mine_ref[mine_at : mine_at + tokens, :].astype(f32)
         total = total + more_ref[more_at : more_at + tokens, :].astype(f32)
         rotated = total.astype(bf16).astype(f32)
-        scaled_ref[index] = (weight[...] * rotated).astype(bf16)
+        scaled_ref[index] = (weights_ref[index] * rotated).astype(bf16)
 
     for first in range(0, tiles, 2):
         pair = (first, first + 1)
@@ -139,7 +139,9 @@
         out[...] = jnp.sum(jnp.where(place == target, values, 0.0), axis=0, keepdims=True)
 
 
-def scores_of(chips_at, tiles_at, core, mine, more, weights, acts, eig, left, rights, number):
+def scores_of(
+    chips_at, tiles_at, core, mine, more, weights, acts, eig, left, rights, right_rows, number
+):
     tokens = acts[0].shape[2]
     kin, cols = eig.shape
     n_x, chips, rank, _ = left.shape
@@ -147,8 +149,8 @@
     held = pl.BlockSpec(memory_space=pltpu.VMEM)
     anywhere = pl.BlockSpec(memory_space=pltpu.HBM)
     return pl.pallas_call(
-        score_kernel,
-        in_specs=[*[scalars] * 3, *[anywhere] * 2, *[held] * 2, *[anywhere] * 12],
+        functools.partial(score_kernel, right_rows=right_rows, count=len(rights)),
+        in_specs=[*[scalars] * 3, *[anywhere] * (8 + len(rights))],
         out_specs=[held, held],
         scratch_shapes=[
             pltpu.VMEM(mine.shape, bf16),
@@ -162,6 +164,7 @@
             pltpu.VMEM((2, n_x * chips, 128), f32),
             pltpu.SemaphoreType.DMA((6 + 8 * n_x,)),
             pltpu.SemaphoreType.DMA((3, acts[0].shape[0])),
+            pltpu.VMEM((2, tokens, 1), f32),
         ],
         out_shape=[jax.ShapeDtypeStruct((1, number), f32)] * 2,
         compiler_params=pltpu.CompilerParams(vmem_limit_bytes=62 * 1024 * 1024),
@@ -169,14 +172,13 @@
     )(chips_at, tiles_at, core, mine, more, *weights, *acts, eig, left, *rights)
 
 
-def cut_kernel(*refs, cuts):
-    count = len(cuts)
-    sems = refs[-1]
+def cut_kernel(*refs, cuts, count):
+    sources, outs, sems = refs[:count], refs[count:-1], refs[-1]
     copies = [
         pltpu.make_async_copy(
-            refs[at].at[pl.ds(start, size)], refs[count + at], sems.at[at]
+            sources[source].at[pl.ds(start, size)], outs[out].at[pl.ds(to, size)], sems.at[at]
         )
-        for at, (start, size) in enumerate(cuts)
+        for at, (source, start, size, out, to) in enumerate(cuts)
     ]
     for copy in copies:
         copy.start()
@@ -185,88 +187,101 @@
 
 
 def cut_out(arrays, cuts):
+    cols = arrays[0].shape[1]
+    lengths = {}
+    for _, _, size, out, to in cuts:
+        lengths[out] = max(lengths.get(out, 0), to + size)
     return pl.pallas_call(
-        functools.partial(cut_kernel, cuts=cuts),
+        functools.partial(cut_kernel, cuts=cuts, count=len(arrays)),
         in_specs=[pl.BlockSpec(memory_space=pltpu.HBM)] * len(arrays),
-        out_specs=[pl.BlockSpec(memory_space=pltpu.VMEM)] * len(arrays),
+        out_specs=[pl.BlockSpec(memory_space=pltpu.VMEM)] * len(lengths),
         out_shape=[
-            jax.ShapeDtypeStruct((size, array.shape[1]), array.dtype)
-            for array, (_, size) in zip(arrays, cuts)
+            jax.ShapeDtypeStruct((lengths[out], cols), arrays[0].dtype)
+            for out in range(len(lengths))
         ],
-        scratch_shapes=[pltpu.SemaphoreType.DMA((len(arrays),))],
+        scratch_shapes=[pltpu.SemaphoreType.DMA((len(cuts),))],
         name="cut",
     )(*arrays)
 
 
-def accumulate_kernel(places_ref, mine, theirs, *refs, plan, carried):
-    count = sum(len(cuts) for cuts in plan)
+def accumulate_kernel(places_ref, mine, theirs, *refs, plan, count, carried):
     pieces = refs[:count]
-    before = refs[count] if carried else None
-    out_ref, grads_ref, basis_ref = refs[count + carried : count + carried + 3]
-    sems = refs[-1]
+    out_ref, grads_ref, basis_ref, sems = refs[count + carried : count + carried + 4]
     tokens = mine.shape[0]
-    rows = sum(deep for _, deep in plan[0])
+    rows = sum(deep for _, deep, _, _ in plan[0])
+    bounds = list(range(len(plan), 0, -2))[::-1]
+    starts = [0] + bounds[:-1]
 
     groups = []
     used = 0
-    at = 0
-    for index, cuts in enumerate(plan):
-        if index % 2 == 0:
-            groups.append([])
-        column = pl.multiple_of(places_ref[index] * rows, 128)
-        for row, source in ((0, theirs), (tokens, mine)):
-            groups[-1].append(
-                pltpu.make_async_copy(
-                    source.at[:, pl.ds(column, rows)],
-                    grads_ref.at[pl.ds(row, tokens), pl.ds(index * rows, rows)],
-                    sems.at[used],
+    for first, last in zip(starts, bounds):
+        group = []
+        for index in range(first, last):
+            column = pl.multiple_of(places_ref[index] * rows, 128)
+            for row, source in ((0, theirs), (tokens, mine)):
+                group.append(
+                    pltpu.make_async_copy(
+                        source.at[:, pl.ds(column, rows)],
+                        grads_ref.at[pl.ds(row, tokens), pl.ds(index * rows, rows)],
+                        sems.at[used],
+                    )
                 )
-            )
-            used += 1
-        for offset, deep in cuts:
-            groups[-1].append(
-                pltpu.make_async_copy(
-                    pieces[at].at[pl.ds(0, deep)],
-                    basis_ref.at[pl.ds(index * rows + offset, deep)],
-                    sems.at[used],
+                used += 1
+            for offset, deep, piece, piece_row in plan[index]:
+                group.append(
+                    pltpu.make_async_copy(
+                        pieces[piece].at[pl.ds(piece_row, deep)],
+                        basis_ref.at[pl.ds(index * rows + offset, deep)],
+                        sems.at[used],
+                    )
                 )
-            )
-            used += 1
-            at += 1
+                used += 1
+        groups.append(group)
     for group in groups:
         for copy in group:
             copy.start()
-    total = before[...] if carried else None
-    for index, group in enumerate(groups):
+    if carried:
+        before_ref = refs[-1]
+        carry = pltpu.make_async_copy(refs[count], before_ref, sems.at[used])
+        carry.start()
+    total = None
+    for first, last, group in zip(starts, bounds, groups):
         for copy in group:
             copy.wait()
-        first, last = 2 * index * rows, min(2 * index + 2, len(plan)) * rows
         product = jnp.dot(
-            grads_ref[:, first:last], basis_ref[first:last, :], preferred_element_type=f32
+            grads_ref[:, first * rows : last * rows],
+            basis_ref[first * rows : last * rows, :],
+            preferred_element_type=f32,
         )
         total = product if total is None else total + product
+    if carried:
+        carry.wait()
+        total = total + before_ref[...]
     out_ref[...] = total.astype(out_ref.dtype)
 
 
 def accumulate(places, mine, theirs, plan, pieces, carried, kind):
     tokens = mine.shape[0]
-    rows = sum(deep for _, deep in plan[0])
+    rows = sum(deep for _, deep, _, _ in plan[0])
     cols = pieces[0].shape[1]
     held = pl.BlockSpec(memory_space=pltpu.VMEM)
     anywhere = pl.BlockSpec(memory_space=pltpu.HBM)
+    copies = sum(2 + len(cuts) for cuts in plan) + 1
     return pl.pallas_call(
-        functools.partial(accumulate_kernel, plan=plan, carried=len(carried)),
+        functools.partial(
+            accumulate_kernel, plan=plan, count=len(pieces), carried=len(carried)
+        ),
         in_specs=[
             pl.BlockSpec(memory_space=pltpu.SMEM),
-            *[anywhere] * (2 + len(pieces)),
-            *[held for _ in carried],
+            *[anywhere] * (2 + len(pieces) + len(carried)),
         ],
         out_specs=held,
         out_shape=jax.ShapeDtypeStruct((2 * tokens, cols), kind),
         scratch_shapes=[
             pltpu.VMEM((2 * tokens, len(plan) * rows), bf16),
             pltpu.VMEM((len(plan) * rows, cols), bf16),
-            pltpu.SemaphoreType.DMA((2 * len(plan) + len(pieces),)),
+            pltpu.SemaphoreType.DMA((copies,)),
+            *[pltpu.VMEM((2 * tokens, cols), f32) for _ in carried],
         ],
         compiler_params=pltpu.CompilerParams(vmem_limit_bytes=62 * 1024 * 1024),
         name="accumulate",
@@ -316,21 +331,28 @@
         return shifted(v, "x", step)
 
     mine_left = lax.dynamic_index_in_dim(query_left, x, 0, keepdims=False)
-    left_dp = lax.all_gather(mine_left, ("y", "zl", "c"), axis=0)
+    other_left = across(mine_left)
+    left_pair = jnp.where(
+        zl == 0, jnp.stack([mine_left, other_left]), jnp.stack([other_left, mine_left])
+    )
+    left_dp = lax.all_gather(left_pair, "y", axis=0)
 
     grads_peer = sibling(out_grads)
     share = lax.dot_general(
         input_basis, activations, (((0,), (1,)), ((), ())), preferred_element_type=f32
     ).astype(bf16)
-    share, output_basis, query_right = lax.optimization_barrier(
-        (share, output_basis, query_right)
-    )
     other = shifted(share, "zh", 1)
 
     block = jnp.concatenate([output_basis, query_right.reshape(queries * rank, cols)], axis=0)
     before, after = forth(block), back(block)
-    block_z, other = lax.optimization_barrier((block, other))
-    beside = across(block_z)
+    half, most = 4 * tile, 5 * tile
+    basis_z, right_z, other, left_pair = lax.optimization_barrier(
+        (output_basis, query_right, other, left_pair)
+    )
+    beside_head = across(basis_z[:most])
+    beside_end = across(
+        jnp.concatenate([basis_z[most:], right_z.reshape(queries * rank, cols)], axis=0)
+    )
 
     pair = jnp.where(zh == 0, jnp.stack([share, other]), jnp.stack([other, share]))
     weights = token_weights(doc_ids, doc_lengths)
@@ -338,9 +360,7 @@
     pair, grads_peer, weights_peer = lax.optimization_barrier((pair, grads_peer, weights_peer))
     pair_before, pair_after = x_shift(pair, 1), x_shift(pair, -1)
     left_dp, pair_before, pair_after = lax.optimization_barrier((left_dp, pair_before, pair_after))
-    left_chips = lax.dynamic_index_in_dim(
-        left_dp.reshape(chips, 2, rank, kin), core, 1, keepdims=False
-    )
+    left_chips = left_dp.reshape(chips, rank, kin)
     pair_far_0 = x_shift(pair_before[:1], 1)
     pair_far_1 = x_shift(pair_after[1:], -1)
     n_zh = lax.axis_size("zh")
@@ -356,61 +376,88 @@
     ).astype(jnp.int32)
     core_at = core.reshape(1).astype(jnp.int32)
     places_a = places((0, 0), (3, 0), (1, 0), (0, 1))
-    places_b = places((2, 0), (3, 1), (1, 1))
-    places_c = places((2, 1))
+    places_c = places((2, 0), (3, 1), (1, 1))
+    places_d = places((2, 1))
     weights = weights.reshape(tokens, 1)
     weights_peer = weights_peer.reshape(tokens, 1)
     (
-        before, after, beside, weights, weights_peer, left_chips, pair_far_0, pair_far_1, tiles_at,
-        chips_at, core_at, places_a, places_b, places_c,
+        before, after, beside_head, weights, weights_peer, left_chips, pair_far_0, pair_far_1,
+        tiles_at, chips_at, core_at, places_a, places_c, places_d,
     ) = lax.optimization_barrier(
         (
-            before, after, beside, weights, weights_peer, left_chips, pair_far_0, pair_far_1,
-            tiles_at, chips_at, core_at, places_a, places_b, places_c,
+            before, after, beside_head, weights, weights_peer, left_chips, pair_far_0,
+            pair_far_1, tiles_at, chips_at, core_at, places_a, places_c, places_d,
         )
     )
 
     left = lax.all_gather(left_chips, "x", axis=0)
-    far = forth(before)
-    after_beside = back(beside)
-    before_beside = across(before)
-    one = ((0, rows),)
+    length = before.shape[0]
+    end = length - most
+    before_head, after_tail, both_ends = cut_out(
+        (before, after),
+        (
+            (0, 0, half, 0, 0),
+            (1, half, length - half, 1, 0),
+            (0, most, end, 2, 0),
+            (1, most, end, 2, end),
+        ),
+    )
+    far_a, far_b = forth(before_head), back(after_tail)
+    beside_ends = across(both_ends)
+    before_beside_a, after_beside_a = forth(beside_head), back(beside_head)
+    acts = jnp.concatenate([pair, pair_before, pair_after, pair_far_0, pair_far_1])
+    before_beside_a, after_beside_a = forth(beside_head), back(beside_head)
+    acts = jnp.concatenate([pair, pair_before, pair_after, pair_far_0, pair_far_1])
     sums = accumulate(
-        places_a, out_grads, grads_peer, (one, one, one, one),
-        (output_basis, before, after, beside), (), f32,
-    )
-    sums, pair, pair_before, pair_after, pair_far_0, pair_far_1 = lax.optimization_barrier(
-        (sums, pair, pair_before, pair_after, pair_far_0, pair_far_1)
-    )
-    acts = jnp.concatenate([pair, pair_before, pair_after, pair_far_0, pair_far_1])
-    far, after_beside, before_beside, sums, acts = lax.optimization_barrier(
-        (far, after_beside, before_beside, sums, acts)
-    )
+        places_a, out_grads, grads_peer,
+        (
+            ((0, rows, 0, 0),),
+            ((0, rows, 1, 0),),
+            ((0, rows, 2, 0),),
+            ((0, most, 3, 0), (most, rows - most, 4, 0)),
+        ),
+        (output_basis, before, after, beside_head, beside_end), (), f32,
+    )
+    before_beside_a, after_beside_a, sums, acts = lax.optimization_barrier(
+        (before_beside_a, after_beside_a, sums, acts)
+    )
+
+    part_a, part_b, part_c = cut_out(
+        (before_beside_a, after_beside_a, far_b),
+        (
+            (0, 0, 3 * tile, 0, 0),
+            (1, 3 * tile, 2 * tile, 1, 0),
+            (2, most - half, end, 2, 0),
+        ),
+    )
+    far_beside_a, far_beside_b, far_beside_c = forth(part_a), back(part_b), across(part_c)
     acts_peer = sibling(acts)
-
-    part_a, part_b, part_c = cut_out(
-        (before_beside, after_beside, far),
-        ((0, 3 * tile), (3 * tile, 3 * tile), (6 * tile, far.shape[0] - 6 * tile)),
-    )
-    far_beside_a, far_beside_b, far_beside_c = forth(part_a), back(part_b), across(part_c)
     sums = accumulate(
-        places_b, out_grads, grads_peer, (one, one, one),
-        (far, before_beside, after_beside), (sums,), f32,
-    )
-    three = ((0, 3 * tile), (3 * tile, 3 * tile), (6 * tile, tile))
+        places_c, out_grads, grads_peer,
+        (
+            ((0, half, 0, 0), (half, rows - half, 1, 0)),
+            ((0, most, 2, 0), (most, rows - most, 4, 0)),
+            ((0, most, 3, 0), (most, rows - most, 4, end)),
+        ),
+        (far_a, far_b, before_beside_a, after_beside_a, beside_ends), (sums,), f32,
+    )
+
     mine = accumulate(
-        places_c, out_grads, grads_peer, (three,),
+        places_d, out_grads, grads_peer,
+        (((0, 3 * tile, 0, 0), (3 * tile, 2 * tile, 1, 0), (most, rows - most, 2, 0)),),
         (far_beside_a, far_beside_b, far_beside_c), (sums,), bf16,
     )
     more = sibling(mine)
 
-    rights = (
-        block, before, after, beside, before_beside, after_beside, far, far_beside_c,
+    rights = (block, before, after, beside_end, beside_ends, far_b, far_beside_c)
+    right_rows = (
+        (0, rows), (1, rows), (2, rows), (3, end - tile), (4, end - tile), (4, 2 * end - tile),
+        (5, far_b.shape[0] - tile), (6, end - tile),
     )
     values, values_peer = scores_of(
         chips_at, tiles_at, core_at, mine, more,
         (weights, weights_peer), (acts, acts_peer),
-        eigenvalues, left, rights, queries * 2 * chips,
+        eigenvalues, left, rights, right_rows, queries * 2 * chips,
     )
     values = values + sibling(values_peer)
     values = values + lax.ppermute(values, "x", [(i, i ^ 1) for i in range(n_x)])

time: 194 us -> 192 us (0.990)
  waiting for transfers between devices: 62.1 us -> 43.9 us
  local copies, waits for them, and re-layouts: 16 us -> 22.1 us
  other arithmetic: 5.97 us -> 11.1 us
  starting transfers between devices: 32.3 us -> 35.2 us
  Pallas kernels: 58.3 us -> 60.4 us
    ppermute x20 -> x24, waiting for transfers between devices: 43.7 us -> 30.1 us  [shifted(): lax.ppermute(value, axis, [(i, (i + step) % size) for i in range(size)])]
    unnamed x36 -> x20, local copies, waits for them, and re-layouts: 6.98 us -> 12 us
    all_gather x1, waiting for transfers between devices: 14.4 us -> 9.51 us  [per_device(): left_dp = lax.all_gather(left_pair, 'y', axis=0)]
    ppermute x20 -> x24, starting transfers between devices: 27.9 us -> 31.1 us  [shifted(): lax.ppermute(value, axis, [(i, (i + step) % size) for i in range(size)])]
    concatenate x1, other arithmetic: 0.15 us -> 2.95 us  [per_device(): jnp.concatenate([output_basis, query_right.reshape(queries * rank, cols)]...]
    squeeze x1 -> x0, local copies, waits for them, and re-layouts: 2.32 us -> none  [per_device(): lax.dynamic_index_in_dim(left_dp.reshape(chips, 2, rank, kin), core, 1, k...]
    pallas_call x5 -> x6, Pallas kernels: 58.3 us -> 60.4 us  [the longest x3 35.1 us: accumulate(): pl.pallas_call(functools.partial(accumulate_kernel, plan=plan, count=len(...]
  transfers between devices with their start and end apart: 24 -> 28, of which waited for: 14 -> 13; matrix products, arithmetic and copies ran while one was open for 11% -> 17% of each run, Pallas kernels for 20% -> 22%
where the time goes in v3:
time: 192 us; the launch traced here: 191 us
  Pallas kernels  60.4 us (31%)
  waiting for transfers between devices  43.9 us (23%)
  starting transfers between devices  35.2 us (18%)
  local copies, waits for them, and re-layouts  22.1 us (12%)
  between operations  14.3 us (7%)
  other arithmetic  11.1 us (6%)
  matrix products  4.23 us (2%)
    pallas_call x3, Pallas kernels, accumulate(): pl.pallas_call(functools.partial(accumulate_kernel, plan=plan, count=len(...  35.1 us
    ppermute x24, starting transfers between devices, shifted(): lax.ppermute(value, axis, [(i, (i + step) % size) for i in range(size)])  31.1 us
    ppermute x24, waiting for transfers between devices, shifted(): lax.ppermute(value, axis, [(i, (i + step) % size) for i in range(size)])  30.1 us
    pallas_call x1, Pallas kernels, scores_of(): pl.pallas_call(functools.partial(score_kernel, right_rows=right_rows, cou...  19 us
    unnamed x20, local copies, waits for them, and re-layouts  12 us
    all_gather x1, waiting for transfers between devices, per_device(): left_dp = lax.all_gather(left_pair, 'y', axis=0)  9.51 us
    pallas_call x2, Pallas kernels, cut_out(): pl.pallas_call(functools.partial(cut_kernel, cuts=cuts, count=len(arrays)...  6.28 us
    dot_general x1, matrix products, per_device(): lax.dot_general(input_basis, activations, (((0,), (1,)), ((), ())), prefe...  4.23 us
  transfers between devices with their start and end apart: 28, of which 13 were waited for; matrix products, arithmetic and copies ran while one was open for 17% of the time, Pallas kernels for 22%

profile of v3, /device:TPU:0, one launch (start us, length us, event | category | flops | bytes accessed | tf_op | source)
XLA Modules:
  0.0 191.2 jit_solution(4891168788238806747)
XLA Ops:
  7.5 2.1 %collective-permute-start.6 = (bf16[32,2048]{1,0:T(8,128)(2,1)S(1)}, bf16[32,2048]{1,0:T(8,128)(2,1)S(1)}, u32[]{:S(2)}, u32[]{:S(2)}) collective-permute-start(bf16[32,2048]{1,0:T(8,128)(2,1)S(1)} %get-tuple-element.76), channel_id=1, source_target_pairs={{0,16},{16,0},{1,17},{17,1},{2,18},{18,2},{3,19},{19,3},{4,20},{20... | collective-permute-start | bytes 393224 | tf_op jit(solution)/shard_map/ppermute | solution.py:17
  9.5 3.0 %pad_maximum_fusion.refs_0_ = bf16[1024,896]{1,0:T(8,128)(2,1)} fusion(bf16[128,896]{1,0:T(8,128)(2,1)} %bitcast.48, bf16[896,896]{1,0:T(8,128)(2,1)} %refs_0_.1), kind=kLoop, calls=%fused_computation | loop fusion | flops 3670016 | bytes 3670016 | tf_op jit(solution)/shard_map/concatenate | solution.py:346
  16.6 4.2 %convolution_convert_fusion = bf16[256,512]{1,0:T(8,128)(2,1)S(1)} fusion(bf16[4096,256]{1,0:T(8,128)(2,1)} %param.13, bf16[512,4096]{1,0:T(8,128)(2,1)} %param.11), kind=kOutput, calls=%fused_computation.1 | convolution fusion | flops 1073872896 | bytes 6553600 | tf_op jit(solution)/shard_map/dot_general | solution.py:341
  21.5 3.6 %collective-permute-start.2 = (bf16[256,512]{1,0:T(8,128)(2,1)S(1)}, bf16[256,512]{1,0:T(8,128)(2,1)}, u32[]{:S(2)}, u32[]{:S(2)}) collective-permute-start(bf16[256,512]{1,0:T(8,128)(2,1)S(1)} %convolution_convert_fusion), channel_id=1, source_target_pairs={{0,4},{4,0},{1,5},{5,1},{2,6},{6,2},{3,7},{7,3},{8,12},{12,8},{9,1... | collective-permute-start | bytes 786440 | tf_op jit(solution)/shard_map/ppermute | solution.py:17
  26.1 5.3 %collective-permute-done.2 = bf16[256,512]{1,0:T(8,128)(2,1)} collective-permute-done((bf16[256,512]{1,0:T(8,128)(2,1)S(1)}, bf16[256,512]{1,0:T(8,128)(2,1)}, u32[]{:S(2)}, u32[]{:S(2)}) %collective-permute-start.2) | collective-permute-done | bytes 262176 | tf_op jit(solution)/shard_map/ppermute | solution.py:17
  38.6 9.5 %all-gather.4.cloned.1.call-done = bf16[4,2,32,2048]{3,2,1,0:T(8,128)(2,1)} async-done(((bf16[1,2,32,2048]{3,2,1,0:T(8,128)(2,1)}), bf16[4,2,32,2048]{3,2,1,0:T(8,128)(2,1)}) %all-gather.4.cloned.1.call-update) | async-done | bytes 1048592 | tf_op jit(solution)/shard_map/all_gather | solution.py:338
  48.1 2.5 %collective-permute-done.7 = bf16[2,256,512]{2,1,0:T(8,128)(2,1)} collective-permute-done((bf16[2,256,512]{2,1,0:T(8,128)(2,1)}, bf16[2,256,512]{2,1,0:T(8,128)(2,1)}, u32[]{:S(2)}, u32[]{:S(2)}) %collective-permute-start.7) | collective-permute-done | bytes 524320 | tf_op jit(solution)/shard_map/ppermute | solution.py:17
  52.3 3.0 %collective-permute-start.10 = (bf16[1,256,512]{2,1,0:T(8,128)(2,1)}, bf16[1,256,512]{2,1,0:T(8,128)(2,1)}, u32[]{:S(2)}, u32[]{:S(2)}) collective-permute-start(bf16[1,256,512]{2,1,0:T(8,128)(2,1)} %slice.14), channel_id=1, source_target_pairs={{0,3},{1,0},{2,1},{3,2},{4,7},{5,4},{6,5},{7,6},{8,11},{9,8},{10,9... | collective-permute-start | bytes 786440 | tf_op jit(solution)/shard_map/ppermute | solution.py:17
  61.3 3.3 %collective-permute-done.refs_1_.refs_0_ = bf16[1024,896]{1,0:T(8,128)(2,1)S(1)} collective-permute-done((bf16[1024,896]{1,0:T(8,128)(2,1)}, bf16[1024,896]{1,0:T(8,128)(2,1)S(1)}, u32[]{:S(2)}, u32[]{:S(2)}) %collective-permute-start) | collective-permute-done | bytes 1835040 | tf_op jit(solution)/shard_map/ppermute | solution.py:17
  69.1 2.9 %collective-permute-start.12 = (bf16[640,896]{1,0:T(8,128)(2,1)}, bf16[640,896]{1,0:T(8,128)(2,1)}, u32[]{:S(2)}, u32[]{:S(2)}) collective-permute-start(bf16[640,896]{1,0:T(8,128)(2,1)} %collective-permute-done.3.refs_3_), channel_id=1, source_target_pairs={{0,96},{32,0},{64,32},{96,64},{1,97},{33,1},{65,33},{97,65},{2,98}... | collective-permute-start | bytes 3440648 | tf_op jit(solution)/shard_map/ppermute | solution.py:17
  72.1 3.6 %cut.2 = (bf16[512,896]{1,0:T(8,128)(2,1)}, bf16[512,896]{1,0:T(8,128)(2,1)}, bf16[768,896]{1,0:T(8,128)(2,1)}) custom-call(bf16[1024,896]{1,0:T(8,128)(2,1)} %copy-done, bf16[1024,896]{1,0:T(8,128)(2,1)} %collective-permute-done.1.refs_2_.refs_1_), custom_call_target="tpu_custom_call" | custom-call | tf_op jit(solution)/shard_map/cut/pallas_call | solution.py:194
  76.9 8.4 %collective-permute-done.13.refs_4_.refs_3_ = bf16[384,896]{1,0:T(8,128)(2,1)} collective-permute-done((bf16[384,896]{1,0:T(8,128)(2,1)S(1)}, bf16[384,896]{1,0:T(8,128)(2,1)}, u32[]{:S(2)}, u32[]{:S(2)}) %collective-permute-start.13) | collective-permute-done | bytes 688160 | tf_op jit(solution)/shard_map/ppermute | solution.py:17
  91.9 15.5 %accumulate.3.refs_5_ = f32[1024,896]{1,0:T(8,128)} custom-call(s32[4]{0:T(128)} %pad_add_fusion.places_ref, bf16[512,14336]{1,0:T(8,128)(2,1)} %mine.5, bf16[512,14336]{1,0:T(8,128)(2,1)} %collective-permute-done.4.theirs, bf16[896,896]{1,0:T(8,128)(2,1)} %refs_0_.1, bf16[1024,896]{1,0:T(8,128)(2,1)} %copy-done, ...), custom_call_target="tpu_custom_call" | custom-call | tf_op jit(solution)/shard_map/accumulate/pallas_call | solution.py:270
  110.8 3.6 %collective-permute-done.14.refs_2_.refs_1_.refs_5_ = bf16[512,896]{1,0:T(8,128)(2,1)S(1)} collective-permute-done((bf16[512,896]{1,0:T(8,128)(2,1)}, bf16[512,896]{1,0:T(8,128)(2,1)S(1)}, u32[]{:S(2)}, u32[]{:S(2)}) %collective-permute-start.14) | collective-permute-done | bytes 917536 | tf_op jit(solution)/shard_map/ppermute | solution.py:17
  115.4 2.7 %cut.3 = (bf16[384,896]{1,0:T(8,128)(2,1)}, bf16[256,896]{1,0:T(8,128)(2,1)}, bf16[384,896]{1,0:T(8,128)(2,1)}) custom-call(bf16[640,896]{1,0:T(8,128)(2,1)} %collective-permute-done.11.refs_0_.refs_2_, bf16[640,896]{1,0:T(8,128)(2,1)} %collective-permute-done.12.refs_1_.refs_3_, bf16[512,896]{1,0:T(8,128)(2,1)} %copy-done.2), custom_call_target="tpu_custom_call" | custom-call | tf_op jit(solution)/shard_map/cut/pallas_call | solution.py:194
  120.1 2.3 %collective-permute-start.16 = (bf16[256,896]{1,0:T(8,128)(2,1)}, bf16[256,896]{1,0:T(8,128)(2,1)}, u32[]{:S(2)}, u32[]{:S(2)}) collective-permute-start(bf16[256,896]{1,0:T(8,128)(2,1)} %get-tuple-element.63), channel_id=1, source_target_pairs={{0,96},{32,0},{64,32},{96,64},{1,97},{33,1},{65,33},{97,65},{2,98}... | collective-permute-start | bytes 1376264 | tf_op jit(solution)/shard_map/ppermute | solution.py:17
  123.3 13.0 %accumulate.4.refs_3_ = f32[1024,896]{1,0:T(8,128)} custom-call(s32[3]{0:T(128)} %pad_add_fusion.1.places_ref, bf16[512,14336]{1,0:T(8,128)(2,1)} %mine.5, bf16[512,14336]{1,0:T(8,128)(2,1)} %collective-permute-done.4.theirs, bf16[512,896]{1,0:T(8,128)(2,1)} %copy-done.5, bf16[512,896]{1,0:T(8,128)(2,1)} %copy-done.2, ...), custom_call_target="tpu_custom_call" | custom-call | tf_op jit(solution)/shard_map/accumulate/pallas_call | solution.py:270
  137.2 6.6 %accumulate.5.mine = bf16[1024,896]{1,0:T(8,128)(2,1)} custom-call(s32[1]{0:T(128)} %bitcast.36.places_ref, bf16[512,14336]{1,0:T(8,128)(2,1)} %mine.5, bf16[512,14336]{1,0:T(8,128)(2,1)} %collective-permute-done.4.theirs, bf16[384,896]{1,0:T(8,128)(2,1)} %collective-permute-done.15.refs_0_, bf16[256,896]{1,0:T(8,128)(2,1)} %collective-permute-done.16.refs_1_, ...), custom_call_target="tpu_custom_call" | custom-call | tf_op jit(solution)/shard_map/accumulate/pallas_call | solution.py:270
  145.0 3.1 %collective-permute-done.20.more = bf16[1024,896]{1,0:T(8,128)(2,1)S(1)} collective-permute-done((bf16[1024,896]{1,0:T(8,128)(2,1)}, bf16[1024,896]{1,0:T(8,128)(2,1)S(1)}, u32[]{:S(2)}, u32[]{:S(2)}) %collective-permute-start.20) | collective-permute-done | bytes 1835040 | tf_op jit(solution)/shard_map/ppermute | solution.py:17
  149.4 19.0 %scores.1 = (f32[1,64]{1,0:T(1,128)}, f32[1,64]{1,0:T(1,128)}) custom-call(s32[8]{0:T(128)} %stack.137.chips_ref, s32[8]{0:T(128)} %stack.128.tiles_ref, s32[1]{0:T(128)} %bitcast.28.core_ref, bf16[1024,896]{1,0:T(8,128)(2,1)} %accumulate.5.mine, bf16[1024,896]{1,0:T(8,128)(2,1)} %copy-done.4, f32[512,1]{1,0:T(8,128)} %fusion.own_weight, ...), custom_call_target="tpu_custom_call" | custom-call | tf_op jit(solution)/shard_map/scores/pallas_call | solution.py:151
  171.8 2.2 %collective-permute-done.23 = f32[1,64]{1,0:T(1,128)S(1)} collective-permute-done((f32[1,64]{1,0:T(1,128)S(1)}, f32[1,64]{1,0:T(1,128)S(1)}, u32[]{:S(2)}, u32[]{:S(2)}) %collective-permute-start.23) | collective-permute-done | bytes 288 | tf_op jit(solution)/shard_map/ppermute | solution.py:463
  174.0 2.6 %collective-permute-start.24 = (f32[1,64]{1,0:T(1,128)S(1)}, f32[1,64]{1,0:T(1,128)S(1)}, u32[]{:S(2)}, u32[]{:S(2)}) collective-permute-start(f32[1,64]{1,0:T(1,128)S(1)} %add.224), channel_id=1, source_target_pairs={{0,3},{1,2},{2,1},{3,0},{4,7},{5,6},{6,5},{7,4},{8,11},{9,10},{10,... | collective-permute-start | bytes 776 | tf_op jit(solution)/shard_map/ppermute | solution.py:464
  176.6 2.1 %collective-permute-done.24 = f32[1,64]{1,0:T(1,128)S(1)} collective-permute-done((f32[1,64]{1,0:T(1,128)S(1)}, f32[1,64]{1,0:T(1,128)S(1)}, u32[]{:S(2)}, u32[]{:S(2)}) %collective-permute-start.24) | collective-permute-done | bytes 288 | tf_op jit(solution)/shard_map/ppermute | solution.py:464
  178.7 3.6 %collective-permute-start.25 = (f32[1,64]{1,0:T(1,128)S(1)}, f32[1,64]{1,0:T(1,128)S(1)}, u32[]{:S(2)}, u32[]{:S(2)}) collective-permute-start(f32[1,64]{1,0:T(1,128)S(1)} %add.225), channel_id=1, source_target_pairs={{0,4},{4,0},{1,5},{5,1},{2,6},{6,2},{3,7},{7,3},{8,12},{12,8},{9,1... | collective-permute-start | bytes 776 | tf_op jit(solution)/shard_map/ppermute | solution.py:17
  (86 shorter events, 49.3 us)
Async XLA Ops:
  6.5 41.6 %all-gather.4.cloned.1.call-start = ((), (), s32[]{:S(2)}) async-start(), calls=%async_computation | async-start | bytes 1310720 | tf_op jit(solution)/shard_map/all_gather | solution.py:338
  6.5 28.2 %collective-permute-start.4 = (bf16[512,14336]{1,0:T(8,128)(2,1)}, bf16[512,14336]{1,0:T(8,128)(2,1)}, u32[]{:S(2)}, u32[]{:S(2)}) collective-permute-start(bf16[512,14336]{1,0:T(8,128)(2,1)} %mine.5), channel_id=1, source_target_pairs={{0,8},{8,0},{1,9},{9,1},{2,10},{10,2},{3,11},{11,3},{4,12},{12,4},... | collective-permute-start | bytes 44040200 | tf_op jit(solution)/shard_map/ppermute | solution.py:17
  7.5 8.3 %collective-permute-start.6 = (bf16[32,2048]{1,0:T(8,128)(2,1)S(1)}, bf16[32,2048]{1,0:T(8,128)(2,1)S(1)}, u32[]{:S(2)}, u32[]{:S(2)}) collective-permute-start(bf16[32,2048]{1,0:T(8,128)(2,1)S(1)} %get-tuple-element.76), channel_id=1, source_target_pairs={{0,16},{16,0},{1,17},{17,1},{2,18},{18,2},{3,19},{19,3},{4,20},{20... | collective-permute-start | bytes 393224 | tf_op jit(solution)/shard_map/ppermute | solution.py:17
  12.5 52.1 %collective-permute-start = (bf16[1024,896]{1,0:T(8,128)(2,1)}, bf16[1024,896]{1,0:T(8,128)(2,1)S(1)}, u32[]{:S(2)}, u32[]{:S(2)}) collective-permute-start(bf16[1024,896]{1,0:T(8,128)(2,1)} %pad_maximum_fusion.refs_0_), channel_id=1, source_target_pairs={{0,32},{32,64},{64,96},{96,0},{1,33},{33,65},{65,97},{97,1},{2,34}... | collective-permute-start | bytes 5505032 | tf_op jit(solution)/shard_map/ppermute | solution.py:17
  14.1 50.6 %collective-permute-start.1 = (bf16[1024,896]{1,0:T(8,128)(2,1)}, bf16[1024,896]{1,0:T(8,128)(2,1)}, u32[]{:S(2)}, u32[]{:S(2)}) collective-permute-start(bf16[1024,896]{1,0:T(8,128)(2,1)} %pad_maximum_fusion.refs_0_), channel_id=1, source_target_pairs={{0,96},{32,0},{64,32},{96,64},{1,97},{33,1},{65,33},{97,65},{2,98}... | collective-permute-start | bytes 5505032 | tf_op jit(solution)/shard_map/ppermute | solution.py:17
  16.5 131.6 %all-gather.6.cloned.1.call-start = ((), (), s32[]{:S(2)}) async-start(), calls=%async_computation.1 | async-start | bytes 5242880 | tf_op jit(solution)/shard_map/all_gather | solution.py:393
  21.5 9.9 %collective-permute-start.2 = (bf16[256,512]{1,0:T(8,128)(2,1)S(1)}, bf16[256,512]{1,0:T(8,128)(2,1)}, u32[]{:S(2)}, u32[]{:S(2)}) collective-permute-start(bf16[256,512]{1,0:T(8,128)(2,1)S(1)} %convolution_convert_fusion), channel_id=1, source_target_pairs={{0,4},{4,0},{1,5},{5,1},{2,6},{6,2},{3,7},{7,3},{8,12},{12,8},{9,1... | collective-permute-start | bytes 786440 | tf_op jit(solution)/shard_map/ppermute | solution.py:17
  32.5 28.8 %collective-permute-start.3 = (bf16[640,896]{1,0:T(8,128)(2,1)}, bf16[640,896]{1,0:T(8,128)(2,1)}, u32[]{:S(2)}, u32[]{:S(2)}) collective-permute-start(bf16[640,896]{1,0:T(8,128)(2,1)} %slice.12), channel_id=1, source_target_pairs={{0,16},{16,0},{1,17},{17,1},{2,18},{18,2},{3,19},{19,3},{4,20},{20... | collective-permute-start | bytes 3440648 | tf_op jit(solution)/shard_map/ppermute | solution.py:17
  34.7 15.9 %collective-permute-start.7 = (bf16[2,256,512]{2,1,0:T(8,128)(2,1)}, bf16[2,256,512]{2,1,0:T(8,128)(2,1)}, u32[]{:S(2)}, u32[]{:S(2)}) collective-permute-start(bf16[2,256,512]{2,1,0:T(8,128)(2,1)} %maximum_select_fusion), channel_id=1, source_target_pairs={{0,1},{1,2},{2,3},{3,0},{4,5},{5,6},{6,7},{7,4},{8,9},{9,10},{10,1... | collective-permute-start | bytes 1572872 | tf_op jit(solution)/shard_map/ppermute | solution.py:17
  36.3 14.3 %collective-permute-start.8 = (bf16[2,256,512]{2,1,0:T(8,128)(2,1)}, bf16[2,256,512]{2,1,0:T(8,128)(2,1)}, u32[]{:S(2)}, u32[]{:S(2)}) collective-permute-start(bf16[2,256,512]{2,1,0:T(8,128)(2,1)} %maximum_select_fusion), channel_id=1, source_target_pairs={{0,3},{1,0},{2,1},{3,2},{4,7},{5,4},{6,5},{7,6},{8,11},{9,8},{10,9... | collective-permute-start | bytes 1572872 | tf_op jit(solution)/shard_map/ppermute | solution.py:17
  52.3 12.4 %collective-permute-start.10 = (bf16[1,256,512]{2,1,0:T(8,128)(2,1)}, bf16[1,256,512]{2,1,0:T(8,128)(2,1)}, u32[]{:S(2)}, u32[]{:S(2)}) collective-permute-start(bf16[1,256,512]{2,1,0:T(8,128)(2,1)} %slice.14), channel_id=1, source_target_pairs={{0,3},{1,0},{2,1},{3,2},{4,7},{5,4},{6,5},{7,6},{8,11},{9,8},{10,9... | collective-permute-start | bytes 786440 | tf_op jit(solution)/shard_map/ppermute | solution.py:17
  56.9 8.8 %collective-permute-start.9 = (bf16[1,256,512]{2,1,0:T(8,128)(2,1)}, bf16[1,256,512]{2,1,0:T(8,128)(2,1)}, u32[]{:S(2)}, u32[]{:S(2)}) collective-permute-start(bf16[1,256,512]{2,1,0:T(8,128)(2,1)} %slice.13), channel_id=1, source_target_pairs={{0,1},{1,2},{2,3},{3,0},{4,5},{5,6},{6,7},{7,4},{8,9},{9,10},{10,1... | collective-permute-start | bytes 786440 | tf_op jit(solution)/shard_map/ppermute | solution.py:17
  66.8 18.6 %collective-permute-start.13 = (bf16[384,896]{1,0:T(8,128)(2,1)S(1)}, bf16[384,896]{1,0:T(8,128)(2,1)}, u32[]{:S(2)}, u32[]{:S(2)}) collective-permute-start(bf16[384,896]{1,0:T(8,128)(2,1)S(1)} %pad_maximum_fusion.1), channel_id=1, source_target_pairs={{0,16},{16,0},{1,17},{17,1},{2,18},{18,2},{3,19},{19,3},{4,20},{20... | collective-permute-start | bytes 2064392 | tf_op jit(solution)/shard_map/ppermute | solution.py:17
  68.8 41.9 %collective-permute-start.11 = (bf16[640,896]{1,0:T(8,128)(2,1)}, bf16[640,896]{1,0:T(8,128)(2,1)}, u32[]{:S(2)}, u32[]{:S(2)}) collective-permute-start(bf16[640,896]{1,0:T(8,128)(2,1)} %collective-permute-done.3.refs_3_), channel_id=1, source_target_pairs={{0,32},{32,64},{64,96},{96,0},{1,33},{33,65},{65,97},{97,1},{2,34}... | collective-permute-start | bytes 3440648 | tf_op jit(solution)/shard_map/ppermute | solution.py:17
  69.1 41.6 %collective-permute-start.12 = (bf16[640,896]{1,0:T(8,128)(2,1)}, bf16[640,896]{1,0:T(8,128)(2,1)}, u32[]{:S(2)}, u32[]{:S(2)}) collective-permute-start(bf16[640,896]{1,0:T(8,128)(2,1)} %collective-permute-done.3.refs_3_), channel_id=1, source_target_pairs={{0,96},{32,0},{64,32},{96,64},{1,97},{33,1},{65,33},{97,65},{2,98}... | collective-permute-start | bytes 3440648 | tf_op jit(solution)/shard_map/ppermute | solution.py:17
  75.7 38.7 %collective-permute-start.14 = (bf16[512,896]{1,0:T(8,128)(2,1)}, bf16[512,896]{1,0:T(8,128)(2,1)S(1)}, u32[]{:S(2)}, u32[]{:S(2)}) collective-permute-start(bf16[512,896]{1,0:T(8,128)(2,1)} %get-tuple-element.61), channel_id=1, source_target_pairs={{0,96},{32,0},{64,32},{96,64},{1,97},{33,1},{65,33},{97,65},{2,98}... | collective-permute-start | bytes 2752520 | tf_op jit(solution)/shard_map/ppermute | solution.py:17
  76.3 46.1 %collective-permute-start.19 = (bf16[768,896]{1,0:T(8,128)(2,1)}, bf16[768,896]{1,0:T(8,128)(2,1)}, u32[]{:S(2)}, u32[]{:S(2)}) collective-permute-start(bf16[768,896]{1,0:T(8,128)(2,1)} %get-tuple-element.67), channel_id=1, source_target_pairs={{0,16},{16,0},{1,17},{17,1},{2,18},{18,2},{3,19},{19,3},{4,20},{20... | collective-permute-start | bytes 4128776 | tf_op jit(solution)/shard_map/ppermute | solution.py:17
  85.3 37.1 %collective-permute-start.18 = (bf16[512,896]{1,0:T(8,128)(2,1)}, bf16[512,896]{1,0:T(8,128)(2,1)S(1)}, u32[]{:S(2)}, u32[]{:S(2)}) collective-permute-start(bf16[512,896]{1,0:T(8,128)(2,1)} %get-tuple-element.66), channel_id=1, source_target_pairs={{0,32},{32,64},{64,96},{96,0},{1,33},{33,65},{65,97},{97,1},{2,34}... | collective-permute-start | bytes 2752520 | tf_op jit(solution)/shard_map/ppermute | solution.py:17
  118.1 18.3 %collective-permute-start.15 = (bf16[384,896]{1,0:T(8,128)(2,1)}, bf16[384,896]{1,0:T(8,128)(2,1)}, u32[]{:S(2)}, u32[]{:S(2)}) collective-permute-start(bf16[384,896]{1,0:T(8,128)(2,1)} %get-tuple-element.62), channel_id=1, source_target_pairs={{0,32},{32,64},{64,96},{96,0},{1,33},{33,65},{65,97},{97,1},{2,34}... | collective-permute-start | bytes 2064392 | tf_op jit(solution)/shard_map/ppermute | solution.py:17
  119.1 17.2 %collective-permute-start.17 = (bf16[384,896]{1,0:T(8,128)(2,1)}, bf16[384,896]{1,0:T(8,128)(2,1)S(1)}, u32[]{:S(2)}, u32[]{:S(2)}) collective-permute-start(bf16[384,896]{1,0:T(8,128)(2,1)} %get-tuple-element.64), channel_id=1, source_target_pairs={{0,16},{16,0},{1,17},{17,1},{2,18},{18,2},{3,19},{19,3},{4,20},{20... | collective-permute-start | bytes 2064392 | tf_op jit(solution)/shard_map/ppermute | solution.py:17
  120.1 16.3 %collective-permute-start.16 = (bf16[256,896]{1,0:T(8,128)(2,1)}, bf16[256,896]{1,0:T(8,128)(2,1)}, u32[]{:S(2)}, u32[]{:S(2)}) collective-permute-start(bf16[256,896]{1,0:T(8,128)(2,1)} %get-tuple-element.63), channel_id=1, source_target_pairs={{0,96},{32,0},{64,32},{96,64},{1,97},{33,1},{65,33},{97,65},{2,98}... | collective-permute-start | bytes 1376264 | tf_op jit(solution)/shard_map/ppermute | solution.py:17
  122.4 22.6 %collective-permute-start.21 = (bf16[8,256,512]{2,1,0:T(8,128)(2,1)}, bf16[8,256,512]{2,1,0:T(8,128)(2,1)}, u32[]{:S(2)}, u32[]{:S(2)}) collective-permute-start(bf16[8,256,512]{2,1,0:T(8,128)(2,1)} %constant_dynamic-update-slice_fusion.own_acts), channel_id=1, source_target_pairs={{0,8},{8,0},{1,9},{9,1},{2,10},{10,2},{3,11},{11,3},{4,12},{12,4},... | collective-permute-start | bytes 6291464 | tf_op jit(solution)/shard_map/ppermute | solution.py:17
  174.0 4.8 %collective-permute-start.24 = (f32[1,64]{1,0:T(1,128)S(1)}, f32[1,64]{1,0:T(1,128)S(1)}, u32[]{:S(2)}, u32[]{:S(2)}) collective-permute-start(f32[1,64]{1,0:T(1,128)S(1)} %add.224), channel_id=1, source_target_pairs={{0,3},{1,2},{2,1},{3,0},{4,7},{5,6},{6,5},{7,4},{8,11},{9,10},{10,... | collective-permute-start | bytes 776 | tf_op jit(solution)/shard_map/ppermute | solution.py:464
  178.7 5.1 %collective-permute-start.25 = (f32[1,64]{1,0:T(1,128)S(1)}, f32[1,64]{1,0:T(1,128)S(1)}, u32[]{:S(2)}, u32[]{:S(2)}) collective-permute-start(f32[1,64]{1,0:T(1,128)S(1)} %add.225), channel_id=1, source_target_pairs={{0,4},{4,0},{1,5},{5,1},{2,6},{6,2},{3,7},{7,3},{8,12},{12,8},{9,1... | collective-permute-start | bytes 776 | tf_op jit(solution)/shard_map/ppermute | solution.py:17
  (12 other events, 47.8 us)
Sparse Core Ops, SparseCore 0:
  16.6 31.4 all-gather.3
  65.9 48.8 all-gather.5

commit v4 on v3

--- a/solution.py
+++ b/solution.py
@@ -150,7 +150,7 @@
     anywhere = pl.BlockSpec(memory_space=pltpu.HBM)
     return pl.pallas_call(
         functools.partial(score_kernel, right_rows=right_rows, count=len(rights)),
-        in_specs=[*[scalars] * 3, *[anywhere] * (8 + len(rights))],
+        in_specs=[*[scalars] * 3, anywhere, held, *[anywhere] * (6 + len(rights))],
         out_specs=[held, held],
         scratch_shapes=[
             pltpu.VMEM(mine.shape, bf16),
@@ -167,7 +167,7 @@
             pltpu.VMEM((2, tokens, 1), f32),
         ],
         out_shape=[jax.ShapeDtypeStruct((1, number), f32)] * 2,
-        compiler_params=pltpu.CompilerParams(vmem_limit_bytes=62 * 1024 * 1024),
+        compiler_params=pltpu.CompilerParams(vmem_limit_bytes=48 * 1024 * 1024),
         name="scores",
     )(chips_at, tiles_at, core, mine, more, *weights, *acts, eig, left, *rights)
 
@@ -260,7 +260,7 @@
     out_ref[...] = total.astype(out_ref.dtype)
 
 
-def accumulate(places, mine, theirs, plan, pieces, carried, kind):
+def accumulate(places, mine, theirs, plan, pieces, carried, kind, near=False):
     tokens = mine.shape[0]
     rows = sum(deep for _, deep, _, _ in plan[0])
     cols = pieces[0].shape[1]
@@ -273,7 +273,9 @@
         ),
         in_specs=[
             pl.BlockSpec(memory_space=pltpu.SMEM),
-            *[anywhere] * (2 + len(pieces) + len(carried)),
+            *[anywhere] * 2,
+            *[held if near else anywhere] * len(pieces),
+            *[anywhere] * len(carried),
         ],
         out_specs=held,
         out_shape=jax.ShapeDtypeStruct((2 * tokens, cols), kind),
@@ -350,9 +352,7 @@
         (output_basis, query_right, other, left_pair)
     )
     beside_head = across(basis_z[:most])
-    beside_end = across(
-        jnp.concatenate([basis_z[most:], right_z.reshape(queries * rank, cols)], axis=0)
-    )
+    block_end = jnp.concatenate([basis_z[most:], right_z.reshape(queries * rank, cols)], axis=0)
 
     pair = jnp.where(zh == 0, jnp.stack([share, other]), jnp.stack([other, share]))
     weights = token_weights(doc_ids, doc_lengths)
@@ -381,16 +381,18 @@
     weights = weights.reshape(tokens, 1)
     weights_peer = weights_peer.reshape(tokens, 1)
     (
-        before, after, beside_head, weights, weights_peer, left_chips, pair_far_0, pair_far_1,
-        tiles_at, chips_at, core_at, places_a, places_c, places_d,
+        before, after, beside_head, block_end, weights, weights_peer, left_chips, pair_far_0,
+        pair_far_1, tiles_at, chips_at, core_at, places_a, places_c, places_d,
     ) = lax.optimization_barrier(
         (
-            before, after, beside_head, weights, weights_peer, left_chips, pair_far_0,
+            before, after, beside_head, block_end, weights, weights_peer, left_chips, pair_far_0,
             pair_far_1, tiles_at, chips_at, core_at, places_a, places_c, places_d,
         )
     )
 
     left = lax.all_gather(left_chips, "x", axis=0)
+    beside_end = across(block_end)
+    before_beside_a = forth(beside_head)
     length = before.shape[0]
     end = length - most
     before_head, after_tail, both_ends = cut_out(
@@ -402,11 +404,11 @@
             (1, most, end, 2, end),
         ),
     )
+    after_tail, beside_late = lax.optimization_barrier((after_tail, beside_head))
     far_a, far_b = forth(before_head), back(after_tail)
+    after_beside_a = back(beside_late)
     beside_ends = across(both_ends)
-    before_beside_a, after_beside_a = forth(beside_head), back(beside_head)
     acts = jnp.concatenate([pair, pair_before, pair_after, pair_far_0, pair_far_1])
-    before_beside_a, after_beside_a = forth(beside_head), back(beside_head)
     acts = jnp.concatenate([pair, pair_before, pair_after, pair_far_0, pair_far_1])
     sums = accumulate(
         places_a, out_grads, grads_peer,
@@ -418,18 +420,11 @@
         ),
         (output_basis, before, after, beside_head, beside_end), (), f32,
     )
-    before_beside_a, after_beside_a, sums, acts = lax.optimization_barrier(
-        (before_beside_a, after_beside_a, sums, acts)
-    )
-
-    part_a, part_b, part_c = cut_out(
-        (before_beside_a, after_beside_a, far_b),
-        (
-            (0, 0, 3 * tile, 0, 0),
-            (1, 3 * tile, 2 * tile, 1, 0),
-            (2, most - half, end, 2, 0),
-        ),
-    )
+    far_b, sums, acts = lax.optimization_barrier((far_b, sums, acts))
+
+    (part_a,) = cut_out((before_beside_a,), ((0, 0, 3 * tile, 0, 0),))
+    (part_b,) = cut_out((after_beside_a,), ((0, 3 * tile, 2 * tile, 0, 0),))
+    (part_c,) = cut_out((far_b,), ((0, most - half, end, 0, 0),))
     far_beside_a, far_beside_b, far_beside_c = forth(part_a), back(part_b), across(part_c)
     acts_peer = sibling(acts)
     sums = accumulate(
@@ -445,7 +440,7 @@
     mine = accumulate(
         places_d, out_grads, grads_peer,
         (((0, 3 * tile, 0, 0), (3 * tile, 2 * tile, 1, 0), (most, rows - most, 2, 0)),),
-        (far_beside_a, far_beside_b, far_beside_c), (sums,), bf16,
+        (far_beside_a, far_beside_b, far_beside_c), (sums,), bf16, near=True,
     )
     more = sibling(mine)
 

time: 192 us -> 188 us (0.979)
  local copies, waits for them, and re-layouts: 22.1 us -> 15 us
  starting transfers between devices: 35.2 us -> 37.8 us
  Pallas kernels: 60.4 us -> 62.9 us
  other arithmetic: 11.1 us -> 8.63 us
    unnamed x20 -> x18, local copies, waits for them, and re-layouts: 12 us -> 7.69 us
    pallas_call x2 -> x4, Pallas kernels: 6.28 us -> 9.31 us  [cut_out(): pl.pallas_call(functools.partial(cut_kernel, cuts=cuts, count=len(arrays)...]
    ppermute x24, starting transfers between devices: 31.1 us -> 33.6 us  [shifted(): lax.ppermute(value, axis, [(i, (i + step) % size) for i in range(size)])]
    select_n x1, other arithmetic: 2.08 us -> 0.08 us  [per_device(): jnp.where(zh == 0, jnp.stack([share, other]), jnp.stack([other, share]))]
    pallas_call x1, Pallas kernels: 19 us -> 17.1 us  [scores_of(): pl.pallas_call(functools.partial(score_kernel, right_rows=right_rows, cou...]
  transfers between devices with their start and end apart: 28 -> 28, of which waited for: 13 -> 14; matrix products, arithmetic and copies ran while one was open for 17% -> 13% of each run, Pallas kernels for 22% -> 24%
where the time goes in v4:
time: 188 us
  Pallas kernels  62.9 us (33%)
  waiting for transfers between devices  44.8 us (24%)
  starting transfers between devices  37.8 us (20%)
  local copies, waits for them, and re-layouts  15 us (8%)
  between operations  14.3 us (8%)
  other arithmetic  8.63 us (5%)
  matrix products  4.23 us (2%)
    pallas_call x3, Pallas kernels, accumulate(): pl.pallas_call(functools.partial(accumulate_kernel, plan=plan, count=len(...  36.5 us
    ppermute x24, starting transfers between devices, shifted(): lax.ppermute(value, axis, [(i, (i + step) % size) for i in range(size)])  33.6 us
    ppermute x24, waiting for transfers between devices, shifted(): lax.ppermute(value, axis, [(i, (i + step) % size) for i in range(size)])  30.6 us
    pallas_call x1, Pallas kernels, scores_of(): pl.pallas_call(functools.partial(score_kernel, right_rows=right_rows, cou...  17.1 us
    all_gather x1, waiting for transfers between devices, per_device(): left_dp = lax.all_gather(left_pair, 'y', axis=0)  10 us
    pallas_call x4, Pallas kernels, cut_out(): pl.pallas_call(functools.partial(cut_kernel, cuts=cuts, count=len(arrays)...  9.31 us
    unnamed x18, local copies, waits for them, and re-layouts  7.69 us
    dot_general x1, matrix products, per_device(): lax.dot_general(input_basis, activations, (((0,), (1,)), ((), ())), prefe...  4.23 us
  transfers between devices with their start and end apart: 28, of which 14 were waited for; matrix products, arithmetic and copies ran while one was open for 13% of the time, Pallas kernels for 24%

profile of v4, /device:TPU:0, one launch (start us, length us, event | category | flops | bytes accessed | tf_op | source)
XLA Modules:
  0.0 187.6 jit_solution(1901579272116206731)
XLA Ops:
  7.5 2.1 %collective-permute-start.6 = (bf16[32,2048]{1,0:T(8,128)(2,1)S(1)}, bf16[32,2048]{1,0:T(8,128)(2,1)S(1)}, u32[]{:S(2)}, u32[]{:S(2)}) collective-permute-start(bf16[32,2048]{1,0:T(8,128)(2,1)S(1)} %get-tuple-element.74), channel_id=1, source_target_pairs={{0,16},{16,0},{1,17},{17,1},{2,18},{18,2},{3,19},{19,3},{4,20},{20... | collective-permute-start | bytes 393224 | tf_op jit(solution)/shard_map/ppermute | solution.py:17
  9.5 3.0 %pad_maximum_fusion.refs_0_ = bf16[1024,896]{1,0:T(8,128)(2,1)} fusion(bf16[128,896]{1,0:T(8,128)(2,1)} %bitcast.48, bf16[896,896]{1,0:T(8,128)(2,1)} %refs_0_.1), kind=kLoop, calls=%fused_computation | loop fusion | flops 3670016 | bytes 3670016 | tf_op jit(solution)/shard_map/concatenate | solution.py:348
  16.6 4.2 %convolution_convert_fusion = bf16[256,512]{1,0:T(8,128)(2,1)S(1)} fusion(bf16[4096,256]{1,0:T(8,128)(2,1)} %param.13, bf16[512,4096]{1,0:T(8,128)(2,1)} %param.11), kind=kOutput, calls=%fused_computation.1 | convolution fusion | flops 1073872896 | bytes 6553600 | tf_op jit(solution)/shard_map/dot_general | solution.py:343
  20.8 3.7 %collective-permute-start.2 = (bf16[256,512]{1,0:T(8,128)(2,1)S(1)}, bf16[256,512]{1,0:T(8,128)(2,1)S(1)}, u32[]{:S(2)}, u32[]{:S(2)}) collective-permute-start(bf16[256,512]{1,0:T(8,128)(2,1)S(1)} %convolution_convert_fusion), channel_id=1, source_target_pairs={{0,4},{4,0},{1,5},{5,1},{2,6},{6,2},{3,7},{7,3},{8,12},{12,8},{9,1... | collective-permute-start | bytes 786440 | tf_op jit(solution)/shard_map/ppermute | solution.py:17
  25.5 5.2 %collective-permute-done.2 = bf16[256,512]{1,0:T(8,128)(2,1)S(1)} collective-permute-done((bf16[256,512]{1,0:T(8,128)(2,1)S(1)}, bf16[256,512]{1,0:T(8,128)(2,1)S(1)}, u32[]{:S(2)}, u32[]{:S(2)}) %collective-permute-start.2) | collective-permute-done | bytes 262176 | tf_op jit(solution)/shard_map/ppermute | solution.py:17
  38.1 10.0 %all-gather.4.cloned.1.call-done = bf16[4,2,32,2048]{3,2,1,0:T(8,128)(2,1)} async-done(((bf16[1,2,32,2048]{3,2,1,0:T(8,128)(2,1)}), bf16[4,2,32,2048]{3,2,1,0:T(8,128)(2,1)}) %all-gather.4.cloned.1.call-update) | async-done | bytes 1048592 | tf_op jit(solution)/shard_map/all_gather | solution.py:340
  50.0 3.0 %collective-permute-start.10 = (bf16[1,256,512]{2,1,0:T(8,128)(2,1)}, bf16[1,256,512]{2,1,0:T(8,128)(2,1)}, u32[]{:S(2)}, u32[]{:S(2)}) collective-permute-start(bf16[1,256,512]{2,1,0:T(8,128)(2,1)} %slice.15), channel_id=1, source_target_pairs={{0,3},{1,0},{2,1},{3,2},{4,7},{5,4},{6,5},{7,6},{8,11},{9,8},{10,9... | collective-permute-start | bytes 786440 | tf_op jit(solution)/shard_map/ppermute | solution.py:17
  58.4 6.2 %collective-permute-done.refs_0_.refs_1_ = bf16[1024,896]{1,0:T(8,128)(2,1)} collective-permute-done((bf16[1024,896]{1,0:T(8,128)(2,1)}, bf16[1024,896]{1,0:T(8,128)(2,1)}, u32[]{:S(2)}, u32[]{:S(2)}) %collective-permute-start) | collective-permute-done | bytes 1835040 | tf_op jit(solution)/shard_map/ppermute | solution.py:17
  66.7 3.6 %cut.5 = (bf16[512,896]{1,0:T(8,128)(2,1)}, bf16[512,896]{1,0:T(8,128)(2,1)}, bf16[768,896]{1,0:T(8,128)(2,1)}) custom-call(bf16[1024,896]{1,0:T(8,128)(2,1)} %collective-permute-done.refs_0_.refs_1_, bf16[1024,896]{1,0:T(8,128)(2,1)} %collective-permute-done.1.refs_1_.refs_2_), custom_call_target="tpu_custom_call" | custom-call | tf_op jit(solution)/shard_map/cut/pallas_call | solution.py:194
  75.4 7.9 %collective-permute-done.16.refs_4_.refs_3_ = bf16[384,896]{1,0:T(8,128)(2,1)S(1)} collective-permute-done((bf16[384,896]{1,0:T(8,128)(2,1)}, bf16[384,896]{1,0:T(8,128)(2,1)S(1)}, u32[]{:S(2)}, u32[]{:S(2)}) %collective-permute-start.16) | collective-permute-done | bytes 688160 | tf_op jit(solution)/shard_map/ppermute | solution.py:17
  86.6 1.9 %constant_dynamic-update-slice_fusion.2 = bf16[8,256,512]{2,1,0:T(8,128)(2,1)} fusion(bf16[8,256,512]{2,1,0:T(8,128)(2,1)} %constant_dynamic-update-slice_fusion.3, bf16[2,256,512]{2,1,0:T(8,128)(2,1)} %collective-permute-done.8), kind=kLoop, calls=%fused_computation.12 | loop fusion | bytes 1048576
  91.9 15.5 %accumulate.3.refs_5_ = f32[1024,896]{1,0:T(8,128)} custom-call(s32[4]{0:T(128)} %pad_add_fusion.places_ref, bf16[512,14336]{1,0:T(8,128)(2,1)} %mine.5, bf16[512,14336]{1,0:T(8,128)(2,1)} %collective-permute-done.4.theirs, bf16[896,896]{1,0:T(8,128)(2,1)} %refs_0_.1, bf16[1024,896]{1,0:T(8,128)(2,1)} %collective-permute-done.refs_0_.refs_1_, ...), custom_call_target="tpu_custom_call" | custom-call | tf_op jit(solution)/shard_map/accumulate/pallas_call | solution.py:270
  108.3 2.0 %cut.7 = bf16[384,896]{1,0:T(8,128)(2,1)} custom-call(bf16[512,896]{1,0:T(8,128)(2,1)} %copy-done), custom_call_target="tpu_custom_call" | custom-call | tf_op jit(solution)/shard_map/cut/pallas_call | solution.py:194
  110.6 2.0 %cut.4 = bf16[384,896]{1,0:T(8,128)(2,1)} custom-call(bf16[640,896]{1,0:T(8,128)(2,1)} %collective-permute-done.11.refs_0_.refs_2_), custom_call_target="tpu_custom_call" | custom-call | tf_op jit(solution)/shard_map/cut/pallas_call | solution.py:194
  114.0 2.3 %collective-permute-done.13.refs_0_.refs_3_ = bf16[640,896]{1,0:T(8,128)(2,1)} collective-permute-done((bf16[640,896]{1,0:T(8,128)(2,1)}, bf16[640,896]{1,0:T(8,128)(2,1)}, u32[]{:S(2)}, u32[]{:S(2)}) %collective-permute-start.13) | collective-permute-done | bytes 1146912 | tf_op jit(solution)/shard_map/ppermute | solution.py:17
  118.0 3.4 %collective-permute-start.14 = (bf16[256,896]{1,0:T(8,128)(2,1)}, bf16[256,896]{1,0:T(8,128)(2,1)}, u32[]{:S(2)}, u32[]{:S(2)}) collective-permute-start(bf16[256,896]{1,0:T(8,128)(2,1)} %cut.6), channel_id=1, source_target_pairs={{0,96},{32,0},{64,32},{96,64},{1,97},{33,1},{65,33},{97,65},{2,98}... | collective-permute-start | bytes 1376264 | tf_op jit(solution)/shard_map/ppermute | solution.py:17
  121.4 13.0 %accumulate.4.refs_3_ = f32[1024,896]{1,0:T(8,128)} custom-call(s32[3]{0:T(128)} %pad_add_fusion.1.places_ref, bf16[512,14336]{1,0:T(8,128)(2,1)} %mine.5, bf16[512,14336]{1,0:T(8,128)(2,1)} %collective-permute-done.4.theirs, bf16[512,896]{1,0:T(8,128)(2,1)} %collective-permute-done.18.refs_0_, bf16[512,896]{1,0:T(8,128)(2,1)} %copy-done, ...), custom_call_target="tpu_custom_call" | custom-call | tf_op jit(solution)/shard_map/accumulate/pallas_call | solution.py:270
  134.4 8.1 %accumulate.5.mine = bf16[1024,896]{1,0:T(8,128)(2,1)} custom-call(s32[1]{0:T(128)} %bitcast.37.places_ref, bf16[512,14336]{1,0:T(8,128)(2,1)} %mine.5, bf16[512,14336]{1,0:T(8,128)(2,1)} %collective-permute-done.4.theirs, bf16[384,896]{1,0:T(8,128)(2,1)} %collective-permute-done.12.refs_0_, bf16[256,896]{1,0:T(8,128)(2,1)} %collective-permute-done.14.refs_1_, ...), custom_call_target="tpu_custom_call" | custom-call | tf_op jit(solution)/shard_map/accumulate/pallas_call | solution.py:270
  143.5 3.6 %collective-permute-done.20.more = bf16[1024,896]{1,0:T(8,128)(2,1)} collective-permute-done((bf16[1024,896]{1,0:T(8,128)(2,1)}, bf16[1024,896]{1,0:T(8,128)(2,1)}, u32[]{:S(2)}, u32[]{:S(2)}) %collective-permute-start.20) | collective-permute-done | bytes 1835040 | tf_op jit(solution)/shard_map/ppermute | solution.py:17
  148.6 17.1 %scores.1 = (f32[1,64]{1,0:T(1,128)S(1)}, f32[1,64]{1,0:T(1,128)S(1)}) custom-call(s32[8]{0:T(128)S(1)} %stack.137.chips_ref, s32[8]{0:T(128)S(1)} %stack.128.tiles_ref, s32[1]{0:T(128)} %bitcast.29.core_ref, bf16[1024,896]{1,0:T(8,128)(2,1)S(1)} %copy-done.2, bf16[1024,896]{1,0:T(8,128)(2,1)} %collective-permute-done.20.more, f32[512,1]{1,0:T(8,128)S(1)} %fusion.own_weight, ...), custom_call_target="tpu_custom_call" | custom-call | tf_op jit(solution)/shard_map/scores/pallas_call | solution.py:151
  168.3 2.1 %collective-permute-done.23 = f32[1,64]{1,0:T(1,128)S(1)} collective-permute-done((f32[1,64]{1,0:T(1,128)S(1)}, f32[1,64]{1,0:T(1,128)S(1)}, u32[]{:S(2)}, u32[]{:S(2)}) %collective-permute-start.23) | collective-permute-done | bytes 288 | tf_op jit(solution)/shard_map/ppermute | solution.py:458
  170.5 2.7 %collective-permute-start.24 = (f32[1,64]{1,0:T(1,128)S(1)}, f32[1,64]{1,0:T(1,128)S(1)}, u32[]{:S(2)}, u32[]{:S(2)}) collective-permute-start(f32[1,64]{1,0:T(1,128)S(1)} %add.224), channel_id=1, source_target_pairs={{0,3},{1,2},{2,1},{3,0},{4,7},{5,6},{6,5},{7,4},{8,11},{9,10},{10,... | collective-permute-start | bytes 776 | tf_op jit(solution)/shard_map/ppermute | solution.py:459
  173.2 2.1 %collective-permute-done.24 = f32[1,64]{1,0:T(1,128)S(1)} collective-permute-done((f32[1,64]{1,0:T(1,128)S(1)}, f32[1,64]{1,0:T(1,128)S(1)}, u32[]{:S(2)}, u32[]{:S(2)}) %collective-permute-start.24) | collective-permute-done | bytes 288 | tf_op jit(solution)/shard_map/ppermute | solution.py:459
  175.2 3.4 %collective-permute-start.25 = (f32[1,64]{1,0:T(1,128)S(1)}, f32[1,64]{1,0:T(1,128)S(1)}, u32[]{:S(2)}, u32[]{:S(2)}) collective-permute-start(f32[1,64]{1,0:T(1,128)S(1)} %add.225), channel_id=1, source_target_pairs={{0,4},{4,0},{1,5},{5,1},{2,6},{6,2},{3,7},{7,3},{8,12},{12,8},{9,1... | collective-permute-start | bytes 776 | tf_op jit(solution)/shard_map/ppermute | solution.py:17
  (87 shorter events, 45.5 us)
Async XLA Ops:
  6.5 41.6 %all-gather.4.cloned.1.call-start = ((), (), s32[]{:S(2)}) async-start(), calls=%async_computation | async-start | bytes 1310720 | tf_op jit(solution)/shard_map/all_gather | solution.py:340
  6.5 26.5 %collective-permute-start.4 = (bf16[512,14336]{1,0:T(8,128)(2,1)}, bf16[512,14336]{1,0:T(8,128)(2,1)}, u32[]{:S(2)}, u32[]{:S(2)}) collective-permute-start(bf16[512,14336]{1,0:T(8,128)(2,1)} %mine.5), channel_id=1, source_target_pairs={{0,8},{8,0},{1,9},{9,1},{2,10},{10,2},{3,11},{11,3},{4,12},{12,4},... | collective-permute-start | bytes 44040200 | tf_op jit(solution)/shard_map/ppermute | solution.py:17
  7.5 8.3 %collective-permute-start.6 = (bf16[32,2048]{1,0:T(8,128)(2,1)S(1)}, bf16[32,2048]{1,0:T(8,128)(2,1)S(1)}, u32[]{:S(2)}, u32[]{:S(2)}) collective-permute-start(bf16[32,2048]{1,0:T(8,128)(2,1)S(1)} %get-tuple-element.74), channel_id=1, source_target_pairs={{0,16},{16,0},{1,17},{17,1},{2,18},{18,2},{3,19},{19,3},{4,20},{20... | collective-permute-start | bytes 393224 | tf_op jit(solution)/shard_map/ppermute | solution.py:17
  12.5 52.2 %collective-permute-start = (bf16[1024,896]{1,0:T(8,128)(2,1)}, bf16[1024,896]{1,0:T(8,128)(2,1)}, u32[]{:S(2)}, u32[]{:S(2)}) collective-permute-start(bf16[1024,896]{1,0:T(8,128)(2,1)} %pad_maximum_fusion.refs_0_), channel_id=1, source_target_pairs={{0,32},{32,64},{64,96},{96,0},{1,33},{33,65},{65,97},{97,1},{2,34}... | collective-permute-start | bytes 5505032 | tf_op jit(solution)/shard_map/ppermute | solution.py:17
  14.1 50.6 %collective-permute-start.1 = (bf16[1024,896]{1,0:T(8,128)(2,1)}, bf16[1024,896]{1,0:T(8,128)(2,1)}, u32[]{:S(2)}, u32[]{:S(2)}) collective-permute-start(bf16[1024,896]{1,0:T(8,128)(2,1)} %pad_maximum_fusion.refs_0_), channel_id=1, source_target_pairs={{0,96},{32,0},{64,32},{96,64},{1,97},{33,1},{65,33},{97,65},{2,98}... | collective-permute-start | bytes 5505032 | tf_op jit(solution)/shard_map/ppermute | solution.py:17
  16.5 130.6 %all-gather.6.cloned.1.call-start = ((), (), s32[]{:S(2)}) async-start(), calls=%async_computation.1 | async-start | bytes 5242880 | tf_op jit(solution)/shard_map/all_gather | solution.py:393
  20.8 9.9 %collective-permute-start.2 = (bf16[256,512]{1,0:T(8,128)(2,1)S(1)}, bf16[256,512]{1,0:T(8,128)(2,1)S(1)}, u32[]{:S(2)}, u32[]{:S(2)}) collective-permute-start(bf16[256,512]{1,0:T(8,128)(2,1)S(1)} %convolution_convert_fusion), channel_id=1, source_target_pairs={{0,4},{4,0},{1,5},{5,1},{2,6},{6,2},{3,7},{7,3},{8,12},{12,8},{9,1... | collective-permute-start | bytes 786440 | tf_op jit(solution)/shard_map/ppermute | solution.py:17
  31.8 26.6 %collective-permute-start.3 = (bf16[640,896]{1,0:T(8,128)(2,1)}, bf16[640,896]{1,0:T(8,128)(2,1)}, u32[]{:S(2)}, u32[]{:S(2)}) collective-permute-start(bf16[640,896]{1,0:T(8,128)(2,1)} %slice.12), channel_id=1, source_target_pairs={{0,16},{16,0},{1,17},{17,1},{2,18},{18,2},{3,19},{19,3},{4,20},{20... | collective-permute-start | bytes 3440648 | tf_op jit(solution)/shard_map/ppermute | solution.py:17
  33.0 15.2 %collective-permute-start.7 = (bf16[2,256,512]{2,1,0:T(8,128)(2,1)S(1)}, bf16[2,256,512]{2,1,0:T(8,128)(2,1)S(1)}, u32[]{:S(2)}, u32[]{:S(2)}) collective-permute-start(bf16[2,256,512]{2,1,0:T(8,128)(2,1)S(1)} %maximum_select_fusion), channel_id=1, source_target_pairs={{0,1},{1,2},{2,3},{3,0},{4,5},{5,6},{6,7},{7,4},{8,9},{9,10},{10,1... | collective-permute-start | bytes 1572872 | tf_op jit(solution)/shard_map/ppermute | solution.py:17
  34.5 13.8 %collective-permute-start.8 = (bf16[2,256,512]{2,1,0:T(8,128)(2,1)S(1)}, bf16[2,256,512]{2,1,0:T(8,128)(2,1)}, u32[]{:S(2)}, u32[]{:S(2)}) collective-permute-start(bf16[2,256,512]{2,1,0:T(8,128)(2,1)S(1)} %maximum_select_fusion), channel_id=1, source_target_pairs={{0,3},{1,0},{2,1},{3,2},{4,7},{5,4},{6,5},{7,6},{8,11},{9,8},{10,9... | collective-permute-start | bytes 1572872 | tf_op jit(solution)/shard_map/ppermute | solution.py:17
  50.0 14.7 %collective-permute-start.10 = (bf16[1,256,512]{2,1,0:T(8,128)(2,1)}, bf16[1,256,512]{2,1,0:T(8,128)(2,1)}, u32[]{:S(2)}, u32[]{:S(2)}) collective-permute-start(bf16[1,256,512]{2,1,0:T(8,128)(2,1)} %slice.15), channel_id=1, source_target_pairs={{0,3},{1,0},{2,1},{3,2},{4,7},{5,4},{6,5},{7,6},{8,11},{9,8},{10,9... | collective-permute-start | bytes 786440 | tf_op jit(solution)/shard_map/ppermute | solution.py:17
  53.7 11.0 %collective-permute-start.9 = (bf16[1,256,512]{2,1,0:T(8,128)(2,1)}, bf16[1,256,512]{2,1,0:T(8,128)(2,1)}, u32[]{:S(2)}, u32[]{:S(2)}) collective-permute-start(bf16[1,256,512]{2,1,0:T(8,128)(2,1)} %slice.14), channel_id=1, source_target_pairs={{0,1},{1,2},{2,3},{3,0},{4,5},{5,6},{6,7},{7,4},{8,9},{9,10},{10,1... | collective-permute-start | bytes 786440 | tf_op jit(solution)/shard_map/ppermute | solution.py:17
  64.7 18.7 %collective-permute-start.16 = (bf16[384,896]{1,0:T(8,128)(2,1)}, bf16[384,896]{1,0:T(8,128)(2,1)S(1)}, u32[]{:S(2)}, u32[]{:S(2)}) collective-permute-start(bf16[384,896]{1,0:T(8,128)(2,1)} %pad_maximum_fusion.1), channel_id=1, source_target_pairs={{0,16},{16,0},{1,17},{17,1},{2,18},{18,2},{3,19},{19,3},{4,20},{20... | collective-permute-start | bytes 2064392 | tf_op jit(solution)/shard_map/ppermute | solution.py:17
  65.1 45.5 %collective-permute-start.11 = (bf16[640,896]{1,0:T(8,128)(2,1)}, bf16[640,896]{1,0:T(8,128)(2,1)}, u32[]{:S(2)}, u32[]{:S(2)}) collective-permute-start(bf16[640,896]{1,0:T(8,128)(2,1)} %collective-permute-done.3.refs_3_), channel_id=1, source_target_pairs={{0,32},{32,64},{64,96},{96,0},{1,33},{33,65},{65,97},{97,1},{2,34}... | collective-permute-start | bytes 3440648 | tf_op jit(solution)/shard_map/ppermute | solution.py:17
  70.3 37.1 %collective-permute-start.15 = (bf16[512,896]{1,0:T(8,128)(2,1)}, bf16[512,896]{1,0:T(8,128)(2,1)S(1)}, u32[]{:S(2)}, u32[]{:S(2)}) collective-permute-start(bf16[512,896]{1,0:T(8,128)(2,1)} %get-tuple-element.57), channel_id=1, source_target_pairs={{0,96},{32,0},{64,32},{96,64},{1,97},{33,1},{65,33},{97,65},{2,98}... | collective-permute-start | bytes 2752520 | tf_op jit(solution)/shard_map/ppermute | solution.py:17
  72.0 44.2 %collective-permute-start.13 = (bf16[640,896]{1,0:T(8,128)(2,1)}, bf16[640,896]{1,0:T(8,128)(2,1)}, u32[]{:S(2)}, u32[]{:S(2)}) collective-permute-start(bf16[640,896]{1,0:T(8,128)(2,1)} %collective-permute-done.3.refs_3_), channel_id=1, source_target_pairs={{0,96},{32,0},{64,32},{96,64},{1,97},{33,1},{65,33},{97,65},{2,98}... | collective-permute-start | bytes 3440648 | tf_op jit(solution)/shard_map/ppermute | solution.py:17
  73.7 47.7 %collective-permute-start.19 = (bf16[768,896]{1,0:T(8,128)(2,1)}, bf16[768,896]{1,0:T(8,128)(2,1)}, u32[]{:S(2)}, u32[]{:S(2)}) collective-permute-start(bf16[768,896]{1,0:T(8,128)(2,1)} %get-tuple-element.65), channel_id=1, source_target_pairs={{0,16},{16,0},{1,17},{17,1},{2,18},{18,2},{3,19},{19,3},{4,20},{20... | collective-permute-start | bytes 4128776 | tf_op jit(solution)/shard_map/ppermute | solution.py:17
  83.4 38.0 %collective-permute-start.18 = (bf16[512,896]{1,0:T(8,128)(2,1)}, bf16[512,896]{1,0:T(8,128)(2,1)}, u32[]{:S(2)}, u32[]{:S(2)}) collective-permute-start(bf16[512,896]{1,0:T(8,128)(2,1)} %get-tuple-element.64), channel_id=1, source_target_pairs={{0,32},{32,64},{64,96},{96,0},{1,33},{33,65},{65,97},{97,1},{2,34}... | collective-permute-start | bytes 2752520 | tf_op jit(solution)/shard_map/ppermute | solution.py:17
  110.3 24.1 %collective-permute-start.17 = (bf16[384,896]{1,0:T(8,128)(2,1)}, bf16[384,896]{1,0:T(8,128)(2,1)}, u32[]{:S(2)}, u32[]{:S(2)}) collective-permute-start(bf16[384,896]{1,0:T(8,128)(2,1)} %cut.7), channel_id=1, source_target_pairs={{0,16},{16,0},{1,17},{17,1},{2,18},{18,2},{3,19},{19,3},{4,20},{20... | collective-permute-start | bytes 2064392 | tf_op jit(solution)/shard_map/ppermute | solution.py:17
  112.6 21.8 %collective-permute-start.12 = (bf16[384,896]{1,0:T(8,128)(2,1)}, bf16[384,896]{1,0:T(8,128)(2,1)}, u32[]{:S(2)}, u32[]{:S(2)}) collective-permute-start(bf16[384,896]{1,0:T(8,128)(2,1)} %cut.4), channel_id=1, source_target_pairs={{0,32},{32,64},{64,96},{96,0},{1,33},{33,65},{65,97},{97,1},{2,34}... | collective-permute-start | bytes 2064392 | tf_op jit(solution)/shard_map/ppermute | solution.py:17
  118.0 16.4 %collective-permute-start.14 = (bf16[256,896]{1,0:T(8,128)(2,1)}, bf16[256,896]{1,0:T(8,128)(2,1)}, u32[]{:S(2)}, u32[]{:S(2)}) collective-permute-start(bf16[256,896]{1,0:T(8,128)(2,1)} %cut.6), channel_id=1, source_target_pairs={{0,96},{32,0},{64,32},{96,64},{1,97},{33,1},{65,33},{97,65},{2,98}... | collective-permute-start | bytes 1376264 | tf_op jit(solution)/shard_map/ppermute | solution.py:17
  121.4 22.1 %collective-permute-start.21 = (bf16[8,256,512]{2,1,0:T(8,128)(2,1)}, bf16[8,256,512]{2,1,0:T(8,128)(2,1)}, u32[]{:S(2)}, u32[]{:S(2)}) collective-permute-start(bf16[8,256,512]{2,1,0:T(8,128)(2,1)} %constant_dynamic-update-slice_fusion.own_acts), channel_id=1, source_target_pairs={{0,8},{8,0},{1,9},{9,1},{2,10},{10,2},{3,11},{11,3},{4,12},{12,4},... | collective-permute-start | bytes 6291464 | tf_op jit(solution)/shard_map/ppermute | solution.py:17
  170.5 4.8 %collective-permute-start.24 = (f32[1,64]{1,0:T(1,128)S(1)}, f32[1,64]{1,0:T(1,128)S(1)}, u32[]{:S(2)}, u32[]{:S(2)}) collective-permute-start(f32[1,64]{1,0:T(1,128)S(1)} %add.224), channel_id=1, source_target_pairs={{0,3},{1,2},{2,1},{3,0},{4,7},{5,6},{6,5},{7,4},{8,11},{9,10},{10,... | collective-permute-start | bytes 776 | tf_op jit(solution)/shard_map/ppermute | solution.py:459
  175.2 5.0 %collective-permute-start.25 = (f32[1,64]{1,0:T(1,128)S(1)}, f32[1,64]{1,0:T(1,128)S(1)}, u32[]{:S(2)}, u32[]{:S(2)}) collective-permute-start(f32[1,64]{1,0:T(1,128)S(1)} %add.225), channel_id=1, source_target_pairs={{0,4},{4,0},{1,5},{5,1},{2,6},{6,2},{3,7},{7,3},{8,12},{12,8},{9,1... | collective-permute-start | bytes 776 | tf_op jit(solution)/shard_map/ppermute | solution.py:17
  (12 other events, 93.0 us)
Sparse Core Ops, SparseCore 0:
  16.6 31.4 all-gather.3
  64.8 49.8 all-gather.5

commit v5 on v4

--- a/solution.py
+++ b/solution.py
@@ -187,7 +187,7 @@
 
 
 def cut_out(arrays, cuts):
-    cols = arrays[0].shape[1]
+    rest = arrays[0].shape[1:]
     lengths = {}
     for _, _, size, out, to in cuts:
         lengths[out] = max(lengths.get(out, 0), to + size)
@@ -196,7 +196,7 @@
         in_specs=[pl.BlockSpec(memory_space=pltpu.HBM)] * len(arrays),
         out_specs=[pl.BlockSpec(memory_space=pltpu.VMEM)] * len(lengths),
         out_shape=[
-            jax.ShapeDtypeStruct((lengths[out], cols), arrays[0].dtype)
+            jax.ShapeDtypeStruct((lengths[out], *rest), arrays[0].dtype)
             for out in range(len(lengths))
         ],
         scratch_shapes=[pltpu.SemaphoreType.DMA((len(cuts),))],
@@ -204,39 +204,39 @@
     )(*arrays)
 
 
-def accumulate_kernel(places_ref, mine, theirs, *refs, plan, count, carried):
+def accumulate_kernel(places_ref, mine, theirs, *refs, plan, rows, count, carried):
     pieces = refs[:count]
     out_ref, grads_ref, basis_ref, sems = refs[count + carried : count + carried + 4]
     tokens = mine.shape[0]
-    rows = sum(deep for _, deep, _, _ in plan[0])
-    bounds = list(range(len(plan), 0, -2))[::-1]
-    starts = [0] + bounds[:-1]
 
     groups = []
+    bounds = [0]
     used = 0
-    for first, last in zip(starts, bounds):
+    for chunks in plan:
         group = []
-        for index in range(first, last):
-            column = pl.multiple_of(places_ref[index] * rows, 128)
+        at = bounds[-1]
+        for block, offset, deep, piece, piece_row in chunks:
+            column = pl.multiple_of(places_ref[block] * rows + offset, 128)
             for row, source in ((0, theirs), (tokens, mine)):
                 group.append(
                     pltpu.make_async_copy(
-                        source.at[:, pl.ds(column, rows)],
-                        grads_ref.at[pl.ds(row, tokens), pl.ds(index * rows, rows)],
+                        source.at[:, pl.ds(column, deep)],
+                        grads_ref.at[pl.ds(row, tokens), pl.ds(at, deep)],
                         sems.at[used],
                     )
                 )
                 used += 1
-            for offset, deep, piece, piece_row in plan[index]:
-                group.append(
-                    pltpu.make_async_copy(
-                        pieces[piece].at[pl.ds(piece_row, deep)],
-                        basis_ref.at[pl.ds(index * rows + offset, deep)],
-                        sems.at[used],
-                    )
+            group.append(
+                pltpu.make_async_copy(
+                    pieces[piece].at[pl.ds(piece_row, deep)],
+                    basis_ref.at[pl.ds(at, deep)],
+                    sems.at[used],
                 )
-                used += 1
+            )
+            used += 1
+            at += deep
         groups.append(group)
+        bounds.append(at)
     for group in groups:
         for copy in group:
             copy.start()
@@ -245,13 +245,11 @@
         carry = pltpu.make_async_copy(refs[count], before_ref, sems.at[used])
         carry.start()
     total = None
-    for first, last, group in zip(starts, bounds, groups):
+    for first, last, group in zip(bounds, bounds[1:], groups):
         for copy in group:
             copy.wait()
         product = jnp.dot(
-            grads_ref[:, first * rows : last * rows],
-            basis_ref[first * rows : last * rows, :],
-            preferred_element_type=f32,
+            grads_ref[:, first:last], basis_ref[first:last, :], preferred_element_type=f32
         )
         total = product if total is None else total + product
     if carried:
@@ -260,16 +258,16 @@
     out_ref[...] = total.astype(out_ref.dtype)
 
 
-def accumulate(places, mine, theirs, plan, pieces, carried, kind, near=False):
+def accumulate(places, mine, theirs, rows, plan, pieces, carried, kind, near=False):
     tokens = mine.shape[0]
-    rows = sum(deep for _, deep, _, _ in plan[0])
     cols = pieces[0].shape[1]
     held = pl.BlockSpec(memory_space=pltpu.VMEM)
     anywhere = pl.BlockSpec(memory_space=pltpu.HBM)
-    copies = sum(2 + len(cuts) for cuts in plan) + 1
+    deep = sum(chunk[2] for chunks in plan for chunk in chunks)
+    copies = 3 * sum(len(chunks) for chunks in plan) + 1
     return pl.pallas_call(
         functools.partial(
-            accumulate_kernel, plan=plan, count=len(pieces), carried=len(carried)
+            accumulate_kernel, plan=plan, rows=rows, count=len(pieces), carried=len(carried)
         ),
         in_specs=[
             pl.BlockSpec(memory_space=pltpu.SMEM),
@@ -280,8 +278,8 @@
         out_specs=held,
         out_shape=jax.ShapeDtypeStruct((2 * tokens, cols), kind),
         scratch_shapes=[
-            pltpu.VMEM((2 * tokens, len(plan) * rows), bf16),
-            pltpu.VMEM((len(plan) * rows, cols), bf16),
+            pltpu.VMEM((2 * tokens, deep), bf16),
+            pltpu.VMEM((deep, cols), bf16),
             pltpu.SemaphoreType.DMA((copies,)),
             *[pltpu.VMEM((2 * tokens, cols), f32) for _ in carried],
         ],
@@ -395,30 +393,36 @@
     before_beside_a = forth(beside_head)
     length = before.shape[0]
     end = length - most
-    before_head, after_tail, both_ends = cut_out(
-        (before, after),
-        (
-            (0, 0, half, 0, 0),
-            (1, half, length - half, 1, 0),
-            (0, most, end, 2, 0),
-            (1, most, end, 2, end),
-        ),
-    )
-    after_tail, beside_late = lax.optimization_barrier((after_tail, beside_head))
+    (after_tail,) = cut_out((after,), ((0, half, length - half, 0, 0),))
+    after_tail, beside_late, before, after = lax.optimization_barrier(
+        (after_tail, beside_head, before, after)
+    )
+    before_head, both_ends = cut_out(
+        (before, after), ((0, 0, half, 0, 0), (0, most, end, 1, 0), (1, most, end, 1, end))
+    )
     far_a, far_b = forth(before_head), back(after_tail)
     after_beside_a = back(beside_late)
     beside_ends = across(both_ends)
-    acts = jnp.concatenate([pair, pair_before, pair_after, pair_far_0, pair_far_1])
-    acts = jnp.concatenate([pair, pair_before, pair_after, pair_far_0, pair_far_1])
+    (acts,) = cut_out(
+        (pair, pair_before, pair_after, pair_far_0, pair_far_1),
+        ((0, 0, 2, 0, 0), (1, 0, 2, 0, 2), (2, 0, 2, 0, 4), (3, 0, 1, 0, 6), (4, 0, 1, 0, 7)),
+    )
+    (acts,) = cut_out(
+        (pair, pair_before, pair_after, pair_far_0, pair_far_1),
+        ((0, 0, 2, 0, 0), (1, 0, 2, 0, 2), (2, 0, 2, 0, 4), (3, 0, 1, 0, 6), (4, 0, 1, 0, 7)),
+    )
     sums = accumulate(
-        places_a, out_grads, grads_peer,
+        places_a, out_grads, grads_peer, rows,
         (
-            ((0, rows, 0, 0),),
-            ((0, rows, 1, 0),),
-            ((0, rows, 2, 0),),
-            ((0, most, 3, 0), (most, rows - most, 4, 0)),
+            ((0, 0, rows, 0, 0), (1, 0, rows, 1, 0)),
+            ((2, 0, rows, 2, 0), (3, 0, most, 3, 0), (3, most, rows - most, 4, 0)),
         ),
         (output_basis, before, after, beside_head, beside_end), (), f32,
+    )
+    sums = accumulate(
+        places_c, out_grads, grads_peer, rows,
+        (((0, half, rows - half, 0, 0), (1, 0, most, 1, 0)),),
+        (far_b, before_beside_a), (sums,), f32,
     )
     far_b, sums, acts = lax.optimization_barrier((far_b, sums, acts))
 
@@ -428,18 +432,27 @@
     far_beside_a, far_beside_b, far_beside_c = forth(part_a), back(part_b), across(part_c)
     acts_peer = sibling(acts)
     sums = accumulate(
-        places_c, out_grads, grads_peer,
+        places_c, out_grads, grads_peer, rows,
         (
-            ((0, half, 0, 0), (half, rows - half, 1, 0)),
-            ((0, most, 2, 0), (most, rows - most, 4, 0)),
-            ((0, most, 3, 0), (most, rows - most, 4, end)),
+            ((0, 0, half, 0, 0),),
+            (
+                (1, most, rows - most, 2, 0),
+                (2, 0, most, 1, 0),
+                (2, most, rows - most, 2, end),
+            ),
         ),
-        (far_a, far_b, before_beside_a, after_beside_a, beside_ends), (sums,), f32,
+        (far_a, after_beside_a, beside_ends), (sums,), f32,
     )
 
     mine = accumulate(
-        places_d, out_grads, grads_peer,
-        (((0, 3 * tile, 0, 0), (3 * tile, 2 * tile, 1, 0), (most, rows - most, 2, 0)),),
+        places_d, out_grads, grads_peer, rows,
+        (
+            (
+                (0, 0, 3 * tile, 0, 0),
+                (0, 3 * tile, 2 * tile, 1, 0),
+                (0, most, rows - most, 2, 0),
+            ),
+        ),
         (far_beside_a, far_beside_b, far_beside_c), (sums,), bf16, near=True,
     )
     more = sibling(mine)

time: 188 us -> 186 us (0.989)
  Pallas kernels: 62.9 us -> 72.3 us
  local copies, waits for them, and re-layouts: 15 us -> 8.18 us
  waiting for transfers between devices: 44.8 us -> 40.8 us
    unnamed x18, local copies, waits for them, and re-layouts: 7.69 us -> 2.46 us
    pallas_call x3 -> x4, Pallas kernels: 36.5 us -> 41.5 us  [accumulate(): pl.pallas_call(functools.partial(accumulate_kernel, plan=plan, rows=rows,...]
    pallas_call x4 -> x6, Pallas kernels: 9.31 us -> 13.8 us  [cut_out(): pl.pallas_call(functools.partial(cut_kernel, cuts=cuts, count=len(arrays)...]
    ppermute x24, waiting for transfers between devices: 30.6 us -> 26.5 us  [shifted(): lax.ppermute(value, axis, [(i, (i + step) % size) for i in range(size)])]
  transfers between devices with their start and end apart: 28 -> 28, of which waited for: 14 -> 14; matrix products, arithmetic and copies ran while one was open for 13% -> 10% of each run, Pallas kernels for 24% -> 30%
where the time goes in v5:
time: 186 us; the launch traced here: 185 us
  Pallas kernels  72.3 us (39%)
  waiting for transfers between devices  40.8 us (22%)
  starting transfers between devices  36.8 us (20%)
  between operations  14.3 us (8%)
  other arithmetic  8.66 us (5%)
  local copies, waits for them, and re-layouts  8.18 us (4%)
  matrix products  4.23 us (2%)
    pallas_call x4, Pallas kernels, accumulate(): pl.pallas_call(functools.partial(accumulate_kernel, plan=plan, rows=rows,...  41.5 us
    ppermute x24, starting transfers between devices, shifted(): lax.ppermute(value, axis, [(i, (i + step) % size) for i in range(size)])  32.7 us
    ppermute x24, waiting for transfers between devices, shifted(): lax.ppermute(value, axis, [(i, (i + step) % size) for i in range(size)])  26.5 us
    pallas_call x1, Pallas kernels, scores_of(): pl.pallas_call(functools.partial(score_kernel, right_rows=right_rows, cou...  17.1 us
    pallas_call x6, Pallas kernels, cut_out(): pl.pallas_call(functools.partial(cut_kernel, cuts=cuts, count=len(arrays)...  13.8 us
    all_gather x1, waiting for transfers between devices, per_device(): left_dp = lax.all_gather(left_pair, 'y', axis=0)  10 us
    dot_general x1, matrix products, per_device(): lax.dot_general(input_basis, activations, (((0,), (1,)), ((), ())), prefe...  4.23 us
  transfers between devices with their start and end apart: 28, of which 14 were waited for; matrix products, arithmetic and copies ran while one was open for 10% of the time, Pallas kernels for 30%

profile of v5, /device:TPU:0, one launch (start us, length us, event | category | flops | bytes accessed | tf_op | source)
XLA Modules:
  0.0 185.3 jit_solution(15778554200124222327)
XLA Ops:
  7.5 2.1 %collective-permute-start.6 = (bf16[32,2048]{1,0:T(8,128)(2,1)S(1)}, bf16[32,2048]{1,0:T(8,128)(2,1)S(1)}, u32[]{:S(2)}, u32[]{:S(2)}) collective-permute-start(bf16[32,2048]{1,0:T(8,128)(2,1)S(1)} %get-tuple-element.76), channel_id=1, source_target_pairs={{0,16},{16,0},{1,17},{17,1},{2,18},{18,2},{3,19},{19,3},{4,20},{20... | collective-permute-start | bytes 393224 | tf_op jit(solution)/shard_map/ppermute | solution.py:17
  9.5 3.0 %pad_maximum_fusion.refs_0_ = bf16[1024,896]{1,0:T(8,128)(2,1)} fusion(bf16[128,896]{1,0:T(8,128)(2,1)} %bitcast.48, bf16[896,896]{1,0:T(8,128)(2,1)} %refs_0_.1), kind=kLoop, calls=%fused_computation | loop fusion | flops 3670016 | bytes 3670016 | tf_op jit(solution)/shard_map/concatenate | solution.py:346
  16.6 4.2 %convolution_convert_fusion = bf16[256,512]{1,0:T(8,128)(2,1)S(1)} fusion(bf16[4096,256]{1,0:T(8,128)(2,1)} %param.13, bf16[512,4096]{1,0:T(8,128)(2,1)} %param.11), kind=kOutput, calls=%fused_computation.1 | convolution fusion | flops 1073872896 | bytes 6553600 | tf_op jit(solution)/shard_map/dot_general | solution.py:341
  20.8 3.7 %collective-permute-start.2 = (bf16[256,512]{1,0:T(8,128)(2,1)S(1)}, bf16[256,512]{1,0:T(8,128)(2,1)S(1)}, u32[]{:S(2)}, u32[]{:S(2)}) collective-permute-start(bf16[256,512]{1,0:T(8,128)(2,1)S(1)} %convolution_convert_fusion), channel_id=1, source_target_pairs={{0,4},{4,0},{1,5},{5,1},{2,6},{6,2},{3,7},{7,3},{8,12},{12,8},{9,1... | collective-permute-start | bytes 786440 | tf_op jit(solution)/shard_map/ppermute | solution.py:17
  25.5 5.2 %collective-permute-done.2 = bf16[256,512]{1,0:T(8,128)(2,1)S(1)} collective-permute-done((bf16[256,512]{1,0:T(8,128)(2,1)S(1)}, bf16[256,512]{1,0:T(8,128)(2,1)S(1)}, u32[]{:S(2)}, u32[]{:S(2)}) %collective-permute-start.2) | collective-permute-done | bytes 262176 | tf_op jit(solution)/shard_map/ppermute | solution.py:17
  38.1 10.0 %all-gather.4.cloned.1.call-done = bf16[4,2,32,2048]{3,2,1,0:T(8,128)(2,1)} async-done(((bf16[1,2,32,2048]{3,2,1,0:T(8,128)(2,1)}), bf16[4,2,32,2048]{3,2,1,0:T(8,128)(2,1)}) %all-gather.4.cloned.1.call-update) | async-done | bytes 1048592 | tf_op jit(solution)/shard_map/all_gather | solution.py:338
  50.1 2.9 %collective-permute-start.10 = (bf16[1,256,512]{2,1,0:T(8,128)(2,1)}, bf16[1,256,512]{2,1,0:T(8,128)(2,1)}, u32[]{:S(2)}, u32[]{:S(2)}) collective-permute-start(bf16[1,256,512]{2,1,0:T(8,128)(2,1)} %slice.15), channel_id=1, source_target_pairs={{0,3},{1,0},{2,1},{3,2},{4,7},{5,4},{6,5},{7,6},{8,11},{9,8},{10,9... | collective-permute-start | bytes 786440 | tf_op jit(solution)/shard_map/ppermute | solution.py:17
  58.5 6.2 %collective-permute-done.refs_1_.refs_0_ = bf16[1024,896]{1,0:T(8,128)(2,1)} collective-permute-done((bf16[1024,896]{1,0:T(8,128)(2,1)}, bf16[1024,896]{1,0:T(8,128)(2,1)}, u32[]{:S(2)}, u32[]{:S(2)}) %collective-permute-start) | collective-permute-done | bytes 1835040 | tf_op jit(solution)/shard_map/ppermute | solution.py:17
  66.7 2.1 %cut.7 = bf16[512,896]{1,0:T(8,128)(2,1)} custom-call(bf16[1024,896]{1,0:T(8,128)(2,1)} %collective-permute-done.1.refs_0_.refs_2_.refs_1_), custom_call_target="tpu_custom_call" | custom-call | tf_op jit(solution)/shard_map/cut/pallas_call | solution.py:194
  72.3 3.0 %cut.11 = (bf16[512,896]{1,0:T(8,128)(2,1)}, bf16[768,896]{1,0:T(8,128)(2,1)}) custom-call(bf16[1024,896]{1,0:T(8,128)(2,1)} %collective-permute-done.refs_1_.refs_0_, bf16[1024,896]{1,0:T(8,128)(2,1)} %collective-permute-done.1.refs_0_.refs_2_.refs_1_), custom_call_target="tpu_custom_call" | custom-call | tf_op jit(solution)/shard_map/cut/pallas_call | solution.py:194
  77.1 6.3 %collective-permute-done.16.refs_4_.refs_3_ = bf16[384,896]{1,0:T(8,128)(2,1)S(1)} collective-permute-done((bf16[384,896]{1,0:T(8,128)(2,1)}, bf16[384,896]{1,0:T(8,128)(2,1)S(1)}, u32[]{:S(2)}, u32[]{:S(2)}) %collective-permute-start.16) | collective-permute-done | bytes 688160 | tf_op jit(solution)/shard_map/ppermute | solution.py:17
  85.0 2.9 %cut.9.own_acts = bf16[8,256,512]{2,1,0:T(8,128)(2,1)} custom-call(bf16[2,256,512]{2,1,0:T(8,128)(2,1)} %copy-done.6, bf16[2,256,512]{2,1,0:T(8,128)(2,1)} %copy-done.7, bf16[2,256,512]{2,1,0:T(8,128)(2,1)} %collective-permute-done.8.refs_2_, bf16[1,256,512]{2,1,0:T(8,128)(2,1)} %collective-permute-done.9.refs_3_, ...), custom_call_target="tpu_custom_call" | custom-call | tf_op jit(solution)/shard_map/cut/pallas_call | solution.py:194
  87.9 15.4 %accumulate.4.refs_2_ = f32[1024,896]{1,0:T(8,128)} custom-call(s32[4]{0:T(128)} %pad_add_fusion.places_ref, bf16[512,14336]{1,0:T(8,128)(2,1)} %mine.7, bf16[512,14336]{1,0:T(8,128)(2,1)} %collective-permute-done.4.theirs, bf16[896,896]{1,0:T(8,128)(2,1)} %refs_0_.1, bf16[1024,896]{1,0:T(8,128)(2,1)} %collective-permute-done.refs_1_.refs_0_, ...), custom_call_target="tpu_custom_call" | custom-call | tf_op jit(solution)/shard_map/accumulate/pallas_call | solution.py:268
  104.3 8.2 %accumulate.5.refs_3_ = f32[1024,896]{1,0:T(8,128)} custom-call(s32[3]{0:T(128)} %pad_add_fusion.1.places_ref, bf16[512,14336]{1,0:T(8,128)(2,1)} %mine.7, bf16[512,14336]{1,0:T(8,128)(2,1)} %collective-permute-done.4.theirs, bf16[512,896]{1,0:T(8,128)(2,1)} %copy-done, bf16[640,896]{1,0:T(8,128)(2,1)} %collective-permute-done.11.refs_0_.refs_1_, ...), custom_call_target="tpu_custom_call" | custom-call | tf_op jit(solution)/shard_map/accumulate/pallas_call | solution.py:268
  112.5 2.0 %cut.10 = bf16[384,896]{1,0:T(8,128)(2,1)} custom-call(bf16[512,896]{1,0:T(8,128)(2,1)} %copy-done), custom_call_target="tpu_custom_call" | custom-call | tf_op jit(solution)/shard_map/cut/pallas_call | solution.py:194
  120.1 2.1 %collective-permute-start.14 = (bf16[256,896]{1,0:T(8,128)(2,1)}, bf16[256,896]{1,0:T(8,128)(2,1)}, u32[]{:S(2)}, u32[]{:S(2)}) collective-permute-start(bf16[256,896]{1,0:T(8,128)(2,1)} %cut.8), channel_id=1, source_target_pairs={{0,96},{32,0},{64,32},{96,64},{1,97},{33,1},{65,33},{97,65},{2,98}... | collective-permute-start | bytes 1376264 | tf_op jit(solution)/shard_map/ppermute | solution.py:17
  122.2 9.8 %accumulate.6.refs_3_ = f32[1024,896]{1,0:T(8,128)} custom-call(s32[3]{0:T(128)} %pad_add_fusion.1.places_ref, bf16[512,14336]{1,0:T(8,128)(2,1)} %mine.7, bf16[512,14336]{1,0:T(8,128)(2,1)} %collective-permute-done.4.theirs, bf16[512,896]{1,0:T(8,128)(2,1)} %collective-permute-done.18.refs_0_, bf16[640,896]{1,0:T(8,128)(2,1)} %collective-permute-done.13.refs_0_.refs_1_, ...), custom_call_target="tpu_custom_call" | custom-call | tf_op jit(solution)/shard_map/accumulate/pallas_call | solution.py:268
  132.1 8.1 %accumulate.7.mine = bf16[1024,896]{1,0:T(8,128)(2,1)} custom-call(s32[1]{0:T(128)} %bitcast.37.places_ref, bf16[512,14336]{1,0:T(8,128)(2,1)} %mine.7, bf16[512,14336]{1,0:T(8,128)(2,1)} %collective-permute-done.4.theirs, bf16[384,896]{1,0:T(8,128)(2,1)} %collective-permute-done.12.refs_0_, bf16[256,896]{1,0:T(8,128)(2,1)} %collective-permute-done.14.refs_1_, ...), custom_call_target="tpu_custom_call" | custom-call | tf_op jit(solution)/shard_map/accumulate/pallas_call | solution.py:268
  141.0 3.6 %collective-permute-done.20.more = bf16[1024,896]{1,0:T(8,128)(2,1)} collective-permute-done((bf16[1024,896]{1,0:T(8,128)(2,1)}, bf16[1024,896]{1,0:T(8,128)(2,1)}, u32[]{:S(2)}, u32[]{:S(2)}) %collective-permute-start.20) | collective-permute-done | bytes 1835040 | tf_op jit(solution)/shard_map/ppermute | solution.py:17
  146.1 17.1 %scores.1 = (f32[1,64]{1,0:T(1,128)S(1)}, f32[1,64]{1,0:T(1,128)S(1)}) custom-call(s32[8]{0:T(128)S(1)} %stack.137.chips_ref, s32[8]{0:T(128)S(1)} %stack.128.tiles_ref, s32[1]{0:T(128)} %bitcast.29.core_ref, bf16[1024,896]{1,0:T(8,128)(2,1)S(1)} %copy-done.2, bf16[1024,896]{1,0:T(8,128)(2,1)} %collective-permute-done.20.more, f32[512,1]{1,0:T(8,128)S(1)} %fusion.own_weight, ...), custom_call_target="tpu_custom_call" | custom-call | tf_op jit(solution)/shard_map/scores/pallas_call | solution.py:151
  165.9 2.1 %collective-permute-done.23 = f32[1,64]{1,0:T(1,128)S(1)} collective-permute-done((f32[1,64]{1,0:T(1,128)S(1)}, f32[1,64]{1,0:T(1,128)S(1)}, u32[]{:S(2)}, u32[]{:S(2)}) %collective-permute-start.23) | collective-permute-done | bytes 288 | tf_op jit(solution)/shard_map/ppermute | solution.py:471
  168.0 2.7 %collective-permute-start.24 = (f32[1,64]{1,0:T(1,128)S(1)}, f32[1,64]{1,0:T(1,128)S(1)}, u32[]{:S(2)}, u32[]{:S(2)}) collective-permute-start(f32[1,64]{1,0:T(1,128)S(1)} %add.224), channel_id=1, source_target_pairs={{0,3},{1,2},{2,1},{3,0},{4,7},{5,6},{6,5},{7,4},{8,11},{9,10},{10,... | collective-permute-start | bytes 776 | tf_op jit(solution)/shard_map/ppermute | solution.py:472
  170.7 2.1 %collective-permute-done.24 = f32[1,64]{1,0:T(1,128)S(1)} collective-permute-done((f32[1,64]{1,0:T(1,128)S(1)}, f32[1,64]{1,0:T(1,128)S(1)}, u32[]{:S(2)}, u32[]{:S(2)}) %collective-permute-start.24) | collective-permute-done | bytes 288 | tf_op jit(solution)/shard_map/ppermute | solution.py:472
  172.8 3.6 %collective-permute-start.25 = (f32[1,64]{1,0:T(1,128)S(1)}, f32[1,64]{1,0:T(1,128)S(1)}, u32[]{:S(2)}, u32[]{:S(2)}) collective-permute-start(f32[1,64]{1,0:T(1,128)S(1)} %add.225), channel_id=1, source_target_pairs={{0,4},{4,0},{1,5},{5,1},{2,6},{6,2},{3,7},{7,3},{8,12},{12,8},{9,1... | collective-permute-start | bytes 776 | tf_op jit(solution)/shard_map/ppermute | solution.py:17
  (89 shorter events, 42.7 us)
Async XLA Ops:
  6.5 41.6 %all-gather.4.cloned.1.call-start = ((), (), s32[]{:S(2)}) async-start(), calls=%async_computation | async-start | bytes 1310720 | tf_op jit(solution)/shard_map/all_gather | solution.py:338
  6.5 26.5 %collective-permute-start.4 = (bf16[512,14336]{1,0:T(8,128)(2,1)}, bf16[512,14336]{1,0:T(8,128)(2,1)}, u32[]{:S(2)}, u32[]{:S(2)}) collective-permute-start(bf16[512,14336]{1,0:T(8,128)(2,1)} %mine.7), channel_id=1, source_target_pairs={{0,8},{8,0},{1,9},{9,1},{2,10},{10,2},{3,11},{11,3},{4,12},{12,4},... | collective-permute-start | bytes 44040200 | tf_op jit(solution)/shard_map/ppermute | solution.py:17
  7.5 8.3 %collective-permute-start.6 = (bf16[32,2048]{1,0:T(8,128)(2,1)S(1)}, bf16[32,2048]{1,0:T(8,128)(2,1)S(1)}, u32[]{:S(2)}, u32[]{:S(2)}) collective-permute-start(bf16[32,2048]{1,0:T(8,128)(2,1)S(1)} %get-tuple-element.76), channel_id=1, source_target_pairs={{0,16},{16,0},{1,17},{17,1},{2,18},{18,2},{3,19},{19,3},{4,20},{20... | collective-permute-start | bytes 393224 | tf_op jit(solution)/shard_map/ppermute | solution.py:17
  12.5 52.2 %collective-permute-start = (bf16[1024,896]{1,0:T(8,128)(2,1)}, bf16[1024,896]{1,0:T(8,128)(2,1)}, u32[]{:S(2)}, u32[]{:S(2)}) collective-permute-start(bf16[1024,896]{1,0:T(8,128)(2,1)} %pad_maximum_fusion.refs_0_), channel_id=1, source_target_pairs={{0,32},{32,64},{64,96},{96,0},{1,33},{33,65},{65,97},{97,1},{2,34}... | collective-permute-start | bytes 5505032 | tf_op jit(solution)/shard_map/ppermute | solution.py:17
  14.1 50.6 %collective-permute-start.1 = (bf16[1024,896]{1,0:T(8,128)(2,1)}, bf16[1024,896]{1,0:T(8,128)(2,1)}, u32[]{:S(2)}, u32[]{:S(2)}) collective-permute-start(bf16[1024,896]{1,0:T(8,128)(2,1)} %pad_maximum_fusion.refs_0_), channel_id=1, source_target_pairs={{0,96},{32,0},{64,32},{96,64},{1,97},{33,1},{65,33},{97,65},{2,98}... | collective-permute-start | bytes 5505032 | tf_op jit(solution)/shard_map/ppermute | solution.py:17
  16.5 128.1 %all-gather.6.cloned.1.call-start = ((), (), s32[]{:S(2)}) async-start(), calls=%async_computation.1 | async-start | bytes 5242880 | tf_op jit(solution)/shard_map/all_gather | solution.py:391
  20.8 9.9 %collective-permute-start.2 = (bf16[256,512]{1,0:T(8,128)(2,1)S(1)}, bf16[256,512]{1,0:T(8,128)(2,1)S(1)}, u32[]{:S(2)}, u32[]{:S(2)}) collective-permute-start(bf16[256,512]{1,0:T(8,128)(2,1)S(1)} %convolution_convert_fusion), channel_id=1, source_target_pairs={{0,4},{4,0},{1,5},{5,1},{2,6},{6,2},{3,7},{7,3},{8,12},{12,8},{9,1... | collective-permute-start | bytes 786440 | tf_op jit(solution)/shard_map/ppermute | solution.py:17
  31.8 26.6 %collective-permute-start.3 = (bf16[640,896]{1,0:T(8,128)(2,1)}, bf16[640,896]{1,0:T(8,128)(2,1)}, u32[]{:S(2)}, u32[]{:S(2)}) collective-permute-start(bf16[640,896]{1,0:T(8,128)(2,1)} %slice.12), channel_id=1, source_target_pairs={{0,16},{16,0},{1,17},{17,1},{2,18},{18,2},{3,19},{19,3},{4,20},{20... | collective-permute-start | bytes 3440648 | tf_op jit(solution)/shard_map/ppermute | solution.py:17
  33.1 15.2 %collective-permute-start.7 = (bf16[2,256,512]{2,1,0:T(8,128)(2,1)S(1)}, bf16[2,256,512]{2,1,0:T(8,128)(2,1)S(1)}, u32[]{:S(2)}, u32[]{:S(2)}) collective-permute-start(bf16[2,256,512]{2,1,0:T(8,128)(2,1)S(1)} %maximum_select_fusion.refs_0_), channel_id=1, source_target_pairs={{0,1},{1,2},{2,3},{3,0},{4,5},{5,6},{6,7},{7,4},{8,9},{9,10},{10,1... | collective-permute-start | bytes 1572872 | tf_op jit(solution)/shard_map/ppermute | solution.py:17
  34.6 13.8 %collective-permute-start.8 = (bf16[2,256,512]{2,1,0:T(8,128)(2,1)S(1)}, bf16[2,256,512]{2,1,0:T(8,128)(2,1)}, u32[]{:S(2)}, u32[]{:S(2)}) collective-permute-start(bf16[2,256,512]{2,1,0:T(8,128)(2,1)S(1)} %maximum_select_fusion.refs_0_), channel_id=1, source_target_pairs={{0,3},{1,0},{2,1},{3,2},{4,7},{5,4},{6,5},{7,6},{8,11},{9,8},{10,9... | collective-permute-start | bytes 1572872 | tf_op jit(solution)/shard_map/ppermute | solution.py:17
  50.1 14.5 %collective-permute-start.10 = (bf16[1,256,512]{2,1,0:T(8,128)(2,1)}, bf16[1,256,512]{2,1,0:T(8,128)(2,1)}, u32[]{:S(2)}, u32[]{:S(2)}) collective-permute-start(bf16[1,256,512]{2,1,0:T(8,128)(2,1)} %slice.15), channel_id=1, source_target_pairs={{0,3},{1,0},{2,1},{3,2},{4,7},{5,4},{6,5},{7,6},{8,11},{9,8},{10,9... | collective-permute-start | bytes 786440 | tf_op jit(solution)/shard_map/ppermute | solution.py:17
  53.7 11.0 %collective-permute-start.9 = (bf16[1,256,512]{2,1,0:T(8,128)(2,1)}, bf16[1,256,512]{2,1,0:T(8,128)(2,1)}, u32[]{:S(2)}, u32[]{:S(2)}) collective-permute-start(bf16[1,256,512]{2,1,0:T(8,128)(2,1)} %slice.14), channel_id=1, source_target_pairs={{0,1},{1,2},{2,3},{3,0},{4,5},{5,6},{6,7},{7,4},{8,9},{9,10},{10,1... | collective-permute-start | bytes 786440 | tf_op jit(solution)/shard_map/ppermute | solution.py:17
  64.7 18.7 %collective-permute-start.16 = (bf16[384,896]{1,0:T(8,128)(2,1)}, bf16[384,896]{1,0:T(8,128)(2,1)S(1)}, u32[]{:S(2)}, u32[]{:S(2)}) collective-permute-start(bf16[384,896]{1,0:T(8,128)(2,1)} %pad_maximum_fusion.1), channel_id=1, source_target_pairs={{0,16},{16,0},{1,17},{17,1},{2,18},{18,2},{3,19},{19,3},{4,20},{20... | collective-permute-start | bytes 2064392 | tf_op jit(solution)/shard_map/ppermute | solution.py:17
  65.2 38.2 %collective-permute-start.11 = (bf16[640,896]{1,0:T(8,128)(2,1)}, bf16[640,896]{1,0:T(8,128)(2,1)}, u32[]{:S(2)}, u32[]{:S(2)}) collective-permute-start(bf16[640,896]{1,0:T(8,128)(2,1)} %collective-permute-done.3.refs_3_), channel_id=1, source_target_pairs={{0,32},{32,64},{64,96},{96,0},{1,33},{33,65},{65,97},{97,1},{2,34}... | collective-permute-start | bytes 3440648 | tf_op jit(solution)/shard_map/ppermute | solution.py:17
  68.8 34.5 %collective-permute-start.15 = (bf16[512,896]{1,0:T(8,128)(2,1)}, bf16[512,896]{1,0:T(8,128)(2,1)S(1)}, u32[]{:S(2)}, u32[]{:S(2)}) collective-permute-start(bf16[512,896]{1,0:T(8,128)(2,1)} %cut.7), channel_id=1, source_target_pairs={{0,96},{32,0},{64,32},{96,64},{1,97},{33,1},{65,33},{97,65},{2,98}... | collective-permute-start | bytes 2752520 | tf_op jit(solution)/shard_map/ppermute | solution.py:17
  70.6 47.7 %collective-permute-start.13 = (bf16[640,896]{1,0:T(8,128)(2,1)}, bf16[640,896]{1,0:T(8,128)(2,1)}, u32[]{:S(2)}, u32[]{:S(2)}) collective-permute-start(bf16[640,896]{1,0:T(8,128)(2,1)} %collective-permute-done.3.refs_3_), channel_id=1, source_target_pairs={{0,96},{32,0},{64,32},{96,64},{1,97},{33,1},{65,33},{97,65},{2,98}... | collective-permute-start | bytes 3440648 | tf_op jit(solution)/shard_map/ppermute | solution.py:17
  75.3 46.9 %collective-permute-start.19 = (bf16[768,896]{1,0:T(8,128)(2,1)}, bf16[768,896]{1,0:T(8,128)(2,1)}, u32[]{:S(2)}, u32[]{:S(2)}) collective-permute-start(bf16[768,896]{1,0:T(8,128)(2,1)} %get-tuple-element.67), channel_id=1, source_target_pairs={{0,16},{16,0},{1,17},{17,1},{2,18},{18,2},{3,19},{19,3},{4,20},{20... | collective-permute-start | bytes 4128776 | tf_op jit(solution)/shard_map/ppermute | solution.py:17
  83.4 38.8 %collective-permute-start.18 = (bf16[512,896]{1,0:T(8,128)(2,1)}, bf16[512,896]{1,0:T(8,128)(2,1)}, u32[]{:S(2)}, u32[]{:S(2)}) collective-permute-start(bf16[512,896]{1,0:T(8,128)(2,1)} %get-tuple-element.66), channel_id=1, source_target_pairs={{0,32},{32,64},{64,96},{96,0},{1,33},{33,65},{65,97},{97,1},{2,34}... | collective-permute-start | bytes 2752520 | tf_op jit(solution)/shard_map/ppermute | solution.py:17
  114.5 17.5 %collective-permute-start.17 = (bf16[384,896]{1,0:T(8,128)(2,1)}, bf16[384,896]{1,0:T(8,128)(2,1)}, u32[]{:S(2)}, u32[]{:S(2)}) collective-permute-start(bf16[384,896]{1,0:T(8,128)(2,1)} %cut.10), channel_id=1, source_target_pairs={{0,16},{16,0},{1,17},{17,1},{2,18},{18,2},{3,19},{19,3},{4,20},{20... | collective-permute-start | bytes 2064392 | tf_op jit(solution)/shard_map/ppermute | solution.py:17
  117.0 15.1 %collective-permute-start.12 = (bf16[384,896]{1,0:T(8,128)(2,1)}, bf16[384,896]{1,0:T(8,128)(2,1)}, u32[]{:S(2)}, u32[]{:S(2)}) collective-permute-start(bf16[384,896]{1,0:T(8,128)(2,1)} %cut.6), channel_id=1, source_target_pairs={{0,32},{32,64},{64,96},{96,0},{1,33},{33,65},{65,97},{97,1},{2,34}... | collective-permute-start | bytes 2064392 | tf_op jit(solution)/shard_map/ppermute | solution.py:17
  120.1 11.9 %collective-permute-start.14 = (bf16[256,896]{1,0:T(8,128)(2,1)}, bf16[256,896]{1,0:T(8,128)(2,1)}, u32[]{:S(2)}, u32[]{:S(2)}) collective-permute-start(bf16[256,896]{1,0:T(8,128)(2,1)} %cut.8), channel_id=1, source_target_pairs={{0,96},{32,0},{64,32},{96,64},{1,97},{33,1},{65,33},{97,65},{2,98}... | collective-permute-start | bytes 1376264 | tf_op jit(solution)/shard_map/ppermute | solution.py:17
  122.2 18.8 %collective-permute-start.21 = (bf16[8,256,512]{2,1,0:T(8,128)(2,1)}, bf16[8,256,512]{2,1,0:T(8,128)(2,1)}, u32[]{:S(2)}, u32[]{:S(2)}) collective-permute-start(bf16[8,256,512]{2,1,0:T(8,128)(2,1)} %cut.9.own_acts), channel_id=1, source_target_pairs={{0,8},{8,0},{1,9},{9,1},{2,10},{10,2},{3,11},{11,3},{4,12},{12,4},... | collective-permute-start | bytes 6291464 | tf_op jit(solution)/shard_map/ppermute | solution.py:17
  168.0 4.8 %collective-permute-start.24 = (f32[1,64]{1,0:T(1,128)S(1)}, f32[1,64]{1,0:T(1,128)S(1)}, u32[]{:S(2)}, u32[]{:S(2)}) collective-permute-start(f32[1,64]{1,0:T(1,128)S(1)} %add.224), channel_id=1, source_target_pairs={{0,3},{1,2},{2,1},{3,0},{4,7},{5,6},{6,5},{7,4},{8,11},{9,10},{10,... | collective-permute-start | bytes 776 | tf_op jit(solution)/shard_map/ppermute | solution.py:472
  172.8 5.2 %collective-permute-start.25 = (f32[1,64]{1,0:T(1,128)S(1)}, f32[1,64]{1,0:T(1,128)S(1)}, u32[]{:S(2)}, u32[]{:S(2)}) collective-permute-start(f32[1,64]{1,0:T(1,128)S(1)} %add.225), channel_id=1, source_target_pairs={{0,4},{4,0},{1,5},{5,1},{2,6},{6,2},{3,7},{7,3},{8,12},{12,8},{9,1... | collective-permute-start | bytes 776 | tf_op jit(solution)/shard_map/ppermute | solution.py:17
  (14 other events, 130.3 us)
Sparse Core Ops, SparseCore 0:
  16.6 31.4 all-gather.3
  64.8 49.9 all-gather.5
